TPU v7x, 256 devices: a whole 4x4x8 slice. The times are simulated.
256 devices in a mesh: tm: 32 (over z, y), state: 8 (over x, core).
Axes of the slice: x: 4, y: 4, z: 8, core: 2. Of those that a mesh axis runs over, the one named last changes fastest.
Arguments:
- inputs: bfloat16 [4, 4096, 256], P(None, 'tm'), may hold values from -6 to 6
- encoder_in: bfloat16 [256, 2048], P(None, 'state'), may hold values from -0.375 to 0.375
- encoder_out: bfloat16 [2048, 1024], P('state'), may hold values from -0.125 to 0.125
- readings: bfloat16 [4, 4096, 8192], P(None, 'tm', 'state'), may hold values from -6 to 6
- available: int32 [4, 4096, 64], P(None, 'tm', 'state'), may hold values 0 or 1
- pattern: int32 [64, 4], P('state'), may hold values from 0 to 7, all different within a row
- gain_blocks: bfloat16 [64, 4, 128, 128], P('state'), may hold values from -0.109375 to 0.109375
- load_blocks: bfloat16 [64, 4, 128, 128], P('state'), may hold values from -0.25 to 0.25
- retain: float32 [1024, 4, 4096], P('state', None, 'tm'), may hold values from 0.1 to 1
- smooth: float32 [1024, 4, 4096], P('state', None, 'tm'), may hold values from 0.1 to 1
- cotangent: bfloat16 [4, 4096, 8192], P(None, 'tm', 'state'), may hold values from -6 to 6
Outputs:
- predicted: bfloat16 [4, 4096, 8192], P(None, 'tm', 'state')
- sensor_grad: bfloat16 [4, 4096, 8192], P(None, 'tm', 'state')
Inputs may be any that keep to these rules, and one draw needn't show every extreme that they name: `pattern`: row q lists 4 different state blocks read by sensor block q; every state block appears in some row.
All inputs are finite; a program needn't handle non-finite values. No bound on the sum of `available` on one device may be relied on, other than what follows from the above.
Results may differ from a plain program's by a relative error of at most 0.005.
Values may be sent and summed in bfloat16 or wider, within the bound.
No kernel may reach another device: no remote copies, remote signals or barrier semaphores. Data moves between devices by JAX's collectives and lax.ppermute only.
A program may use at most 128 MiB of HBM per device.

v0:
```python
import functools

import jax
import jax.numpy as jnp
from jax import lax
from jax.experimental import pallas as pl
from jax.experimental.pallas import tpu as pltpu
from jax.sharding import PartitionSpec as P


F32, BF16 = jnp.float32, jnp.bfloat16
VMEM = 20 << 20
BLK = 128
SEG = 8
NT = (((1,), (1,)), ((), ()))
NN = (((1,), (0,)), ((), ()))


def call(kernel, outs, operands, scratch=(), smem=0, hbm=0, hbm_out=False, flops=0):
    vmem, scalar = pl.BlockSpec(memory_space=pltpu.VMEM), pl.BlockSpec(memory_space=pltpu.SMEM)
    far = pl.BlockSpec(memory_space=pltpu.HBM)
    moved = sum(a.size * a.dtype.itemsize for a in (*operands, *outs))
    return pl.pallas_call(
        kernel,
        out_shape=outs,
        in_specs=[scalar] * smem + [vmem] * (len(operands) - smem - hbm) + [far] * hbm,
        out_specs=tuple([far if hbm_out else vmem] * len(outs)),
        scratch_shapes=list(scratch),
        compiler_params=pltpu.CompilerParams(vmem_limit_bytes=VMEM),
        cost_estimate=pl.CostEstimate(flops=flops, bytes_accessed=moved, transcendentals=0),
    )(*[pltpu.with_memory_space_constraint(a, pltpu.HBM) if i >= len(operands) - hbm else a for i, a in enumerate(operands)])


def struct(shape, dtype):
    return jax.ShapeDtypeStruct(shape, dtype)


def front_kernel(
    place, pattern, available, load_far, cot_far, gain_far, readings_far, rows_far, enc_in_far, enc_out_far,
    load_weights, gain_weights, keep, send, mask,
    load, cotangent, gain, lhs, rows_in, enc_in, enc_out, sems,
):
    core = place[1]
    pairs = (
        (load_far, load), (cot_far, cotangent), (gain_far, gain), (readings_far, lhs),
        (rows_far, rows_in), (enc_in_far, enc_in), (enc_out_far, enc_out),
    )
    copies = [pltpu.make_async_copy(far, near, sems.at[i]) for i, (far, near) in enumerate(pairs)]
    for copy in copies:
        copy.start()
    load_weights[...] = jnp.zeros_like(load_weights)
    gain_weights[...] = jnp.zeros_like(gain_weights)
    traces, blocks, steps = available.shape
    reads = pattern.shape[0]
    for b in range(traces):
        mask[b * steps : (b + 1) * steps, :] = available[b].astype(F32).T

    def split(which, at, total):
        low, high = total[:, :BLK], total[:, BLK:]
        keep[at, which] = jnp.where(core == 0, low, high)
        send[at, which] = jnp.where(core == 0, high, low).astype(BF16)

    copies[0].wait()
    for q in range(blocks):
        for k in range(reads):
            row = pl.multiple_of(pattern[k, q] * BLK, BLK)
            load_weights[pl.ds(row, BLK), q * BLK : (q + 1) * BLK] = load[q, k]
    copies[1].wait()

    def pull_columns(at, _):
        window = pl.ds(pl.multiple_of(at * 2 * BLK, 2 * BLK), 2 * BLK)
        split(1, at, lax.dot_general(cotangent[...], load_weights[window, :], NT, preferred_element_type=F32))
        return 0

    lax.fori_loop(0, 4, pull_columns, 0)
    copies[2].wait()
    for q in range(blocks):
        for k in range(reads):
            column = pl.multiple_of(pattern[k, q] * BLK, BLK)
            gain_weights[q * BLK : (q + 1) * BLK, pl.ds(column, BLK)] = gain[q, k]
    for copy in copies[3:]:
        copy.wait()
    for q in range(blocks):
        lhs[:, q * BLK : (q + 1) * BLK] = lhs[:, q * BLK : (q + 1) * BLK] * mask[:, q : q + 1].astype(BF16)
    hidden = jax.nn.gelu(jnp.dot(rows_in[...], enc_in[...], preferred_element_type=F32)).astype(BF16)

    def drive_columns(at, _):
        window = pl.ds(pl.multiple_of(at * 2 * BLK, 2 * BLK), 2 * BLK)
        total = jnp.dot(lhs[...], gain_weights[:, window], preferred_element_type=F32)
        total += jnp.dot(hidden, enc_out[:, window], preferred_element_type=F32)
        split(0, at, total)
        return 0

    lax.fori_loop(0, 4, drive_columns, 0)


def merge_kernel(place, keep, came, parcel, own):
    for at in range(parcel.shape[0]):
        parcel[at] = (keep[at] + came[at].astype(F32)).astype(BF16)
    own[...] = keep[place[0]] + came[place[0]].astype(F32)


def rows_of(b, u, steps):
    return pl.ds(b * steps + u, SEG, stride=steps // SEG)


def turn(x, by, fill, backward):
    row = lax.broadcasted_iota(jnp.int32, x.shape, 0)
    if backward:
        return jnp.where(row < SEG - by, pltpu.roll(x, SEG - by, 0), fill)
    return jnp.where(row >= by, pltpu.roll(x, by, 0), fill)


def chain(factor, value, backward):
    for by in (1, 2, 4):
        value = factor * turn(value, by, 0.0, backward) + value
        factor = factor * turn(factor, by, 1.0, backward)
    return factor, value, turn(factor, 1, 1.0, backward), turn(value, 1, 0.0, backward)


def decay_kernel(traces, steps, retain, smooth, keep_r, keep_s, root, ahead_p, filt_p, rise_p, fall_p, seg_r, seg_s):
    for b in range(traces):
        span = slice(b * steps, (b + 1) * steps)
        keep_r[span, :] = retain[pl.ds(b, BLK, stride=traces), :].T
        keep_s[span, :] = smooth[pl.ds(b, BLK, stride=traces), :].T
    root[...] = jnp.sqrt(1.0 - keep_r[...] * keep_r[...])
    ones = jnp.ones((SEG, BLK), F32)
    for b in range(traces):
        filt, rise = ones, ones
        for u in range(steps // SEG):
            at = rows_of(b, u, steps)
            r, s = keep_r[at, :], keep_s[at, :]
            filt = filt * r
            filt_p[at, :] = filt
            rise_p[at, :] = rise
            rise = rise * s
        seg_r[b] = filt
        seg_s[b] = rise
        ahead, fall = ones, ones
        for u in reversed(range(steps // SEG)):
            at = rows_of(b, u, steps)
            r, s = keep_r[at, :], keep_s[at, :]
            ahead = ahead * s
            ahead_p[at, :] = ahead
            fall_p[at, :] = fall
            fall = fall * r


def scan_kernel(
    traces, steps, place,
    own, came, keep_r, keep_s, root, seg_r, seg_s,
    states, grads, before, parcel,
    source, pull, ends,
):
    others = [lax.rem(place[0] + k, 4) for k in (1, 2, 3)]
    source[...] = root[...] * (own[0] + sum(came[other, 0].astype(F32) for other in others))
    pull[...] = own[1] + sum(came[other, 1].astype(F32) for other in others)
    for b in range(traces):
        filt = jnp.zeros((SEG, BLK), F32)
        rise, ahead, fall = filt, filt, filt
        for u in range(steps // SEG):
            at = rows_of(b, u, steps)
            r, s, g, p = keep_r[at, :], keep_s[at, :], source[at, :], pull[at, :]
            filt = r * filt + g
            states[at, :] = filt
            carried = rise + p
            grads[at, :] = carried
            rise = s * carried
        for u in reversed(range(steps // SEG)):
            at = rows_of(b, u, steps)
            r, s, g, p = keep_r[at, :], keep_s[at, :], source[at, :], pull[at, :]
            later = s * ahead
            states[at, :] = states[at, :] + later
            ahead = later + g
            grads[at, :] = grads[at, :] + fall
            fall = r * (fall + p)
        for which, (factor, value, backward) in enumerate(
            ((seg_r[b], filt, False), (seg_s[b], rise, False), (seg_s[b], ahead, True), (seg_r[b], fall, True))
        ):
            whole, total, factor_before, value_before = chain(factor, value, backward)
            before[which, b, 0] = factor_before
            before[which, b, 1] = value_before
            end = 0 if backward else SEG - 1
            half, row = which // 2, (which % 2) * traces + b
            ends[half, 0, row : row + 1, :] = total[end : end + 1, :]
            ends[half, 1, row : row + 1, :] = whole[end : end + 1, :]
    me = place[2]
    for target in range(parcel.shape[0]):
        onward = target > me
        parcel[target, :SEG] = jnp.where(onward, ends[0, 0], ends[1, 0])
        parcel[target, SEG:] = jnp.where(onward, ends[0, 1], ends[1, 1])


def settle_kernel(
    traces, steps, place,
    parcel, before, states, grads, root, ahead_p, filt_p, rise_p, fall_p,
    states_bf, grads_bf,
    sums, carry,
):
    me, length = place[2], parcel.shape[0]
    onward = jnp.zeros((SEG, BLK), F32)
    back = onward
    for j in range(length):
        onward = jnp.where(j < me, parcel[j, SEG:] * onward + parcel[j, :SEG], onward)
        i = length - 1 - j
        back = jnp.where(i > me, parcel[i, SEG:] * back + parcel[i, :SEG], back)
    carry[0] = onward
    carry[1] = back
    for b in range(traces):
        filt, rise, ahead, fall = (
            before[w, b, 1] + before[w, b, 0] * carry[w // 2, (w % 2) * traces + b : (w % 2) * traces + b + 1, :]
            for w in range(4)
        )
        for u in range(steps // SEG):
            at = rows_of(b, u, steps)
            sums[0, at, :] = states[at, :] + filt_p[at, :] * filt + ahead_p[at, :] * ahead
            sums[1, at, :] = root[at, :] * (grads[at, :] + rise_p[at, :] * rise + fall_p[at, :] * fall)
    states_bf[...] = sums[0].astype(BF16)
    grads_bf[...] = sums[1].astype(BF16)


def project_kernel(dims, masked, place, *refs):
    *pieces, weights, mask, out, lhs, stage, sems = refs
    x, core = place[0], place[1]
    for k in range(4):
        column = 2 * lax.rem(x - k + 4, 4)
        for side in range(2):
            block = column + (core if side == 0 else 1 - core)
            lhs[:, pl.ds(pl.multiple_of(block * BLK, BLK), BLK)] = pieces[side * 4 + k][...]
    copies = []
    for at in range(4):
        window = slice(at * 2 * BLK, (at + 1) * 2 * BLK)
        chosen = weights[window, :] if dims is NT else weights[:, window]
        total = lax.dot_general(lhs[...], chosen, dims, preferred_element_type=F32)
        for half in range(2):
            q = 2 * at + half
            piece = total[:, half * BLK : (half + 1) * BLK]
            if masked:
                piece = piece * mask[:, q : q + 1]
            stage[:, q * BLK : (q + 1) * BLK] = piece.astype(BF16)
        copies.append(pltpu.make_async_copy(stage.at[:, window], out.at[:, window], sems.at[at]))
        copies[-1].start()
    for copy in copies:
        copy.wait()


def local(inputs, encoder_in, encoder_out, readings, available, pattern, gain, load, retain, smooth, cotangent):
    traces, steps, features = inputs.shape
    rows = traces * steps
    sensors, blocks = readings.shape[2], available.shape[2]
    states = encoder_out.shape[1]
    axis, times = lax.axis_size("state"), lax.axis_size("tm")
    at = lax.axis_index("state")
    place = jnp.stack([at // 2, at % 2, lax.axis_index("tm")]).astype(jnp.int32)
    swap = [(i, i ^ 1) for i in range(axis)]
    shift = {k: [(i, (i + 2 * k) % axis) for i in range(axis)] for k in (1, 2, 3)}
    columns = [[2 * x + core for x in range(axis // 2)] for core in range(2)]
    work = 2 * rows * sensors * states

    far = (
        load, cotangent.reshape(rows, sensors), gain, readings.reshape(rows, sensors),
        inputs.reshape(rows, features), encoder_in, encoder_out,
    )
    load_weights, gain_weights, keep, send, mask = call(
        front_kernel,
        (
            struct((states, sensors), BF16),
            struct((sensors, states), BF16),
            struct((axis // 2, 2, rows, BLK), F32),
            struct((axis // 2, 2, rows, BLK), BF16),
            struct((rows, blocks), F32),
        ),
        (place, pattern.T, available.transpose(0, 2, 1), *far),
        scratch=[pltpu.VMEM(a.shape, a.dtype) for a in far] + [pltpu.SemaphoreType.DMA((len(far),))],
        smem=2,
        hbm=len(far),
        flops=2 * work,
    )
    came = lax.ppermute(send, "state", swap)
    full, segments = struct((rows, BLK), F32), struct((traces, SEG, BLK), F32)
    keep_r, keep_s, root, ahead_p, filt_p, rise_p, fall_p, seg_r, seg_s = call(
        functools.partial(decay_kernel, traces, steps),
        (full,) * 7 + (segments,) * 2,
        (retain.reshape(-1, steps), smooth.reshape(-1, steps)),
    )
    decays = (keep_r, keep_s, root, ahead_p, filt_p, rise_p, fall_p, seg_r, seg_s)
    keep, decays = lax.optimization_barrier((keep, decays))
    keep_r, keep_s, root, ahead_p, filt_p, rise_p, fall_p, seg_r, seg_s = decays
    sums, own = call(
        merge_kernel,
        (struct(send.shape, BF16), struct((2, rows, BLK), F32)),
        (place, keep, came),
        smem=1,
    )
    sums = lax.all_to_all(sums, "state", 0, 0, axis_index_groups=columns)
    scanned, pulled, before, parcel = call(
        functools.partial(scan_kernel, traces, steps),
        (full, full, struct((4, traces, 2, SEG, BLK), F32), struct((times, 2 * SEG, BLK), F32)),
        (place, own, sums, keep_r, keep_s, root, seg_r, seg_s),
        scratch=[pltpu.VMEM((rows, BLK), F32)] * 2 + [pltpu.VMEM((2, 2, SEG, BLK), F32)],
        smem=1,
    )
    parcel = lax.all_to_all(parcel, "tm", 0, 0)
    half = struct((rows, BLK), BF16)
    states_bf, grads_bf = call(
        functools.partial(settle_kernel, traces, steps),
        (half, half),
        (place, parcel, before, scanned, pulled, root, ahead_p, filt_p, rise_p, fall_p),
        scratch=[pltpu.VMEM((2, rows, BLK), F32), pltpu.VMEM((2, SEG, BLK), F32)],
        smem=1,
    )

    def across(piece):
        return [piece] + [lax.ppermute(piece, "state", shift[k]) for k in (1, 2, 3)]

    def project(dims, masked, same, weights):
        other = [lax.ppermute(one, "state", swap) for one in same]
        (out,) = call(
            functools.partial(project_kernel, dims, masked),
            (struct((rows, sensors), BF16),),
            (place, *same, *other, weights, mask),
            scratch=[pltpu.VMEM((rows, states), BF16), pltpu.VMEM((rows, sensors), BF16), pltpu.SemaphoreType.DMA((4,))],
            smem=1,
            hbm_out=True,
            flops=work,
        )
        return out

    all_states, all_grads = across(states_bf), across(grads_bf)
    predicted = project(NN, False, all_states, load_weights)
    predicted, all_grads = lax.optimization_barrier((predicted, all_grads))
    sensor_grad = project(NT, True, all_grads, gain_weights)
    return predicted.reshape(readings.shape), sensor_grad.reshape(readings.shape)


def solution(mesh):
    placed = (
        P(None, "tm", None),
        P(None, "state"),
        P("state", None),
        P(None, "tm", "state"),
        P(None, "tm", "state"),
        P("state", None),
        P("state", None, None, None),
        P("state", None, None, None),
        P("state", None, "tm"),
        P("state", None, "tm"),
        P(None, "tm", "state"),
    )
    return jax.shard_map(
        local,
        mesh=mesh,
        in_specs=placed,
        out_specs=(P(None, "tm", "state"), P(None, "tm", "state")),
        check_vma=False,
    )
```

profile of v0, /device:TPU:1, one launch (start us, length us, event | category | flops | bytes accessed | tf_op | source)
XLA Modules:
  0.0 84.8 jit_solution(13478669970628655594)
XLA Ops:
  0.6 0.1 pad_add_fusion.place
  0.7 0.0 copy-start.2
  0.7 0.7 copy-done.2
  1.4 0.0 copy-start.3
  1.4 0.7 copy-done.3
  2.1 0.0 copy-start
  2.1 0.0 copy-start.1
  2.1 7.0 %shard_map.122 = (bf16[1024,1024]{1,0:T(8,128)(2,1)S(1)}, bf16[1024,1024]{1,0:T(8,128)(2,1)S(1)}, f32[4,2,512,128]{3,2,1,0:T(8,128)S(1)}, bf16[4,2,512,128]{3,2,1,0:T(8,128)(2,1)S(1)}, f32[512,8]{1,0:T(8,128)S(1)}) custom-call(s32[3]{0:T(128)S(1)} %pad_add_fusion.place, s32[4,8]{1,0:T(4,128)S(1)} %bitcast.15, s32[4,8,128]{2,1,0:T(8,128)S(1)} %bitcast.14, ...), custom_call_target="tpu_custom_call" | custom-call | flops 2147483648 | bytes 12484748 | tf_op jit(solution)/shard_map/pallas_call | solution.py:23
  9.2 3.3 %collective-permute-start = (bf16[4,2,512,128]{3,2,1,0:T(8,128)(2,1)S(1)}, bf16[4,2,512,128]{3,2,1,0:T(8,128)(2,1)S(1)}, u32[]{:S(2)}, u32[]{:S(2)}) collective-permute-start(bf16[4,2,512,128]{3,2,1,0:T(8,128)(2,1)S(1)} %get-tuple-element.50), channel_id=1, source_target_pairs={{0,1},{1,0},{2,3},{3,2},{4,5},{5,4},{6,7},{7,6},{8,9},{9,8},{10,11... | collective-permute-start | bytes 3145736 | tf_op jit(solution)/shard_map/ppermute | solution.py:279
  12.5 0.0 copy-done
  12.5 0.0 copy-done.1
  12.5 0.6 shard_map.123
  13.1 1.7 %collective-permute-done.came = bf16[4,2,512,128]{3,2,1,0:T(8,128)(2,1)S(1)} collective-permute-done((bf16[4,2,512,128]{3,2,1,0:T(8,128)(2,1)S(1)}, bf16[4,2,512,128]{3,2,1,0:T(8,128)(2,1)S(1)}, u32[]{:S(2)}, u32[]{:S(2)}) %collective-permute-start) | collective-permute-done | bytes 1048608 | tf_op jit(solution)/shard_map/ppermute | solution.py:279
  14.7 0.8 shard_map.124
  15.5 17.2 %all_to_all.10.came = bf16[4,2,512,128]{3,2,1,0:T(8,128)(2,1)S(1)} all-to-all(bf16[4,2,512,128]{3,2,1,0:T(8,128)(2,1)S(1)} %get-tuple-element.52), channel_id=1, replica_groups={{0,2,4,6},{1,3,5,7},{8,10,12,14},{9,11,13,15},{16,18,20,22},{17,19,21,2..., dimensions={0} | all-to-all | bytes 2097152 | tf_op jit(solution)/shard_map/all_to_all | solution.py:295
  32.8 1.7 %shard_map.125 = (f32[512,128]{1,0:T(8,128)S(1)}, f32[512,128]{1,0:T(8,128)S(1)}, f32[4,4,2,8,128]{4,3,2,1,0:T(8,128)S(1)}, f32[32,16,128]{2,1,0:T(8,128)S(1)}) custom-call(s32[3]{0:T(128)S(1)} %pad_add_fusion.place, f32[2,512,128]{2,1,0:T(8,128)S(1)} %get-tuple-element.51.own, bf16[4,2,512,128]{3,2,1,0:T(8,128)(2,1)S(1)} %all_to_all.10.came, ...), custom_call_target="tpu_custom_call" | custom-call | bytes 3309580 | tf_op jit(solution)/shard_map/pallas_call | solution.py:23
  34.5 20.5 %all_to_all.11.parcel = f32[32,16,128]{2,1,0:T(8,128)S(1)} all-to-all(f32[32,16,128]{2,1,0:T(8,128)S(1)} %get-tuple-element.58), channel_id=1, replica_groups=mesh['tm'=32,'state'=8] {'tm'}, dimensions={0} | all-to-all | bytes 524288 | tf_op jit(solution)/shard_map/all_to_all | solution.py:303
  55.0 1.3 %shard_map.126 = (bf16[512,128]{1,0:T(8,128)(2,1)S(1)}, bf16[512,128]{1,0:T(8,128)(2,1)S(1)}) custom-call(s32[3]{0:T(128)S(1)} %pad_add_fusion.place, f32[32,16,128]{2,1,0:T(8,128)S(1)} %all_to_all.11.parcel, f32[4,4,2,8,128]{4,3,2,1,0:T(8,128)S(1)} %get-tuple-element.59.before, f32[512,128]{1,0:T(8,128)S(1)} %get-tuple-element.60.states, ...), custom_call_target="tpu_custom_call" | custom-call | bytes 2490380 | tf_op jit(solution)/shard_map/pallas_call | solution.py:23
  56.3 1.0 %collective-permute-start.3 = (bf16[512,128]{1,0:T(8,128)(2,1)S(1)}, bf16[512,128]{1,0:T(8,128)(2,1)S(1)}, u32[]{:S(2)}, u32[]{:S(2)}) collective-permute-start(bf16[512,128]{1,0:T(8,128)(2,1)S(1)} %get-tuple-element.66.refs_0_), channel_id=1, source_target_pairs={{0,6},{1,7},{2,0},{3,1},{4,2},{5,3},{6,4},{7,5},{8,14},{9,15},{10,... | collective-permute-start | bytes 393224 | tf_op jit(solution)/shard_map/ppermute | solution.py:314
  57.2 1.2 %collective-permute-start.2 = (bf16[512,128]{1,0:T(8,128)(2,1)S(1)}, bf16[512,128]{1,0:T(8,128)(2,1)S(1)}, u32[]{:S(2)}, u32[]{:S(2)}) collective-permute-start(bf16[512,128]{1,0:T(8,128)(2,1)S(1)} %get-tuple-element.66.refs_0_), channel_id=1, source_target_pairs={{0,4},{1,5},{2,6},{3,7},{4,0},{5,1},{6,2},{7,3},{8,12},{9,13},{10,... | collective-permute-start | bytes 393224 | tf_op jit(solution)/shard_map/ppermute | solution.py:314
  58.4 0.0 collective-permute-start.1
  58.4 4.3 %collective-permute-start.4 = (bf16[512,128]{1,0:T(8,128)(2,1)S(1)}, bf16[512,128]{1,0:T(8,128)(2,1)S(1)}, u32[]{:S(2)}, u32[]{:S(2)}) collective-permute-start(bf16[512,128]{1,0:T(8,128)(2,1)S(1)} %get-tuple-element.66.refs_0_), channel_id=1, source_target_pairs={{0,1},{1,0},{2,3},{3,2},{4,5},{5,4},{6,7},{7,6},{8,9},{9,8},{10,11... | collective-permute-start | bytes 393224 | tf_op jit(solution)/shard_map/ppermute | solution.py:317
  62.7 0.0 collective-permute-done.3.refs_3_
  62.7 2.3 %collective-permute-start.7 = (bf16[512,128]{1,0:T(8,128)(2,1)S(1)}, bf16[512,128]{1,0:T(8,128)(2,1)S(1)}, u32[]{:S(2)}, u32[]{:S(2)}) collective-permute-start(bf16[512,128]{1,0:T(8,128)(2,1)S(1)} %collective-permute-done.3.refs_3_), channel_id=1, source_target_pairs={{0,1},{1,0},{2,3},{3,2},{4,5},{5,4},{6,7},{7,6},{8,9},{9,8},{10,11... | collective-permute-start | bytes 393224 | tf_op jit(solution)/shard_map/ppermute | solution.py:317
  65.1 0.0 collective-permute-done.2.refs_2_
  65.1 2.7 %collective-permute-start.6 = (bf16[512,128]{1,0:T(8,128)(2,1)S(1)}, bf16[512,128]{1,0:T(8,128)(2,1)S(1)}, u32[]{:S(2)}, u32[]{:S(2)}) collective-permute-start(bf16[512,128]{1,0:T(8,128)(2,1)S(1)} %collective-permute-done.2.refs_2_), channel_id=1, source_target_pairs={{0,1},{1,0},{2,3},{3,2},{4,5},{5,4},{6,7},{7,6},{8,9},{9,8},{10,11... | collective-permute-start | bytes 393224 | tf_op jit(solution)/shard_map/ppermute | solution.py:317
  67.8 0.0 collective-permute-done.1.refs_1_
  67.8 1.4 %collective-permute-start.5 = (bf16[512,128]{1,0:T(8,128)(2,1)S(1)}, bf16[512,128]{1,0:T(8,128)(2,1)S(1)}, u32[]{:S(2)}, u32[]{:S(2)}) collective-permute-start(bf16[512,128]{1,0:T(8,128)(2,1)S(1)} %collective-permute-done.1.refs_1_), channel_id=1, source_target_pairs={{0,1},{1,0},{2,3},{3,2},{4,5},{5,4},{6,7},{7,6},{8,9},{9,8},{10,11... | collective-permute-start | bytes 393224 | tf_op jit(solution)/shard_map/ppermute | solution.py:317
  69.1 0.3 collective-permute-start.10
  69.5 0.0 collective-permute-done.4.refs_4_
  69.5 1.1 %collective-permute-start.9 = (bf16[512,128]{1,0:T(8,128)(2,1)S(1)}, bf16[512,128]{1,0:T(8,128)(2,1)S(1)}, u32[]{:S(2)}, u32[]{:S(2)}) collective-permute-start(bf16[512,128]{1,0:T(8,128)(2,1)S(1)} %get-tuple-element.71.refs_0_), channel_id=1, source_target_pairs={{0,4},{1,5},{2,6},{3,7},{4,0},{5,1},{6,2},{7,3},{8,12},{9,13},{10,... | collective-permute-start | bytes 393224 | tf_op jit(solution)/shard_map/ppermute | solution.py:314
  70.6 0.0 collective-permute-done.7.refs_7_
  70.6 0.6 collective-permute-start.8
  71.2 0.0 collective-permute-done.6.refs_6_
  71.2 0.0 collective-permute-done.5.refs_5_
  71.2 3.0 %shard_map.127 = bf16[512,1024]{1,0:T(8,128)(2,1)} custom-call(s32[3]{0:T(128)S(1)} %pad_add_fusion.place, bf16[512,128]{1,0:T(8,128)(2,1)S(1)} %get-tuple-element.66.refs_0_, bf16[512,128]{1,0:T(8,128)(2,1)S(1)} %collective-permute-done.1.refs_1_, bf16[512,128]{1,0:T(8,128)(2,1)S(1)} %collective-permute-done.2.refs_2_, ...), custom_call_target="tpu_custom_call" | custom-call | flops 1073741824 | bytes 4210700 | tf_op jit(solution)/shard_map/pallas_call | solution.py:23
  74.2 0.0 collective-permute-done.10.refs_3_
  74.2 1.5 %collective-permute-done.9.refs_2_ = bf16[512,128]{1,0:T(8,128)(2,1)S(1)} collective-permute-done((bf16[512,128]{1,0:T(8,128)(2,1)S(1)}, bf16[512,128]{1,0:T(8,128)(2,1)S(1)}, u32[]{:S(2)}, u32[]{:S(2)}) %collective-permute-start.9) | collective-permute-done | bytes 131104 | tf_op jit(solution)/shard_map/ppermute | solution.py:314
  75.8 3.5 %collective-permute-done.8.refs_1_ = bf16[512,128]{1,0:T(8,128)(2,1)S(1)} collective-permute-done((bf16[512,128]{1,0:T(8,128)(2,1)S(1)}, bf16[512,128]{1,0:T(8,128)(2,1)S(1)}, u32[]{:S(2)}, u32[]{:S(2)}) %collective-permute-start.8) | collective-permute-done | bytes 131104 | tf_op jit(solution)/shard_map/ppermute | solution.py:314
  79.2 0.5 collective-permute-start.11
  79.7 0.0 collective-permute-start.12
  79.7 0.5 collective-permute-start.13
  80.2 0.0 collective-permute-start.14
  80.2 0.5 collective-permute-done.11.refs_4_
  80.7 0.4 collective-permute-done.12.refs_5_
  81.1 0.2 collective-permute-done.13.refs_6_
  81.3 0.3 collective-permute-done.14.refs_7_
  81.6 3.0 %shard_map.128 = bf16[512,1024]{1,0:T(8,128)(2,1)} custom-call(s32[3]{0:T(128)S(1)} %pad_add_fusion.place, bf16[512,128]{1,0:T(8,128)(2,1)S(1)} %get-tuple-element.71.refs_0_, bf16[512,128]{1,0:T(8,128)(2,1)S(1)} %collective-permute-done.8.refs_1_, bf16[512,128]{1,0:T(8,128)(2,1)S(1)} %collective-permute-done.9.refs_2_, ...), custom_call_target="tpu_custom_call" | custom-call | flops 1073741824 | bytes 4210700 | tf_op jit(solution)/shard_map/pallas_call | solution.py:23
Async XLA Ops:
  0.7 0.7 copy-start.2
  1.4 0.7 copy-start.3
  2.1 10.3 %copy-start = (f32[128,4,128]{2,1,0:T(4,128)S(1)}, f32[128,4,128]{2,1,0:T(4,128)}, u32[]{:S(2)}) copy-start(f32[128,4,128]{2,1,0:T(4,128)} %param.19) | copy-start | bytes 786436
  2.1 10.3 %copy-start.1 = (f32[128,4,128]{2,1,0:T(4,128)S(1)}, f32[128,4,128]{2,1,0:T(4,128)}, u32[]{:S(2)}) copy-start(f32[128,4,128]{2,1,0:T(4,128)} %param.20) | copy-start | bytes 786436
  9.2 5.6 %collective-permute-start = (bf16[4,2,512,128]{3,2,1,0:T(8,128)(2,1)S(1)}, bf16[4,2,512,128]{3,2,1,0:T(8,128)(2,1)S(1)}, u32[]{:S(2)}, u32[]{:S(2)}) collective-permute-start(bf16[4,2,512,128]{3,2,1,0:T(8,128)(2,1)S(1)} %get-tuple-element.50), channel_id=1, source_target_pairs={{0,1},{1,0},{2,3},{3,2},{4,5},{5,4},{6,7},{7,6},{8,9},{9,8},{10,11... | collective-permute-start | bytes 3145736 | tf_op jit(solution)/shard_map/ppermute | solution.py:279
  56.3 6.5 %collective-permute-start.3 = (bf16[512,128]{1,0:T(8,128)(2,1)S(1)}, bf16[512,128]{1,0:T(8,128)(2,1)S(1)}, u32[]{:S(2)}, u32[]{:S(2)}) collective-permute-start(bf16[512,128]{1,0:T(8,128)(2,1)S(1)} %get-tuple-element.66.refs_0_), channel_id=1, source_target_pairs={{0,6},{1,7},{2,0},{3,1},{4,2},{5,3},{6,4},{7,5},{8,14},{9,15},{10,... | collective-permute-start | bytes 393224 | tf_op jit(solution)/shard_map/ppermute | solution.py:314
  57.2 7.8 %collective-permute-start.2 = (bf16[512,128]{1,0:T(8,128)(2,1)S(1)}, bf16[512,128]{1,0:T(8,128)(2,1)S(1)}, u32[]{:S(2)}, u32[]{:S(2)}) collective-permute-start(bf16[512,128]{1,0:T(8,128)(2,1)S(1)} %get-tuple-element.66.refs_0_), channel_id=1, source_target_pairs={{0,4},{1,5},{2,6},{3,7},{4,0},{5,1},{6,2},{7,3},{8,12},{9,13},{10,... | collective-permute-start | bytes 393224 | tf_op jit(solution)/shard_map/ppermute | solution.py:314
  58.4 9.4 %collective-permute-start.1 = (bf16[512,128]{1,0:T(8,128)(2,1)S(1)}, bf16[512,128]{1,0:T(8,128)(2,1)S(1)}, u32[]{:S(2)}, u32[]{:S(2)}) collective-permute-start(bf16[512,128]{1,0:T(8,128)(2,1)S(1)} %get-tuple-element.66.refs_0_), channel_id=1, source_target_pairs={{0,2},{1,3},{2,4},{3,5},{4,6},{5,7},{6,0},{7,1},{8,10},{9,11},{10,... | collective-permute-start | bytes 393224 | tf_op jit(solution)/shard_map/ppermute | solution.py:314
  58.4 11.1 %collective-permute-start.4 = (bf16[512,128]{1,0:T(8,128)(2,1)S(1)}, bf16[512,128]{1,0:T(8,128)(2,1)S(1)}, u32[]{:S(2)}, u32[]{:S(2)}) collective-permute-start(bf16[512,128]{1,0:T(8,128)(2,1)S(1)} %get-tuple-element.66.refs_0_), channel_id=1, source_target_pairs={{0,1},{1,0},{2,3},{3,2},{4,5},{5,4},{6,7},{7,6},{8,9},{9,8},{10,11... | collective-permute-start | bytes 393224 | tf_op jit(solution)/shard_map/ppermute | solution.py:317
  62.7 7.9 %collective-permute-start.7 = (bf16[512,128]{1,0:T(8,128)(2,1)S(1)}, bf16[512,128]{1,0:T(8,128)(2,1)S(1)}, u32[]{:S(2)}, u32[]{:S(2)}) collective-permute-start(bf16[512,128]{1,0:T(8,128)(2,1)S(1)} %collective-permute-done.3.refs_3_), channel_id=1, source_target_pairs={{0,1},{1,0},{2,3},{3,2},{4,5},{5,4},{6,7},{7,6},{8,9},{9,8},{10,11... | collective-permute-start | bytes 393224 | tf_op jit(solution)/shard_map/ppermute | solution.py:317
  65.1 6.1 %collective-permute-start.6 = (bf16[512,128]{1,0:T(8,128)(2,1)S(1)}, bf16[512,128]{1,0:T(8,128)(2,1)S(1)}, u32[]{:S(2)}, u32[]{:S(2)}) collective-permute-start(bf16[512,128]{1,0:T(8,128)(2,1)S(1)} %collective-permute-done.2.refs_2_), channel_id=1, source_target_pairs={{0,1},{1,0},{2,3},{3,2},{4,5},{5,4},{6,7},{7,6},{8,9},{9,8},{10,11... | collective-permute-start | bytes 393224 | tf_op jit(solution)/shard_map/ppermute | solution.py:317
  67.8 3.4 %collective-permute-start.5 = (bf16[512,128]{1,0:T(8,128)(2,1)S(1)}, bf16[512,128]{1,0:T(8,128)(2,1)S(1)}, u32[]{:S(2)}, u32[]{:S(2)}) collective-permute-start(bf16[512,128]{1,0:T(8,128)(2,1)S(1)} %collective-permute-done.1.refs_1_), channel_id=1, source_target_pairs={{0,1},{1,0},{2,3},{3,2},{4,5},{5,4},{6,7},{7,6},{8,9},{9,8},{10,11... | collective-permute-start | bytes 393224 | tf_op jit(solution)/shard_map/ppermute | solution.py:317
  69.1 5.1 %collective-permute-start.10 = (bf16[512,128]{1,0:T(8,128)(2,1)S(1)}, bf16[512,128]{1,0:T(8,128)(2,1)S(1)}, u32[]{:S(2)}, u32[]{:S(2)}) collective-permute-start(bf16[512,128]{1,0:T(8,128)(2,1)S(1)} %get-tuple-element.71.refs_0_), channel_id=1, source_target_pairs={{0,6},{1,7},{2,0},{3,1},{4,2},{5,3},{6,4},{7,5},{8,14},{9,15},{10,... | collective-permute-start | bytes 393224 | tf_op jit(solution)/shard_map/ppermute | solution.py:314
  69.5 6.3 %collective-permute-start.9 = (bf16[512,128]{1,0:T(8,128)(2,1)S(1)}, bf16[512,128]{1,0:T(8,128)(2,1)S(1)}, u32[]{:S(2)}, u32[]{:S(2)}) collective-permute-start(bf16[512,128]{1,0:T(8,128)(2,1)S(1)} %get-tuple-element.71.refs_0_), channel_id=1, source_target_pairs={{0,4},{1,5},{2,6},{3,7},{4,0},{5,1},{6,2},{7,3},{8,12},{9,13},{10,... | collective-permute-start | bytes 393224 | tf_op jit(solution)/shard_map/ppermute | solution.py:314
  70.6 8.6 %collective-permute-start.8 = (bf16[512,128]{1,0:T(8,128)(2,1)S(1)}, bf16[512,128]{1,0:T(8,128)(2,1)S(1)}, u32[]{:S(2)}, u32[]{:S(2)}) collective-permute-start(bf16[512,128]{1,0:T(8,128)(2,1)S(1)} %get-tuple-element.71.refs_0_), channel_id=1, source_target_pairs={{0,2},{1,3},{2,4},{3,5},{4,6},{5,7},{6,0},{7,1},{8,10},{9,11},{10,... | collective-permute-start | bytes 393224 | tf_op jit(solution)/shard_map/ppermute | solution.py:314
  79.2 1.5 %collective-permute-start.11 = (bf16[512,128]{1,0:T(8,128)(2,1)S(1)}, bf16[512,128]{1,0:T(8,128)(2,1)S(1)}, u32[]{:S(2)}, u32[]{:S(2)}) collective-permute-start(bf16[512,128]{1,0:T(8,128)(2,1)S(1)} %get-tuple-element.71.refs_0_), channel_id=1, source_target_pairs={{0,1},{1,0},{2,3},{3,2},{4,5},{5,4},{6,7},{7,6},{8,9},{9,8},{10,11... | collective-permute-start | bytes 393224 | tf_op jit(solution)/shard_map/ppermute | solution.py:317
  79.7 1.3 %collective-permute-start.12 = (bf16[512,128]{1,0:T(8,128)(2,1)S(1)}, bf16[512,128]{1,0:T(8,128)(2,1)S(1)}, u32[]{:S(2)}, u32[]{:S(2)}) collective-permute-start(bf16[512,128]{1,0:T(8,128)(2,1)S(1)} %collective-permute-done.8.refs_1_), channel_id=1, source_target_pairs={{0,1},{1,0},{2,3},{3,2},{4,5},{5,4},{6,7},{7,6},{8,9},{9,8},{10,11... | collective-permute-start | bytes 393224 | tf_op jit(solution)/shard_map/ppermute | solution.py:317
  79.7 1.5 %collective-permute-start.13 = (bf16[512,128]{1,0:T(8,128)(2,1)S(1)}, bf16[512,128]{1,0:T(8,128)(2,1)S(1)}, u32[]{:S(2)}, u32[]{:S(2)}) collective-permute-start(bf16[512,128]{1,0:T(8,128)(2,1)S(1)} %collective-permute-done.9.refs_2_), channel_id=1, source_target_pairs={{0,1},{1,0},{2,3},{3,2},{4,5},{5,4},{6,7},{7,6},{8,9},{9,8},{10,11... | collective-permute-start | bytes 393224 | tf_op jit(solution)/shard_map/ppermute | solution.py:317
  80.2 1.3 %collective-permute-start.14 = (bf16[512,128]{1,0:T(8,128)(2,1)S(1)}, bf16[512,128]{1,0:T(8,128)(2,1)S(1)}, u32[]{:S(2)}, u32[]{:S(2)}) collective-permute-start(bf16[512,128]{1,0:T(8,128)(2,1)S(1)} %collective-permute-done.10.refs_3_), channel_id=1, source_target_pairs={{0,1},{1,0},{2,3},{3,2},{4,5},{5,4},{6,7},{7,6},{8,9},{9,8},{10,11... | collective-permute-start | bytes 393224 | tf_op jit(solution)/shard_map/ppermute | solution.py:317
where the time goes:
time: 85 us; the launch traced here: 84.8 us
  blocking collectives  37.8 us (44%)
  starting transfers between devices  19.2 us (23%)
  Pallas kernels  17.4 us (20%)
  waiting for transfers between devices  8.04 us (9%)
  local copies, waits for them, and re-layouts  1.41 us (2%)
  between operations  0.88 us (1%)
    all_to_all x1, blocking collectives, local(): parcel = lax.all_to_all(parcel, 'tm', 0, 0)  20.5 us
    pallas_call x7, Pallas kernels, call(): pl.pallas_call(kernel, out_shape=outs, in_specs=[scalar] * smem + [vmem]...  17.4 us
    all_to_all x1, blocking collectives, local(): sums = lax.all_to_all(sums, 'state', 0, 0, axis_index_groups=columns)  17.2 us
    ppermute x8, starting transfers between devices, project(): other = [lax.ppermute(one, 'state', swap) for one in same]  11.7 us
    ppermute x6, waiting for transfers between devices, across(): return [piece] + [lax.ppermute(piece, 'state', shift[k]) for k in (1, 2, 3)]  5.01 us
    ppermute x6, starting transfers between devices, across(): return [piece] + [lax.ppermute(piece, 'state', shift[k]) for k in (1, 2, 3)]  4.19 us
    ppermute x1, starting transfers between devices, local(): came = lax.ppermute(send, 'state', swap)  3.29 us
  transfers between devices with their start and end apart: 15, of which 7 were waited for; matrix products, arithmetic and copies ran while one was open for 0% of the time, Pallas kernels for 4%

commit v1 on v0

--- a/solution.py
+++ b/solution.py
@@ -28,7 +28,11 @@
         scratch_shapes=list(scratch),
         compiler_params=pltpu.CompilerParams(vmem_limit_bytes=VMEM),
         cost_estimate=pl.CostEstimate(flops=flops, bytes_accessed=moved, transcendentals=0),
-    )(*[pltpu.with_memory_space_constraint(a, pltpu.HBM) if i >= len(operands) - hbm else a for i, a in enumerate(operands)])
+    )(*operands[: len(operands) - hbm], *[in_hbm(a) for a in operands[len(operands) - hbm :]])
+
+
+def in_hbm(array):
+    return pltpu.with_memory_space_constraint(array, pltpu.HBM)
 
 
 def struct(shape, dtype):
@@ -36,14 +40,14 @@
 
 
 def front_kernel(
-    place, pattern, available, load_far, cot_far, gain_far, readings_far, rows_far, enc_in_far, enc_out_far,
+    place, pattern, load_far, cot_far, gain_far, available_far, readings_far, rows_far, enc_in_far, enc_out_far,
     load_weights, gain_weights, keep, send, mask,
-    load, cotangent, gain, lhs, rows_in, enc_in, enc_out, sems,
+    load, cotangent, gain, available, lhs, rows_in, enc_in, enc_out, sems,
 ):
     core = place[1]
     pairs = (
-        (load_far, load), (cot_far, cotangent), (gain_far, gain), (readings_far, lhs),
-        (rows_far, rows_in), (enc_in_far, enc_in), (enc_out_far, enc_out),
+        (load_far, load), (cot_far, cotangent), (gain_far, gain), (available_far, available),
+        (readings_far, lhs), (rows_far, rows_in), (enc_in_far, enc_in), (enc_out_far, enc_out),
     )
     copies = [pltpu.make_async_copy(far, near, sems.at[i]) for i, (far, near) in enumerate(pairs)]
     for copy in copies:
@@ -52,8 +56,6 @@
     gain_weights[...] = jnp.zeros_like(gain_weights)
     traces, blocks, steps = available.shape
     reads = pattern.shape[0]
-    for b in range(traces):
-        mask[b * steps : (b + 1) * steps, :] = available[b].astype(F32).T
 
     def split(which, at, total):
         low, high = total[:, :BLK], total[:, BLK:]
@@ -80,6 +82,8 @@
             gain_weights[q * BLK : (q + 1) * BLK, pl.ds(column, BLK)] = gain[q, k]
     for copy in copies[3:]:
         copy.wait()
+    for b in range(traces):
+        mask[b * steps : (b + 1) * steps, :] = available[b].astype(F32).T
     for q in range(blocks):
         lhs[:, q * BLK : (q + 1) * BLK] = lhs[:, q * BLK : (q + 1) * BLK] * mask[:, q : q + 1].astype(BF16)
     hidden = jax.nn.gelu(jnp.dot(rows_in[...], enc_in[...], preferred_element_type=F32)).astype(BF16)
@@ -94,10 +98,11 @@
     lax.fori_loop(0, 4, drive_columns, 0)
 
 
-def merge_kernel(place, keep, came, parcel, own):
-    for at in range(parcel.shape[0]):
-        parcel[at] = (keep[at] + came[at].astype(F32)).astype(BF16)
+def merge_kernel(place, keep, came, own, *pieces):
     own[...] = keep[place[0]] + came[place[0]].astype(F32)
+    for k, piece in enumerate(pieces):
+        at = lax.rem(place[0] + k + 1, keep.shape[0])
+        piece[...] = (keep[at] + came[at].astype(F32)).astype(BF16)
 
 
 def rows_of(b, u, steps):
@@ -148,13 +153,13 @@
 
 def scan_kernel(
     traces, steps, place,
-    own, came, keep_r, keep_s, root, seg_r, seg_s,
+    own, one, two, three, keep_r, keep_s, root, seg_r, seg_s,
     states, grads, before, parcel,
     source, pull, ends,
 ):
-    others = [lax.rem(place[0] + k, 4) for k in (1, 2, 3)]
-    source[...] = root[...] * (own[0] + sum(came[other, 0].astype(F32) for other in others))
-    pull[...] = own[1] + sum(came[other, 1].astype(F32) for other in others)
+    pieces = (one, two, three)
+    source[...] = root[...] * (own[0] + sum(piece[0].astype(F32) for piece in pieces))
+    pull[...] = own[1] + sum(piece[1].astype(F32) for piece in pieces)
     for b in range(traces):
         filt = jnp.zeros((SEG, BLK), F32)
         rise, ahead, fall = filt, filt, filt
@@ -194,7 +199,7 @@
 def settle_kernel(
     traces, steps, place,
     parcel, before, states, grads, root, ahead_p, filt_p, rise_p, fall_p,
-    states_bf, grads_bf,
+    smoothed,
     sums, carry,
 ):
     me, length = place[2], parcel.shape[0]
@@ -215,31 +220,42 @@
             at = rows_of(b, u, steps)
             sums[0, at, :] = states[at, :] + filt_p[at, :] * filt + ahead_p[at, :] * ahead
             sums[1, at, :] = root[at, :] * (grads[at, :] + rise_p[at, :] * rise + fall_p[at, :] * fall)
-    states_bf[...] = sums[0].astype(BF16)
-    grads_bf[...] = sums[1].astype(BF16)
-
-
-def project_kernel(dims, masked, place, *refs):
-    *pieces, weights, mask, out, lhs, stage, sems = refs
-    x, core = place[0], place[1]
-    for k in range(4):
-        column = 2 * lax.rem(x - k + 4, 4)
-        for side in range(2):
-            block = column + (core if side == 0 else 1 - core)
-            lhs[:, pl.ds(pl.multiple_of(block * BLK, BLK), BLK)] = pieces[side * 4 + k][...]
+    smoothed[...] = sums[...].astype(BF16)
+
+
+def project_kernel(shift, last, place, mine, partner, load_weights, gain_weights, mask, *refs):
+    before, refs = ((), refs) if shift == 0 else (refs[:2], refs[2:])
+    outs, lhs, *rest = refs[:2], *refs[2:]
+    core = place[1]
+    block = pl.multiple_of(2 * BLK * lax.rem(place[0] - shift + 4, 4), 2 * BLK)
+    states = pl.ds(block, 2 * BLK)
     copies = []
-    for at in range(4):
-        window = slice(at * 2 * BLK, (at + 1) * 2 * BLK)
-        chosen = weights[window, :] if dims is NT else weights[:, window]
-        total = lax.dot_general(lhs[...], chosen, dims, preferred_element_type=F32)
-        for half in range(2):
-            q = 2 * at + half
-            piece = total[:, half * BLK : (half + 1) * BLK]
-            if masked:
-                piece = piece * mask[:, q : q + 1]
-            stage[:, q * BLK : (q + 1) * BLK] = piece.astype(BF16)
-        copies.append(pltpu.make_async_copy(stage.at[:, window], out.at[:, window], sems.at[at]))
-        copies[-1].start()
+    for which in range(2):
+        for side, piece in enumerate((mine, partner)):
+            column = pl.multiple_of(BLK * (core if side == 0 else 1 - core), BLK)
+            lhs[which, :, pl.ds(column, BLK)] = piece[which]
+        for at in range(4):
+            window = slice(at * 2 * BLK, (at + 1) * 2 * BLK)
+            if which == 0:
+                total = lax.dot_general(lhs[0], load_weights[states, window], NN, preferred_element_type=F32)
+            else:
+                total = lax.dot_general(lhs[1], gain_weights[window, states], NT, preferred_element_type=F32)
+            if before:
+                total = before[which][:, window] + total
+            if not last:
+                outs[which][:, window] = total
+                continue
+            stage, sems = rest
+            for half in range(2):
+                q = 2 * at + half
+                piece = total[:, half * BLK : (half + 1) * BLK]
+                if which == 1:
+                    piece = piece * mask[:, q : q + 1]
+                stage[which, :, q * BLK : (q + 1) * BLK] = piece.astype(BF16)
+            copies.append(
+                pltpu.make_async_copy(stage.at[which, :, window], outs[which].at[:, window], sems.at[which, at])
+            )
+            copies[-1].start()
     for copy in copies:
         copy.wait()
 
@@ -253,13 +269,16 @@
     at = lax.axis_index("state")
     place = jnp.stack([at // 2, at % 2, lax.axis_index("tm")]).astype(jnp.int32)
     swap = [(i, i ^ 1) for i in range(axis)]
-    shift = {k: [(i, (i + 2 * k) % axis) for i in range(axis)] for k in (1, 2, 3)}
-    columns = [[2 * x + core for x in range(axis // 2)] for core in range(2)]
+
+    def across(pieces):
+        moved = {k: lax.ppermute(pieces[k - 1], "state", [(i, (i + 2 * k) % axis) for i in range(axis)]) for k in (1, 3, 2)}
+        return [moved[k] for k in (1, 2, 3)]
+
     work = 2 * rows * sensors * states
 
     far = (
-        load, cotangent.reshape(rows, sensors), gain, readings.reshape(rows, sensors),
-        inputs.reshape(rows, features), encoder_in, encoder_out,
+        load, cotangent.reshape(rows, sensors), gain, available.transpose(0, 2, 1),
+        readings.reshape(rows, sensors), inputs.reshape(rows, features), encoder_in, encoder_out,
     )
     load_weights, gain_weights, keep, send, mask = call(
         front_kernel,
@@ -270,7 +289,7 @@
             struct((axis // 2, 2, rows, BLK), BF16),
             struct((rows, blocks), F32),
         ),
-        (place, pattern.T, available.transpose(0, 2, 1), *far),
+        (place, in_hbm(pattern.T), *far),
         scratch=[pltpu.VMEM(a.shape, a.dtype) for a in far] + [pltpu.SemaphoreType.DMA((len(far),))],
         smem=2,
         hbm=len(far),
@@ -286,50 +305,45 @@
     decays = (keep_r, keep_s, root, ahead_p, filt_p, rise_p, fall_p, seg_r, seg_s)
     keep, decays = lax.optimization_barrier((keep, decays))
     keep_r, keep_s, root, ahead_p, filt_p, rise_p, fall_p, seg_r, seg_s = decays
-    sums, own = call(
-        merge_kernel,
-        (struct(send.shape, BF16), struct((2, rows, BLK), F32)),
-        (place, keep, came),
-        smem=1,
-    )
-    sums = lax.all_to_all(sums, "state", 0, 0, axis_index_groups=columns)
+    both = struct((2, rows, BLK), BF16)
+    own, *sums = call(merge_kernel, (struct(both.shape, F32),) + (both,) * 3, (place, keep, came), smem=1)
+    sums = across(sums)
     scanned, pulled, before, parcel = call(
         functools.partial(scan_kernel, traces, steps),
         (full, full, struct((4, traces, 2, SEG, BLK), F32), struct((times, 2 * SEG, BLK), F32)),
-        (place, own, sums, keep_r, keep_s, root, seg_r, seg_s),
+        (place, own, *sums, keep_r, keep_s, root, seg_r, seg_s),
         scratch=[pltpu.VMEM((rows, BLK), F32)] * 2 + [pltpu.VMEM((2, 2, SEG, BLK), F32)],
         smem=1,
     )
     parcel = lax.all_to_all(parcel, "tm", 0, 0)
-    half = struct((rows, BLK), BF16)
-    states_bf, grads_bf = call(
+    (smoothed,) = call(
         functools.partial(settle_kernel, traces, steps),
-        (half, half),
+        (both,),
         (place, parcel, before, scanned, pulled, root, ahead_p, filt_p, rise_p, fall_p),
         scratch=[pltpu.VMEM((2, rows, BLK), F32), pltpu.VMEM((2, SEG, BLK), F32)],
         smem=1,
     )
-
-    def across(piece):
-        return [piece] + [lax.ppermute(piece, "state", shift[k]) for k in (1, 2, 3)]
-
-    def project(dims, masked, same, weights):
-        other = [lax.ppermute(one, "state", swap) for one in same]
-        (out,) = call(
-            functools.partial(project_kernel, dims, masked),
-            (struct((rows, sensors), BF16),),
-            (place, *same, *other, weights, mask),
-            scratch=[pltpu.VMEM((rows, states), BF16), pltpu.VMEM((rows, sensors), BF16), pltpu.SemaphoreType.DMA((4,))],
+    same = [smoothed, *across([smoothed] * 3)]
+    totals = ()
+    for shift in (0, 1, 3, 2):
+        last = shift == 2
+        if shift == 1:
+            totals, same[1] = lax.optimization_barrier((totals, same[1]))
+            totals, same[3] = lax.optimization_barrier((totals, same[3]))
+        if shift == 3:
+            totals, same[2] = lax.optimization_barrier((totals, same[2]))
+        partner = lax.ppermute(same[shift], "state", swap)
+        totals = call(
+            functools.partial(project_kernel, shift, last),
+            (struct((rows, sensors), BF16 if last else F32),) * 2,
+            (place, same[shift], partner, load_weights, gain_weights, mask, *totals),
+            scratch=[pltpu.VMEM((2, rows, 2 * BLK), BF16)]
+            + ([pltpu.VMEM((2, rows, sensors), BF16), pltpu.SemaphoreType.DMA((2, 4))] if last else []),
             smem=1,
-            hbm_out=True,
-            flops=work,
+            hbm_out=last,
+            flops=work // 2,
         )
-        return out
-
-    all_states, all_grads = across(states_bf), across(grads_bf)
-    predicted = project(NN, False, all_states, load_weights)
-    predicted, all_grads = lax.optimization_barrier((predicted, all_grads))
-    sensor_grad = project(NT, True, all_grads, gain_weights)
+    predicted, sensor_grad = totals
     return predicted.reshape(readings.shape), sensor_grad.reshape(readings.shape)
 
 

time: 85 us -> 80.4 us (0.946)
  blocking collectives: 37.8 us -> 20.6 us
  waiting for transfers between devices: 8.04 us -> 24.8 us
  starting transfers between devices: 19.2 us -> 15.8 us
  local copies, waits for them, and re-layouts: 1.41 us -> 0.01 us
    all_to_all x1 -> x0, blocking collectives: 17.2 us -> none  [local(): sums = lax.all_to_all(sums, 'state', 0, 0, axis_index_groups=columns)]
    ppermute x14 -> x10, waiting for transfers between devices: 6.35 us -> 23.1 us  [the longest x6 23.1 us: across(): lax.ppermute(pieces[k - 1], 'state', [(i, (i + 2 * k) % axis) for i in ra...]
    ppermute x14 -> x10, starting transfers between devices: 15.9 us -> 12.5 us  [the longest x6 7.09 us: across(): lax.ppermute(pieces[k - 1], 'state', [(i, (i + 2 * k) % axis) for i in ra...]
    unnamed x8 -> x4, local copies, waits for them, and re-layouts: 1.41 us -> 0.01 us
    pallas_call x7 -> x9, Pallas kernels: 17.4 us -> 18.2 us  [call(): pl.pallas_call(kernel, out_shape=outs, in_specs=[scalar] * smem + [vmem]...]
  transfers between devices with their start and end apart: 15 -> 11, of which waited for: 7 -> 6; matrix products, arithmetic and copies ran while one was open for 0% -> 0% of each run, Pallas kernels for 4% -> 6%
where the time goes in v1:
time: 80.4 us; the launch traced here: 80.3 us
  waiting for transfers between devices  24.8 us (31%)
  blocking collectives  20.6 us (26%)
  Pallas kernels  18.2 us (23%)
  starting transfers between devices  15.8 us (20%)
  between operations  0.89 us (1%)
    ppermute x6, waiting for transfers between devices, across(): lax.ppermute(pieces[k - 1], 'state', [(i, (i + 2 * k) % axis) for i in ra...  23.1 us
    all_to_all x1, blocking collectives, local(): parcel = lax.all_to_all(parcel, 'tm', 0, 0)  20.6 us
    pallas_call x9, Pallas kernels, call(): pl.pallas_call(kernel, out_shape=outs, in_specs=[scalar] * smem + [vmem]...  18.2 us
    ppermute x6, starting transfers between devices, across(): lax.ppermute(pieces[k - 1], 'state', [(i, (i + 2 * k) % axis) for i in ra...  7.09 us
    ppermute x4, starting transfers between devices, local(): partner = lax.ppermute(same[shift], 'state', swap)  5.39 us
    ppermute x1, starting transfers between devices, local(): came = lax.ppermute(send, 'state', swap)  3.29 us
    ppermute x1, waiting for transfers between devices, local(): came = lax.ppermute(send, 'state', swap)  1.69 us
  transfers between devices with their start and end apart: 11, of which 6 were waited for; matrix products, arithmetic and copies ran while one was open for 0% of the time, Pallas kernels for 6%

profile of v1, /device:TPU:1, one launch (start us, length us, event | category | flops | bytes accessed | tf_op | source)
XLA Modules:
  0.0 80.3 jit_solution(13122961934143060336)
XLA Ops:
  0.6 0.1 pad_add_fusion.place
  0.7 0.0 copy-start
  0.7 0.0 copy-start.1
  0.7 7.4 %shard_map.122 = (bf16[1024,1024]{1,0:T(8,128)(2,1)S(1)}, bf16[1024,1024]{1,0:T(8,128)(2,1)S(1)}, f32[4,2,512,128]{3,2,1,0:T(8,128)S(1)}, bf16[4,2,512,128]{3,2,1,0:T(8,128)(2,1)S(1)}, f32[512,8]{1,0:T(8,128)S(1)}) custom-call(s32[3]{0:T(128)S(1)} %pad_add_fusion.place, s32[4,8]{1,0:T(4,128)} %bitcast.20, bf16[8,4,128,128]{3,2,1,0:T(8,128)(2,1)} %load_far.1, ...), custom_call_target="tpu_custom_call" | custom-call | flops 2147483648 | bytes 12484748 | tf_op jit(solution)/shard_map/pallas_call | solution.py:23
  8.2 3.3 %collective-permute-start = (bf16[4,2,512,128]{3,2,1,0:T(8,128)(2,1)S(1)}, bf16[4,2,512,128]{3,2,1,0:T(8,128)(2,1)S(1)}, u32[]{:S(2)}, u32[]{:S(2)}) collective-permute-start(bf16[4,2,512,128]{3,2,1,0:T(8,128)(2,1)S(1)} %get-tuple-element.62), channel_id=1, source_target_pairs={{0,1},{1,0},{2,3},{3,2},{4,5},{5,4},{6,7},{7,6},{8,9},{9,8},{10,11... | collective-permute-start | bytes 3145736 | tf_op jit(solution)/shard_map/ppermute | solution.py:298
  11.5 0.0 copy-done
  11.5 0.0 copy-done.1
  11.5 0.6 shard_map.123
  12.1 1.7 %collective-permute-done.came = bf16[4,2,512,128]{3,2,1,0:T(8,128)(2,1)S(1)} collective-permute-done((bf16[4,2,512,128]{3,2,1,0:T(8,128)(2,1)S(1)}, bf16[4,2,512,128]{3,2,1,0:T(8,128)(2,1)S(1)}, u32[]{:S(2)}, u32[]{:S(2)}) %collective-permute-start) | collective-permute-done | bytes 1048608 | tf_op jit(solution)/shard_map/ppermute | solution.py:298
  13.8 0.7 shard_map.124
  14.5 0.1 collective-permute-start.1
  14.6 1.9 %collective-permute-start.2 = (bf16[2,512,128]{2,1,0:T(8,128)(2,1)S(1)}, bf16[2,512,128]{2,1,0:T(8,128)(2,1)S(1)}, u32[]{:S(2)}, u32[]{:S(2)}) collective-permute-start(bf16[2,512,128]{2,1,0:T(8,128)(2,1)S(1)} %get-tuple-element.65), channel_id=1, source_target_pairs={{0,4},{1,5},{2,6},{3,7},{4,0},{5,1},{6,2},{7,3},{8,12},{9,13},{10,... | collective-permute-start | bytes 786440 | tf_op jit(solution)/shard_map/ppermute | solution.py:274
  16.5 1.2 %collective-permute-start.3 = (bf16[2,512,128]{2,1,0:T(8,128)(2,1)S(1)}, bf16[2,512,128]{2,1,0:T(8,128)(2,1)S(1)}, u32[]{:S(2)}, u32[]{:S(2)}) collective-permute-start(bf16[2,512,128]{2,1,0:T(8,128)(2,1)S(1)} %get-tuple-element.66), channel_id=1, source_target_pairs={{0,6},{1,7},{2,0},{3,1},{4,2},{5,3},{6,4},{7,5},{8,14},{9,15},{10,... | collective-permute-start | bytes 786440 | tf_op jit(solution)/shard_map/ppermute | solution.py:274
  17.7 6.3 %collective-permute-done.1.one = bf16[2,512,128]{2,1,0:T(8,128)(2,1)S(1)} collective-permute-done((bf16[2,512,128]{2,1,0:T(8,128)(2,1)S(1)}, bf16[2,512,128]{2,1,0:T(8,128)(2,1)S(1)}, u32[]{:S(2)}, u32[]{:S(2)}) %collective-permute-start.1) | collective-permute-done | bytes 262176 | tf_op jit(solution)/shard_map/ppermute | solution.py:274
  24.0 4.2 %collective-permute-done.2.two = bf16[2,512,128]{2,1,0:T(8,128)(2,1)S(1)} collective-permute-done((bf16[2,512,128]{2,1,0:T(8,128)(2,1)S(1)}, bf16[2,512,128]{2,1,0:T(8,128)(2,1)S(1)}, u32[]{:S(2)}, u32[]{:S(2)}) %collective-permute-start.2) | collective-permute-done | bytes 262176 | tf_op jit(solution)/shard_map/ppermute | solution.py:274
  28.2 1.0 %collective-permute-done.3.three = bf16[2,512,128]{2,1,0:T(8,128)(2,1)S(1)} collective-permute-done((bf16[2,512,128]{2,1,0:T(8,128)(2,1)S(1)}, bf16[2,512,128]{2,1,0:T(8,128)(2,1)S(1)}, u32[]{:S(2)}, u32[]{:S(2)}) %collective-permute-start.3) | collective-permute-done | bytes 262176 | tf_op jit(solution)/shard_map/ppermute | solution.py:274
  29.2 1.7 %shard_map.125 = (f32[512,128]{1,0:T(8,128)S(1)}, f32[512,128]{1,0:T(8,128)S(1)}, f32[4,4,2,8,128]{4,3,2,1,0:T(8,128)S(1)}, f32[32,16,128]{2,1,0:T(8,128)S(1)}) custom-call(s32[3]{0:T(128)S(1)} %pad_add_fusion.place, f32[2,512,128]{2,1,0:T(8,128)S(1)} %get-tuple-element.63.own, bf16[2,512,128]{2,1,0:T(8,128)(2,1)S(1)} %collective-permute-done.1.one, ...), custom_call_target="tpu_custom_call" | custom-call | bytes 3047436 | tf_op jit(solution)/shard_map/pallas_call | solution.py:23
  30.9 20.6 %all_to_all.5.parcel = f32[32,16,128]{2,1,0:T(8,128)S(1)} all-to-all(f32[32,16,128]{2,1,0:T(8,128)S(1)} %get-tuple-element.72), channel_id=1, replica_groups=mesh['tm'=32,'state'=8] {'tm'}, dimensions={0} | all-to-all | bytes 524288 | tf_op jit(solution)/shard_map/all_to_all | solution.py:318
  51.5 1.3 %shard_map.126.mine = bf16[2,512,128]{2,1,0:T(8,128)(2,1)S(1)} custom-call(s32[3]{0:T(128)S(1)} %pad_add_fusion.place, f32[32,16,128]{2,1,0:T(8,128)S(1)} %all_to_all.5.parcel, f32[4,4,2,8,128]{4,3,2,1,0:T(8,128)S(1)} %get-tuple-element.73.before, f32[512,128]{1,0:T(8,128)S(1)} %get-tuple-element.74.states, f32[512,128]{1,0:T(8,128)S(1)} %get-tuple-element.75.grads, ...), custom_call_target="tpu_custom_call" | custom-call | bytes 2490380 | tf_op jit(solution)/shard_map/pallas_call | solution.py:23
  52.7 3.3 %collective-permute-start.4 = (bf16[2,512,128]{2,1,0:T(8,128)(2,1)S(1)}, bf16[2,512,128]{2,1,0:T(8,128)(2,1)S(1)}, u32[]{:S(2)}, u32[]{:S(2)}) collective-permute-start(bf16[2,512,128]{2,1,0:T(8,128)(2,1)S(1)} %shard_map.126.mine), channel_id=1, source_target_pairs={{0,1},{1,0},{2,3},{3,2},{4,5},{5,4},{6,7},{7,6},{8,9},{9,8},{10,11... | collective-permute-start | bytes 786440 | tf_op jit(solution)/shard_map/ppermute | solution.py:335
  56.0 1.1 %collective-permute-start.5 = (bf16[2,512,128]{2,1,0:T(8,128)(2,1)S(1)}, bf16[2,512,128]{2,1,0:T(8,128)(2,1)S(1)}, u32[]{:S(2)}, u32[]{:S(2)}) collective-permute-start(bf16[2,512,128]{2,1,0:T(8,128)(2,1)S(1)} %shard_map.126.mine), channel_id=1, source_target_pairs={{0,2},{1,3},{2,4},{3,5},{4,6},{5,7},{6,0},{7,1},{8,10},{9,11},{10,... | collective-permute-start | bytes 786440 | tf_op jit(solution)/shard_map/ppermute | solution.py:274
  57.1 1.6 %collective-permute-start.7 = (bf16[2,512,128]{2,1,0:T(8,128)(2,1)S(1)}, bf16[2,512,128]{2,1,0:T(8,128)(2,1)S(1)}, u32[]{:S(2)}, u32[]{:S(2)}) collective-permute-start(bf16[2,512,128]{2,1,0:T(8,128)(2,1)S(1)} %shard_map.126.mine), channel_id=1, source_target_pairs={{0,6},{1,7},{2,0},{3,1},{4,2},{5,3},{6,4},{7,5},{8,14},{9,15},{10,... | collective-permute-start | bytes 786440 | tf_op jit(solution)/shard_map/ppermute | solution.py:274
  58.7 0.0 collective-permute-done.4.partner
  58.7 1.3 %shard_map.127 = (f32[512,1024]{1,0:T(8,128)S(1)}, f32[512,1024]{1,0:T(8,128)S(1)}) custom-call(s32[3]{0:T(128)S(1)} %pad_add_fusion.place, bf16[2,512,128]{2,1,0:T(8,128)(2,1)S(1)} %shard_map.126.mine, bf16[2,512,128]{2,1,0:T(8,128)(2,1)S(1)} %collective-permute-done.4.partner, bf16[1024,1024]{1,0:T(8,128)(2,1)S(1)} %get-tuple-element.80.load_weights, ...), custom_call_target="tpu_custom_call" | custom-call | flops 536870912 | bytes 8929292 | tf_op jit(solution)/shard_map/pallas_call | solution.py:23
  60.0 5.0 %collective-permute-done.5.mine = bf16[2,512,128]{2,1,0:T(8,128)(2,1)S(1)} collective-permute-done((bf16[2,512,128]{2,1,0:T(8,128)(2,1)S(1)}, bf16[2,512,128]{2,1,0:T(8,128)(2,1)S(1)}, u32[]{:S(2)}, u32[]{:S(2)}) %collective-permute-start.5) | collective-permute-done | bytes 262176 | tf_op jit(solution)/shard_map/ppermute | solution.py:274
  65.0 0.9 %collective-permute-start.6 = (bf16[2,512,128]{2,1,0:T(8,128)(2,1)S(1)}, bf16[2,512,128]{2,1,0:T(8,128)(2,1)S(1)}, u32[]{:S(2)}, u32[]{:S(2)}) collective-permute-start(bf16[2,512,128]{2,1,0:T(8,128)(2,1)S(1)} %collective-permute-done.5.mine), channel_id=1, source_target_pairs={{0,1},{1,0},{2,3},{3,2},{4,5},{5,4},{6,7},{7,6},{8,9},{9,8},{10,11... | collective-permute-start | bytes 786440 | tf_op jit(solution)/shard_map/ppermute | solution.py:335
  66.0 1.2 %collective-permute-start.8 = (bf16[2,512,128]{2,1,0:T(8,128)(2,1)S(1)}, bf16[2,512,128]{2,1,0:T(8,128)(2,1)S(1)}, u32[]{:S(2)}, u32[]{:S(2)}) collective-permute-start(bf16[2,512,128]{2,1,0:T(8,128)(2,1)S(1)} %shard_map.126.mine), channel_id=1, source_target_pairs={{0,4},{1,5},{2,6},{3,7},{4,0},{5,1},{6,2},{7,3},{8,12},{9,13},{10,... | collective-permute-start | bytes 786440 | tf_op jit(solution)/shard_map/ppermute | solution.py:274
  67.2 0.0 collective-permute-done.7.mine
  67.2 0.3 collective-permute-start.10
  67.5 0.0 collective-permute-done.6.partner
  67.5 1.3 %shard_map.128 = (f32[512,1024]{1,0:T(8,128)S(1)}, f32[512,1024]{1,0:T(8,128)S(1)}) custom-call(s32[3]{0:T(128)S(1)} %pad_add_fusion.place, bf16[2,512,128]{2,1,0:T(8,128)(2,1)S(1)} %collective-permute-done.5.mine, bf16[2,512,128]{2,1,0:T(8,128)(2,1)S(1)} %collective-permute-done.6.partner, bf16[1024,1024]{1,0:T(8,128)(2,1)S(1)} %get-tuple-element.80.load_weights, ...), custom_call_target="tpu_custom_call" | custom-call | flops 536870912 | bytes 13123596 | tf_op jit(solution)/shard_map/pallas_call | solution.py:23
  68.8 6.5 %collective-permute-done.8.mine = bf16[2,512,128]{2,1,0:T(8,128)(2,1)S(1)} collective-permute-done((bf16[2,512,128]{2,1,0:T(8,128)(2,1)S(1)}, bf16[2,512,128]{2,1,0:T(8,128)(2,1)S(1)}, u32[]{:S(2)}, u32[]{:S(2)}) %collective-permute-start.8) | collective-permute-done | bytes 262176 | tf_op jit(solution)/shard_map/ppermute | solution.py:274
  75.3 0.9 %collective-permute-start.9 = (bf16[2,512,128]{2,1,0:T(8,128)(2,1)S(1)}, bf16[2,512,128]{2,1,0:T(8,128)(2,1)S(1)}, u32[]{:S(2)}, u32[]{:S(2)}) collective-permute-start(bf16[2,512,128]{2,1,0:T(8,128)(2,1)S(1)} %collective-permute-done.8.mine), channel_id=1, source_target_pairs={{0,1},{1,0},{2,3},{3,2},{4,5},{5,4},{6,7},{7,6},{8,9},{9,8},{10,11... | collective-permute-start | bytes 786440 | tf_op jit(solution)/shard_map/ppermute | solution.py:335
  76.2 0.0 collective-permute-done.10.partner
  76.2 1.3 %shard_map.129 = (f32[512,1024]{1,0:T(8,128)S(1)}, f32[512,1024]{1,0:T(8,128)S(1)}) custom-call(s32[3]{0:T(128)S(1)} %pad_add_fusion.place, bf16[2,512,128]{2,1,0:T(8,128)(2,1)S(1)} %collective-permute-done.7.mine, bf16[2,512,128]{2,1,0:T(8,128)(2,1)S(1)} %collective-permute-done.10.partner, bf16[1024,1024]{1,0:T(8,128)(2,1)S(1)} %get-tuple-element.80.load_weights, ...), custom_call_target="tpu_custom_call" | custom-call | flops 536870912 | bytes 13123596 | tf_op jit(solution)/shard_map/pallas_call | solution.py:23
  77.6 0.0 collective-permute-done.9.partner
  77.6 2.6 %shard_map.130 = (bf16[512,1024]{1,0:T(8,128)(2,1)}, bf16[512,1024]{1,0:T(8,128)(2,1)}) custom-call(s32[3]{0:T(128)S(1)} %pad_add_fusion.place, bf16[2,512,128]{2,1,0:T(8,128)(2,1)S(1)} %collective-permute-done.8.mine, bf16[2,512,128]{2,1,0:T(8,128)(2,1)S(1)} %collective-permute-done.9.partner, bf16[1024,1024]{1,0:T(8,128)(2,1)S(1)} %get-tuple-element.80.load_weights, ...), custom_call_target="tpu_custom_call" | custom-call | flops 536870912 | bytes 11026444 | tf_op jit(solution)/shard_map/pallas_call | solution.py:23
Async XLA Ops:
  0.7 10.7 %copy-start = (f32[128,4,128]{2,1,0:T(4,128)S(1)}, f32[128,4,128]{2,1,0:T(4,128)}, u32[]{:S(2)}) copy-start(f32[128,4,128]{2,1,0:T(4,128)} %param.19) | copy-start | bytes 786436
  0.7 10.7 %copy-start.1 = (f32[128,4,128]{2,1,0:T(4,128)S(1)}, f32[128,4,128]{2,1,0:T(4,128)}, u32[]{:S(2)}) copy-start(f32[128,4,128]{2,1,0:T(4,128)} %param.20) | copy-start | bytes 786436
  8.2 5.6 %collective-permute-start = (bf16[4,2,512,128]{3,2,1,0:T(8,128)(2,1)S(1)}, bf16[4,2,512,128]{3,2,1,0:T(8,128)(2,1)S(1)}, u32[]{:S(2)}, u32[]{:S(2)}) collective-permute-start(bf16[4,2,512,128]{3,2,1,0:T(8,128)(2,1)S(1)} %get-tuple-element.62), channel_id=1, source_target_pairs={{0,1},{1,0},{2,3},{3,2},{4,5},{5,4},{6,7},{7,6},{8,9},{9,8},{10,11... | collective-permute-start | bytes 3145736 | tf_op jit(solution)/shard_map/ppermute | solution.py:298
  14.5 9.5 %collective-permute-start.1 = (bf16[2,512,128]{2,1,0:T(8,128)(2,1)S(1)}, bf16[2,512,128]{2,1,0:T(8,128)(2,1)S(1)}, u32[]{:S(2)}, u32[]{:S(2)}) collective-permute-start(bf16[2,512,128]{2,1,0:T(8,128)(2,1)S(1)} %get-tuple-element.64), channel_id=1, source_target_pairs={{0,2},{1,3},{2,4},{3,5},{4,6},{5,7},{6,0},{7,1},{8,10},{9,11},{10,... | collective-permute-start | bytes 786440 | tf_op jit(solution)/shard_map/ppermute | solution.py:274
  14.6 13.6 %collective-permute-start.2 = (bf16[2,512,128]{2,1,0:T(8,128)(2,1)S(1)}, bf16[2,512,128]{2,1,0:T(8,128)(2,1)S(1)}, u32[]{:S(2)}, u32[]{:S(2)}) collective-permute-start(bf16[2,512,128]{2,1,0:T(8,128)(2,1)S(1)} %get-tuple-element.65), channel_id=1, source_target_pairs={{0,4},{1,5},{2,6},{3,7},{4,0},{5,1},{6,2},{7,3},{8,12},{9,13},{10,... | collective-permute-start | bytes 786440 | tf_op jit(solution)/shard_map/ppermute | solution.py:274
  16.5 12.7 %collective-permute-start.3 = (bf16[2,512,128]{2,1,0:T(8,128)(2,1)S(1)}, bf16[2,512,128]{2,1,0:T(8,128)(2,1)S(1)}, u32[]{:S(2)}, u32[]{:S(2)}) collective-permute-start(bf16[2,512,128]{2,1,0:T(8,128)(2,1)S(1)} %get-tuple-element.66), channel_id=1, source_target_pairs={{0,6},{1,7},{2,0},{3,1},{4,2},{5,3},{6,4},{7,5},{8,14},{9,15},{10,... | collective-permute-start | bytes 786440 | tf_op jit(solution)/shard_map/ppermute | solution.py:274
  52.7 6.0 %collective-permute-start.4 = (bf16[2,512,128]{2,1,0:T(8,128)(2,1)S(1)}, bf16[2,512,128]{2,1,0:T(8,128)(2,1)S(1)}, u32[]{:S(2)}, u32[]{:S(2)}) collective-permute-start(bf16[2,512,128]{2,1,0:T(8,128)(2,1)S(1)} %shard_map.126.mine), channel_id=1, source_target_pairs={{0,1},{1,0},{2,3},{3,2},{4,5},{5,4},{6,7},{7,6},{8,9},{9,8},{10,11... | collective-permute-start | bytes 786440 | tf_op jit(solution)/shard_map/ppermute | solution.py:335
  56.0 9.0 %collective-permute-start.5 = (bf16[2,512,128]{2,1,0:T(8,128)(2,1)S(1)}, bf16[2,512,128]{2,1,0:T(8,128)(2,1)S(1)}, u32[]{:S(2)}, u32[]{:S(2)}) collective-permute-start(bf16[2,512,128]{2,1,0:T(8,128)(2,1)S(1)} %shard_map.126.mine), channel_id=1, source_target_pairs={{0,2},{1,3},{2,4},{3,5},{4,6},{5,7},{6,0},{7,1},{8,10},{9,11},{10,... | collective-permute-start | bytes 786440 | tf_op jit(solution)/shard_map/ppermute | solution.py:274
  57.1 10.1 %collective-permute-start.7 = (bf16[2,512,128]{2,1,0:T(8,128)(2,1)S(1)}, bf16[2,512,128]{2,1,0:T(8,128)(2,1)S(1)}, u32[]{:S(2)}, u32[]{:S(2)}) collective-permute-start(bf16[2,512,128]{2,1,0:T(8,128)(2,1)S(1)} %shard_map.126.mine), channel_id=1, source_target_pairs={{0,6},{1,7},{2,0},{3,1},{4,2},{5,3},{6,4},{7,5},{8,14},{9,15},{10,... | collective-permute-start | bytes 786440 | tf_op jit(solution)/shard_map/ppermute | solution.py:274
  65.0 2.5 %collective-permute-start.6 = (bf16[2,512,128]{2,1,0:T(8,128)(2,1)S(1)}, bf16[2,512,128]{2,1,0:T(8,128)(2,1)S(1)}, u32[]{:S(2)}, u32[]{:S(2)}) collective-permute-start(bf16[2,512,128]{2,1,0:T(8,128)(2,1)S(1)} %collective-permute-done.5.mine), channel_id=1, source_target_pairs={{0,1},{1,0},{2,3},{3,2},{4,5},{5,4},{6,7},{7,6},{8,9},{9,8},{10,11... | collective-permute-start | bytes 786440 | tf_op jit(solution)/shard_map/ppermute | solution.py:335
  66.0 9.4 %collective-permute-start.8 = (bf16[2,512,128]{2,1,0:T(8,128)(2,1)S(1)}, bf16[2,512,128]{2,1,0:T(8,128)(2,1)S(1)}, u32[]{:S(2)}, u32[]{:S(2)}) collective-permute-start(bf16[2,512,128]{2,1,0:T(8,128)(2,1)S(1)} %shard_map.126.mine), channel_id=1, source_target_pairs={{0,4},{1,5},{2,6},{3,7},{4,0},{5,1},{6,2},{7,3},{8,12},{9,13},{10,... | collective-permute-start | bytes 786440 | tf_op jit(solution)/shard_map/ppermute | solution.py:274
  67.2 9.0 %collective-permute-start.10 = (bf16[2,512,128]{2,1,0:T(8,128)(2,1)S(1)}, bf16[2,512,128]{2,1,0:T(8,128)(2,1)S(1)}, u32[]{:S(2)}, u32[]{:S(2)}) collective-permute-start(bf16[2,512,128]{2,1,0:T(8,128)(2,1)S(1)} %collective-permute-done.7.mine), channel_id=1, source_target_pairs={{0,1},{1,0},{2,3},{3,2},{4,5},{5,4},{6,7},{7,6},{8,9},{9,8},{10,11... | collective-permute-start | bytes 786440 | tf_op jit(solution)/shard_map/ppermute | solution.py:335
  75.3 2.2 %collective-permute-start.9 = (bf16[2,512,128]{2,1,0:T(8,128)(2,1)S(1)}, bf16[2,512,128]{2,1,0:T(8,128)(2,1)S(1)}, u32[]{:S(2)}, u32[]{:S(2)}) collective-permute-start(bf16[2,512,128]{2,1,0:T(8,128)(2,1)S(1)} %collective-permute-done.8.mine), channel_id=1, source_target_pairs={{0,1},{1,0},{2,3},{3,2},{4,5},{5,4},{6,7},{7,6},{8,9},{9,8},{10,11... | collective-permute-start | bytes 786440 | tf_op jit(solution)/shard_map/ppermute | solution.py:335

commit v2 on v1

--- a/solution.py
+++ b/solution.py
@@ -39,70 +39,68 @@
     return jax.ShapeDtypeStruct(shape, dtype)
 
 
-def front_kernel(
-    place, pattern, load_far, cot_far, gain_far, available_far, readings_far, rows_far, enc_in_far, enc_out_far,
-    load_weights, gain_weights, keep, send, mask,
-    load, cotangent, gain, available, lhs, rows_in, enc_in, enc_out, sems,
+def split(place, keep, send, at, total):
+    mine = place[1] == 0
+    low, high = total[:, :BLK], total[:, BLK:]
+    keep[at] = jnp.where(mine, low, high)
+    send[at] = jnp.where(mine, high, low).astype(BF16)
+
+
+def window_of(at):
+    return slice(at * 2 * BLK, (at + 1) * 2 * BLK)
+
+
+def pull_kernel(
+    place, pattern, load_far, cot_far, rows_far, enc_in_far, enc_out_far, gain_far, available_far, readings_far,
+    weights, keep, send, rows_in, enc_in, enc_out, gain, available, readings,
+    load, cotangent, sems,
 ):
-    core = place[1]
     pairs = (
-        (load_far, load), (cot_far, cotangent), (gain_far, gain), (available_far, available),
-        (readings_far, lhs), (rows_far, rows_in), (enc_in_far, enc_in), (enc_out_far, enc_out),
+        (load_far, load), (cot_far, cotangent), (rows_far, rows_in), (enc_in_far, enc_in), (enc_out_far, enc_out),
+        (gain_far, gain), (available_far, available), (readings_far, readings),
     )
     copies = [pltpu.make_async_copy(far, near, sems.at[i]) for i, (far, near) in enumerate(pairs)]
     for copy in copies:
         copy.start()
-    load_weights[...] = jnp.zeros_like(load_weights)
-    gain_weights[...] = jnp.zeros_like(gain_weights)
+    weights[...] = jnp.zeros_like(weights)
+    copies[0].wait()
+    for q in range(load.shape[0]):
+        for k in range(load.shape[1]):
+            row = pl.multiple_of(pattern[k, q] * BLK, BLK)
+            weights[pl.ds(row, BLK), q * BLK : (q + 1) * BLK] = load[q, k]
+    copies[1].wait()
+    for at in range(keep.shape[0]):
+        total = lax.dot_general(cotangent[...], weights[window_of(at), :], NT, preferred_element_type=F32)
+        split(place, keep, send, at, total)
+    for copy in copies[2:]:
+        copy.wait()
+
+
+def drive_kernel(
+    place, pattern, rows_in, enc_in, enc_out, gain, available, readings,
+    weights, keep, send, mask,
+    lhs,
+):
     traces, blocks, steps = available.shape
-    reads = pattern.shape[0]
-
-    def split(which, at, total):
-        low, high = total[:, :BLK], total[:, BLK:]
-        keep[at, which] = jnp.where(core == 0, low, high)
-        send[at, which] = jnp.where(core == 0, high, low).astype(BF16)
-
-    copies[0].wait()
-    for q in range(blocks):
-        for k in range(reads):
-            row = pl.multiple_of(pattern[k, q] * BLK, BLK)
-            load_weights[pl.ds(row, BLK), q * BLK : (q + 1) * BLK] = load[q, k]
-    copies[1].wait()
-
-    def pull_columns(at, _):
-        window = pl.ds(pl.multiple_of(at * 2 * BLK, 2 * BLK), 2 * BLK)
-        split(1, at, lax.dot_general(cotangent[...], load_weights[window, :], NT, preferred_element_type=F32))
-        return 0
-
-    lax.fori_loop(0, 4, pull_columns, 0)
-    copies[2].wait()
-    for q in range(blocks):
-        for k in range(reads):
-            column = pl.multiple_of(pattern[k, q] * BLK, BLK)
-            gain_weights[q * BLK : (q + 1) * BLK, pl.ds(column, BLK)] = gain[q, k]
-    for copy in copies[3:]:
-        copy.wait()
+    hidden = jax.nn.gelu(jnp.dot(rows_in[...], enc_in[...], preferred_element_type=F32)).astype(BF16)
+    weights[...] = jnp.zeros_like(weights)
     for b in range(traces):
         mask[b * steps : (b + 1) * steps, :] = available[b].astype(F32).T
     for q in range(blocks):
-        lhs[:, q * BLK : (q + 1) * BLK] = lhs[:, q * BLK : (q + 1) * BLK] * mask[:, q : q + 1].astype(BF16)
-    hidden = jax.nn.gelu(jnp.dot(rows_in[...], enc_in[...], preferred_element_type=F32)).astype(BF16)
-
-    def drive_columns(at, _):
-        window = pl.ds(pl.multiple_of(at * 2 * BLK, 2 * BLK), 2 * BLK)
-        total = jnp.dot(lhs[...], gain_weights[:, window], preferred_element_type=F32)
-        total += jnp.dot(hidden, enc_out[:, window], preferred_element_type=F32)
-        split(0, at, total)
-        return 0
-
-    lax.fori_loop(0, 4, drive_columns, 0)
-
-
-def merge_kernel(place, keep, came, own, *pieces):
-    own[...] = keep[place[0]] + came[place[0]].astype(F32)
-    for k, piece in enumerate(pieces):
-        at = lax.rem(place[0] + k + 1, keep.shape[0])
-        piece[...] = (keep[at] + came[at].astype(F32)).astype(BF16)
+        for k in range(gain.shape[1]):
+            column = pl.multiple_of(pattern[k, q] * BLK, BLK)
+            weights[q * BLK : (q + 1) * BLK, pl.ds(column, BLK)] = gain[q, k]
+        lhs[:, q * BLK : (q + 1) * BLK] = readings[:, q * BLK : (q + 1) * BLK] * mask[:, q : q + 1].astype(BF16)
+    for at in range(keep.shape[0]):
+        total = jnp.dot(lhs[...], weights[:, window_of(at)], preferred_element_type=F32)
+        total += jnp.dot(hidden, enc_out[:, window_of(at)], preferred_element_type=F32)
+        split(place, keep, send, at, total)
+
+
+def merge_kernel(shift, place, keep_a, keep_b, came_a, came_b, piece):
+    at = lax.rem(place[0] + shift, keep_a.shape[0])
+    for which, (keep, came) in enumerate(((keep_a, came_a), (keep_b, came_b))):
+        piece[which] = (keep[at] + came[at].astype(F32)).astype(piece.dtype)
 
 
 def rows_of(b, u, steps):
@@ -199,7 +197,7 @@
 def settle_kernel(
     traces, steps, place,
     parcel, before, states, grads, root, ahead_p, filt_p, rise_p, fall_p,
-    smoothed,
+    smoothed, states_bf, grads_bf,
     sums, carry,
 ):
     me, length = place[2], parcel.shape[0]
@@ -221,40 +219,45 @@
             sums[0, at, :] = states[at, :] + filt_p[at, :] * filt + ahead_p[at, :] * ahead
             sums[1, at, :] = root[at, :] * (grads[at, :] + rise_p[at, :] * rise + fall_p[at, :] * fall)
     smoothed[...] = sums[...].astype(BF16)
-
-
-def project_kernel(shift, last, place, mine, partner, load_weights, gain_weights, mask, *refs):
-    before, refs = ((), refs) if shift == 0 else (refs[:2], refs[2:])
-    outs, lhs, *rest = refs[:2], *refs[2:]
+    states_bf[0] = sums[0].astype(BF16)
+    grads_bf[0] = sums[1].astype(BF16)
+
+
+def project_kernel(shift, chains, last, place, load_weights, gain_weights, mask, *refs):
+    count = len(chains)
+    mine, partner = refs[:2]
+    refs = refs[2:]
+    before = ()
+    if shift:
+        before, refs = refs[:count], refs[count:]
+    outs, lhs, rest = refs[:count], refs[count], refs[count + 1 :]
     core = place[1]
     block = pl.multiple_of(2 * BLK * lax.rem(place[0] - shift + 4, 4), 2 * BLK)
     states = pl.ds(block, 2 * BLK)
     copies = []
-    for which in range(2):
+    for i, chain_id in enumerate(chains):
         for side, piece in enumerate((mine, partner)):
             column = pl.multiple_of(BLK * (core if side == 0 else 1 - core), BLK)
-            lhs[which, :, pl.ds(column, BLK)] = piece[which]
+            lhs[i, :, pl.ds(column, BLK)] = piece[i]
         for at in range(4):
-            window = slice(at * 2 * BLK, (at + 1) * 2 * BLK)
-            if which == 0:
-                total = lax.dot_general(lhs[0], load_weights[states, window], NN, preferred_element_type=F32)
+            window = window_of(at)
+            if chain_id == 0:
+                total = lax.dot_general(lhs[i], load_weights[states, window], NN, preferred_element_type=F32)
             else:
-                total = lax.dot_general(lhs[1], gain_weights[window, states], NT, preferred_element_type=F32)
+                total = lax.dot_general(lhs[i], gain_weights[window, states], NT, preferred_element_type=F32)
             if before:
-                total = before[which][:, window] + total
+                total = before[i][:, window] + total
             if not last:
-                outs[which][:, window] = total
+                outs[i][:, window] = total
                 continue
             stage, sems = rest
             for half in range(2):
                 q = 2 * at + half
-                piece = total[:, half * BLK : (half + 1) * BLK]
-                if which == 1:
-                    piece = piece * mask[:, q : q + 1]
-                stage[which, :, q * BLK : (q + 1) * BLK] = piece.astype(BF16)
-            copies.append(
-                pltpu.make_async_copy(stage.at[which, :, window], outs[which].at[:, window], sems.at[which, at])
-            )
+                part = total[:, half * BLK : (half + 1) * BLK]
+                if chain_id == 1:
+                    part = part * mask[:, q : q + 1]
+                stage[i, :, q * BLK : (q + 1) * BLK] = part.astype(BF16)
+            copies.append(pltpu.make_async_copy(stage.at[i, :, window], outs[i].at[:, window], sems.at[i, at]))
             copies[-1].start()
     for copy in copies:
         copy.wait()
@@ -270,32 +273,39 @@
     place = jnp.stack([at // 2, at % 2, lax.axis_index("tm")]).astype(jnp.int32)
     swap = [(i, i ^ 1) for i in range(axis)]
 
-    def across(pieces):
-        moved = {k: lax.ppermute(pieces[k - 1], "state", [(i, (i + 2 * k) % axis) for i in range(axis)]) for k in (1, 3, 2)}
-        return [moved[k] for k in (1, 2, 3)]
-
     work = 2 * rows * sensors * states
-
-    far = (
-        load, cotangent.reshape(rows, sensors), gain, available.transpose(0, 2, 1),
-        readings.reshape(rows, sensors), inputs.reshape(rows, features), encoder_in, encoder_out,
-    )
-    load_weights, gain_weights, keep, send, mask = call(
-        front_kernel,
-        (
-            struct((states, sensors), BF16),
-            struct((sensors, states), BF16),
-            struct((axis // 2, 2, rows, BLK), F32),
-            struct((axis // 2, 2, rows, BLK), BF16),
-            struct((rows, blocks), F32),
-        ),
-        (place, in_hbm(pattern.T), *far),
-        scratch=[pltpu.VMEM(a.shape, a.dtype) for a in far] + [pltpu.SemaphoreType.DMA((len(far),))],
+    both = struct((2, rows, BLK), BF16)
+
+    def across(piece, shift):
+        return lax.ppermute(piece, "state", [(i, (i + 2 * shift) % axis) for i in range(axis)])
+
+    near = (
+        inputs.reshape(rows, features), encoder_in, encoder_out, gain, available.transpose(0, 2, 1),
+        readings.reshape(rows, sensors),
+    )
+    pulled_from = (load, cotangent.reshape(rows, sensors))
+    table = in_hbm(pattern.T)
+    chips = axis // 2
+    parts = (struct((chips, rows, BLK), F32), struct((chips, rows, BLK), BF16))
+    load_weights, keep_b, send_b, *near = call(
+        pull_kernel,
+        (struct((states, sensors), BF16), *parts, *(struct(a.shape, a.dtype) for a in near)),
+        (place, table, *pulled_from, *near),
+        scratch=[pltpu.VMEM(a.shape, a.dtype) for a in pulled_from] + [pltpu.SemaphoreType.DMA((8,))],
         smem=2,
-        hbm=len(far),
-        flops=2 * work,
-    )
-    came = lax.ppermute(send, "state", swap)
+        hbm=8,
+        flops=work,
+    )
+    came_b = lax.ppermute(send_b, "state", swap)
+    gain_weights, keep_a, send_a, mask = call(
+        drive_kernel,
+        (struct((sensors, states), BF16), *parts, struct((rows, blocks), F32)),
+        (place, table, *near),
+        scratch=[pltpu.VMEM((rows, sensors), BF16)],
+        smem=2,
+        flops=work,
+    )
+    came_a = lax.ppermute(send_a, "state", swap)
     full, segments = struct((rows, BLK), F32), struct((traces, SEG, BLK), F32)
     keep_r, keep_s, root, ahead_p, filt_p, rise_p, fall_p, seg_r, seg_s = call(
         functools.partial(decay_kernel, traces, steps),
@@ -303,47 +313,62 @@
         (retain.reshape(-1, steps), smooth.reshape(-1, steps)),
     )
     decays = (keep_r, keep_s, root, ahead_p, filt_p, rise_p, fall_p, seg_r, seg_s)
-    keep, decays = lax.optimization_barrier((keep, decays))
+    keep_a, decays = lax.optimization_barrier((keep_a, decays))
     keep_r, keep_s, root, ahead_p, filt_p, rise_p, fall_p, seg_r, seg_s = decays
     both = struct((2, rows, BLK), BF16)
-    own, *sums = call(merge_kernel, (struct(both.shape, F32),) + (both,) * 3, (place, keep, came), smem=1)
-    sums = across(sums)
+    sums = {}
+    for shift in (1, 3, 2, 0):
+        (piece,) = call(
+            functools.partial(merge_kernel, shift),
+            (both if shift else struct(both.shape, F32),),
+            (place, keep_a, keep_b, came_a, came_b),
+            smem=1,
+        )
+        sums[shift] = across(piece, shift) if shift else piece
+    own, one, two, three = (sums[k] for k in range(4))
     scanned, pulled, before, parcel = call(
         functools.partial(scan_kernel, traces, steps),
         (full, full, struct((4, traces, 2, SEG, BLK), F32), struct((times, 2 * SEG, BLK), F32)),
-        (place, own, *sums, keep_r, keep_s, root, seg_r, seg_s),
+        (place, own, one, two, three, keep_r, keep_s, root, seg_r, seg_s),
         scratch=[pltpu.VMEM((rows, BLK), F32)] * 2 + [pltpu.VMEM((2, 2, SEG, BLK), F32)],
         smem=1,
     )
     parcel = lax.all_to_all(parcel, "tm", 0, 0)
-    (smoothed,) = call(
+    half = struct((1, rows, BLK), BF16)
+    smoothed, states_bf, grads_bf = call(
         functools.partial(settle_kernel, traces, steps),
-        (both,),
+        (both, half, half),
         (place, parcel, before, scanned, pulled, root, ahead_p, filt_p, rise_p, fall_p),
         scratch=[pltpu.VMEM((2, rows, BLK), F32), pltpu.VMEM((2, SEG, BLK), F32)],
         smem=1,
     )
-    same = [smoothed, *across([smoothed] * 3)]
-    totals = ()
-    for shift in (0, 1, 3, 2):
+    one, three = across(smoothed, 1), across(smoothed, 3)
+    far_states = across(states_bf, 2)
+    far_grads = across(grads_bf, 2)
+
+    def project(shift, chains, mine, totals):
         last = shift == 2
-        if shift == 1:
-            totals, same[1] = lax.optimization_barrier((totals, same[1]))
-            totals, same[3] = lax.optimization_barrier((totals, same[3]))
-        if shift == 3:
-            totals, same[2] = lax.optimization_barrier((totals, same[2]))
-        partner = lax.ppermute(same[shift], "state", swap)
-        totals = call(
-            functools.partial(project_kernel, shift, last),
-            (struct((rows, sensors), BF16 if last else F32),) * 2,
-            (place, same[shift], partner, load_weights, gain_weights, mask, *totals),
-            scratch=[pltpu.VMEM((2, rows, 2 * BLK), BF16)]
-            + ([pltpu.VMEM((2, rows, sensors), BF16), pltpu.SemaphoreType.DMA((2, 4))] if last else []),
+        partner = lax.ppermute(mine, "state", swap)
+        return call(
+            functools.partial(project_kernel, shift, chains, last),
+            (struct((rows, sensors), BF16 if last else F32),) * len(chains),
+            (place, load_weights, gain_weights, mask, mine, partner, *totals),
+            scratch=[pltpu.VMEM((len(chains), rows, 2 * BLK), BF16)]
+            + ([pltpu.VMEM((1, rows, sensors), BF16), pltpu.SemaphoreType.DMA((1, 4))] if last else []),
             smem=1,
             hbm_out=last,
-            flops=work // 2,
+            flops=work * len(chains) // 4,
         )
-    predicted, sensor_grad = totals
+
+    totals = project(0, (0, 1), smoothed, ())
+    totals, one = lax.optimization_barrier((totals, one))
+    totals, three = lax.optimization_barrier((totals, three))
+    totals = project(1, (0, 1), one, totals)
+    totals, far_states = lax.optimization_barrier((totals, far_states))
+    totals = project(3, (0, 1), three, totals)
+    (predicted,) = project(2, (0,), far_states, totals[:1])
+    predicted, far_grads = lax.optimization_barrier((predicted, far_grads))
+    (sensor_grad,) = project(2, (1,), far_grads, totals[1:])
     return predicted.reshape(readings.shape), sensor_grad.reshape(readings.shape)
 
 

time: 80.4 us -> 86.5 us (1.076)
  Pallas kernels: 18.2 us -> 20.5 us
  blocking collectives: 20.6 us -> 22.6 us
  waiting for transfers between devices: 24.8 us -> 26.2 us
    pallas_call x9 -> x14, Pallas kernels: 18.2 us -> 20.5 us  [call(): pl.pallas_call(kernel, out_shape=outs, in_specs=[scalar] * smem + [vmem]...]
    all_to_all x1, blocking collectives: 20.6 us -> 22.6 us  [local(): parcel = lax.all_to_all(parcel, 'tm', 0, 0)]
    ppermute x11 -> x14, waiting for transfers between devices: 24.8 us -> 26.2 us  [the longest x7 23.6 us: across(): lax.ppermute(piece, 'state', [(i, (i + 2 * shift) % axis) for i in range(...]
    ppermute x11 -> x14, starting transfers between devices: 15.8 us -> 16 us  [the longest x7 7.17 us: across(): lax.ppermute(piece, 'state', [(i, (i + 2 * shift) % axis) for i in range(...]
  transfers between devices with their start and end apart: 11 -> 14, of which waited for: 6 -> 9; matrix products, arithmetic and copies ran while one was open for 0% -> 0% of each run, Pallas kernels for 6% -> 10%
where the time goes in v2:
time: 86.5 us; the launch traced here: 86.4 us
  waiting for transfers between devices  26.2 us (30%)
  blocking collectives  22.6 us (26%)
  Pallas kernels  20.5 us (24%)
  starting transfers between devices  16 us (18%)
  between operations  0.94 us (1%)
    ppermute x7, waiting for transfers between devices, across(): lax.ppermute(piece, 'state', [(i, (i + 2 * shift) % axis) for i in range(...  23.6 us
    all_to_all x1, blocking collectives, local(): parcel = lax.all_to_all(parcel, 'tm', 0, 0)  22.6 us
    pallas_call x14, Pallas kernels, call(): pl.pallas_call(kernel, out_shape=outs, in_specs=[scalar] * smem + [vmem]...  20.5 us
    ppermute x7, starting transfers between devices, across(): lax.ppermute(piece, 'state', [(i, (i + 2 * shift) % axis) for i in range(...  7.17 us
    ppermute x5, starting transfers between devices, project(): partner = lax.ppermute(mine, 'state', swap)  5.5 us
    ppermute x1, starting transfers between devices, local(): came_a = lax.ppermute(send_a, 'state', swap)  3.27 us
  transfers between devices with their start and end apart: 14, of which 9 were waited for; matrix products, arithmetic and copies ran while one was open for 0% of the time, Pallas kernels for 10%

profile of v2, /device:TPU:1, one launch (start us, length us, event | category | flops | bytes accessed | tf_op | source)
XLA Modules:
  0.0 86.4 jit_solution(1182379720496090441)
XLA Ops:
  0.6 0.1 pad_add_fusion.place
  0.7 3.6 %shard_map.122 = (bf16[1024,1024]{1,0:T(8,128)(2,1)S(1)}, f32[4,512,128]{2,1,0:T(8,128)S(1)}, bf16[4,512,128]{2,1,0:T(8,128)(2,1)S(1)}, bf16[512,256]{1,0:T(8,12...) custom-call(s32[3]{0:T(128)S(1)} %pad_add_fusion.place, ...), custom_call_target="tpu_custom_call" | custom-call | flops 1073741824 | bytes 11829388 | tf_op jit(solution)/shard_map/pallas_call | solution.py:23
  4.4 0.0 copy-start
  4.4 0.0 copy-start.1
  4.4 3.1 %shard_map.123 = (bf16[1024,1024]{1,0:T(8,128)(2,1)S(1)}, f32[4,512,128]{2,1,0:T(8,128)S(1)}, bf16[4,512,128]{2,1,0:T(8,128)(2,1)S(1)}, f32[512,8]{1,0:T(8,128)S(1)}) custom-call(s32[3]{0:T(128)S(1)} %pad_add_fusion.place, s32[4,8]{1,0:T(4,128)} %bitcast.21, bf16[512,256]{1,0:T(8,128)(2,1)S(1)} %get-tuple-element.59.rows_in, ...), custom_call_target="tpu_custom_call" | custom-call | flops 1073741824 | bytes 6717580 | tf_op jit(solution)/shard_map/pallas_call | solution.py:23
  7.4 3.3 %collective-permute-start = (bf16[4,512,128]{2,1,0:T(8,128)(2,1)S(1)}, bf16[4,512,128]{2,1,0:T(8,128)(2,1)S(1)}, u32[]{:S(2)}, u32[]{:S(2)}) collective-permute-start(bf16[4,512,128]{2,1,0:T(8,128)(2,1)S(1)} %get-tuple-element.79), channel_id=1, source_target_pairs={{0,1},{1,0},{2,3},{3,2},{4,5},{5,4},{6,7},{7,6},{8,9},{9,8},{10,11... | collective-permute-start | bytes 1572872 | tf_op jit(solution)/shard_map/ppermute | solution.py:308
  10.7 0.1 collective-permute-start.1
  10.8 0.0 copy-done
  10.8 0.0 copy-done.1
  10.8 0.6 shard_map.124
  11.4 0.8 collective-permute-done.came_a
  12.3 0.7 collective-permute-done.1.came_b
  13.0 0.6 shard_map.128
  13.6 0.9 collective-permute-start.4
  14.5 0.6 shard_map.127
  15.1 0.6 collective-permute-start.3
  15.7 0.6 shard_map.126
  16.3 0.7 collective-permute-start.2
  16.9 0.6 shard_map.125.own
  17.5 3.6 %collective-permute-done.4.three = bf16[2,512,128]{2,1,0:T(8,128)(2,1)S(1)} collective-permute-done((bf16[2,512,128]{2,1,0:T(8,128)(2,1)S(1)}, bf16[2,512,128]{2,1,0:T(8,128)(2,1)S(1)}, u32[]{:S(2)}, u32[]{:S(2)}) %collective-permute-start.4) | collective-permute-done | bytes 262176 | tf_op jit(solution)/shard_map/ppermute | solution.py:280
  21.2 2.7 %collective-permute-done.3.two = bf16[2,512,128]{2,1,0:T(8,128)(2,1)S(1)} collective-permute-done((bf16[2,512,128]{2,1,0:T(8,128)(2,1)S(1)}, bf16[2,512,128]{2,1,0:T(8,128)(2,1)S(1)}, u32[]{:S(2)}, u32[]{:S(2)}) %collective-permute-start.3) | collective-permute-done | bytes 262176 | tf_op jit(solution)/shard_map/ppermute | solution.py:280
  23.9 6.6 %collective-permute-done.2.one = bf16[2,512,128]{2,1,0:T(8,128)(2,1)S(1)} collective-permute-done((bf16[2,512,128]{2,1,0:T(8,128)(2,1)S(1)}, bf16[2,512,128]{2,1,0:T(8,128)(2,1)S(1)}, u32[]{:S(2)}, u32[]{:S(2)}) %collective-permute-start.2) | collective-permute-done | bytes 262176 | tf_op jit(solution)/shard_map/ppermute | solution.py:280
  30.5 1.7 %shard_map.129 = (f32[512,128]{1,0:T(8,128)S(1)}, f32[512,128]{1,0:T(8,128)S(1)}, f32[4,4,2,8,128]{4,3,2,1,0:T(8,128)S(1)}, f32[32,16,128]{2,1,0:T(8,128)S(1)}) custom-call(s32[3]{0:T(128)S(1)} %pad_add_fusion.place, f32[2,512,128]{2,1,0:T(8,128)S(1)} %shard_map.125.own, bf16[2,512,128]{2,1,0:T(8,128)(2,1)S(1)} %collective-permute-done.2.one, ...), custom_call_target="tpu_custom_call" | custom-call | bytes 3047436 | tf_op jit(solution)/shard_map/pallas_call | solution.py:23
  32.2 22.6 %all_to_all.5.parcel = f32[32,16,128]{2,1,0:T(8,128)S(1)} all-to-all(f32[32,16,128]{2,1,0:T(8,128)S(1)} %get-tuple-element.86), channel_id=1, replica_groups=mesh['tm'=32,'state'=8] {'tm'}, dimensions={0} | all-to-all | bytes 524288 | tf_op jit(solution)/shard_map/all_to_all | solution.py:336
  54.7 1.3 %shard_map.130 = (bf16[2,512,128]{2,1,0:T(8,128)(2,1)S(1)}, bf16[1,512,128]{2,1,0:T(8,128)(2,1)S(1)}, bf16[1,512,128]{2,1,0:T(8,128)(2,1)S(1)}) custom-call(s32[3]{0:T(128)S(1)} %pad_add_fusion.place, f32[32,16,128]{2,1,0:T(8,128)S(1)} %all_to_all.5.parcel, f32[4,4,2,8,128]{4,3,2,1,0:T(8,128)S(1)} %get-tuple-element.87.before, ...), custom_call_target="tpu_custom_call" | custom-call | bytes 2752524 | tf_op jit(solution)/shard_map/pallas_call | solution.py:23
  56.0 2.3 %collective-permute-start.5 = (bf16[2,512,128]{2,1,0:T(8,128)(2,1)S(1)}, bf16[2,512,128]{2,1,0:T(8,128)(2,1)S(1)}, u32[]{:S(2)}, u32[]{:S(2)}) collective-permute-start(bf16[2,512,128]{2,1,0:T(8,128)(2,1)S(1)} %get-tuple-element.94.refs_0_), channel_id=1, source_target_pairs={{0,1},{1,0},{2,3},{3,2},{4,5},{5,4},{6,7},{7,6},{8,9},{9,8},{10,11... | collective-permute-start | bytes 786440 | tf_op jit(solution)/shard_map/ppermute | solution.py:351
  58.4 0.0 collective-permute-start.6
  58.4 2.7 %collective-permute-start.8 = (bf16[2,512,128]{2,1,0:T(8,128)(2,1)S(1)}, bf16[2,512,128]{2,1,0:T(8,128)(2,1)S(1)}, u32[]{:S(2)}, u32[]{:S(2)}) collective-permute-start(bf16[2,512,128]{2,1,0:T(8,128)(2,1)S(1)} %get-tuple-element.94.refs_0_), channel_id=1, source_target_pairs={{0,6},{1,7},{2,0},{3,1},{4,2},{5,3},{6,4},{7,5},{8,14},{9,15},{10,... | collective-permute-start | bytes 786440 | tf_op jit(solution)/shard_map/ppermute | solution.py:280
  61.0 0.0 collective-permute-done.5.refs_1_
  61.0 1.3 %shard_map.131 = (f32[512,1024]{1,0:T(8,128)S(1)}, f32[512,1024]{1,0:T(8,128)S(1)}) custom-call(s32[3]{0:T(128)S(1)} %pad_add_fusion.place, bf16[1024,1024]{1,0:T(8,128)(2,1)S(1)} %get-tuple-element.58.load_weights, bf16[1024,1024]{1,0:T(8,128)(2,1)S(1)} %get-tuple-element.65.gain_weights, f32[512,8]{1,0:T(8,128)S(1)} %get-tuple-element.66.mask, ...), custom_call_target="tpu_custom_call" | custom-call | flops 536870912 | bytes 8929292 | tf_op jit(solution)/shard_map/pallas_call | solution.py:23
  62.3 5.0 %collective-permute-done.6.refs_0_ = bf16[2,512,128]{2,1,0:T(8,128)(2,1)S(1)} collective-permute-done((bf16[2,512,128]{2,1,0:T(8,128)(2,1)S(1)}, bf16[2,512,128]{2,1,0:T(8,128)(2,1)S(1)}, u32[]{:S(2)}, u32[]{:S(2)}) %collective-permute-start.6) | collective-permute-done | bytes 262176 | tf_op jit(solution)/shard_map/ppermute | solution.py:280
  67.3 0.9 %collective-permute-start.7 = (bf16[2,512,128]{2,1,0:T(8,128)(2,1)S(1)}, bf16[2,512,128]{2,1,0:T(8,128)(2,1)S(1)}, u32[]{:S(2)}, u32[]{:S(2)}) collective-permute-start(bf16[2,512,128]{2,1,0:T(8,128)(2,1)S(1)} %collective-permute-done.6.refs_0_), channel_id=1, source_target_pairs={{0,1},{1,0},{2,3},{3,2},{4,5},{5,4},{6,7},{7,6},{8,9},{9,8},{10,11... | collective-permute-start | bytes 786440 | tf_op jit(solution)/shard_map/ppermute | solution.py:351
  68.3 0.0 collective-permute-done.8.refs_0_
  68.3 0.0 collective-permute-start.11
  68.3 1.2 %collective-permute-start.9 = (bf16[1,512,128]{2,1,0:T(8,128)(2,1)S(1)}, bf16[1,512,128]{2,1,0:T(8,128)(2,1)S(1)}, u32[]{:S(2)}, u32[]{:S(2)}) collective-permute-start(bf16[1,512,128]{2,1,0:T(8,128)(2,1)S(1)} %get-tuple-element.104), channel_id=1, source_target_pairs={{0,4},{1,5},{2,6},{3,7},{4,0},{5,1},{6,2},{7,3},{8,12},{9,13},{10,... | collective-permute-start | bytes 393224 | tf_op jit(solution)/shard_map/ppermute | solution.py:280
  69.5 0.0 collective-permute-done.7.refs_1_
  69.5 1.3 %shard_map.132 = (f32[512,1024]{1,0:T(8,128)S(1)}, f32[512,1024]{1,0:T(8,128)S(1)}) custom-call(s32[3]{0:T(128)S(1)} %pad_add_fusion.place, bf16[1024,1024]{1,0:T(8,128)(2,1)S(1)} %get-tuple-element.58.load_weights, bf16[1024,1024]{1,0:T(8,128)(2,1)S(1)} %get-tuple-element.65.gain_weights, f32[512,8]{1,0:T(8,128)S(1)} %get-tuple-element.66.mask, ...), custom_call_target="tpu_custom_call" | custom-call | flops 536870912 | bytes 13123596 | tf_op jit(solution)/shard_map/pallas_call | solution.py:23
  70.8 3.5 %collective-permute-done.9.refs_0_ = bf16[1,512,128]{2,1,0:T(8,128)(2,1)S(1)} collective-permute-done((bf16[1,512,128]{2,1,0:T(8,128)(2,1)S(1)}, bf16[1,512,128]{2,1,0:T(8,128)(2,1)S(1)}, u32[]{:S(2)}, u32[]{:S(2)}) %collective-permute-start.9) | collective-permute-done | bytes 131104 | tf_op jit(solution)/shard_map/ppermute | solution.py:280
  74.3 1.4 %collective-permute-start.10 = (bf16[1,512,128]{2,1,0:T(8,128)(2,1)S(1)}, bf16[1,512,128]{2,1,0:T(8,128)(2,1)S(1)}, u32[]{:S(2)}, u32[]{:S(2)}) collective-permute-start(bf16[1,512,128]{2,1,0:T(8,128)(2,1)S(1)} %collective-permute-done.9.refs_0_), channel_id=1, source_target_pairs={{0,1},{1,0},{2,3},{3,2},{4,5},{5,4},{6,7},{7,6},{8,9},{9,8},{10,11... | collective-permute-start | bytes 393224 | tf_op jit(solution)/shard_map/ppermute | solution.py:351
  75.7 1.2 %collective-permute-start.12 = (bf16[1,512,128]{2,1,0:T(8,128)(2,1)S(1)}, bf16[1,512,128]{2,1,0:T(8,128)(2,1)S(1)}, u32[]{:S(2)}, u32[]{:S(2)}) collective-permute-start(bf16[1,512,128]{2,1,0:T(8,128)(2,1)S(1)} %get-tuple-element.110), channel_id=1, source_target_pairs={{0,4},{1,5},{2,6},{3,7},{4,0},{5,1},{6,2},{7,3},{8,12},{9,13},{10,... | collective-permute-start | bytes 393224 | tf_op jit(solution)/shard_map/ppermute | solution.py:280
  76.9 0.0 collective-permute-done.11.refs_1_
  76.9 1.3 %shard_map.133 = (f32[512,1024]{1,0:T(8,128)S(1)}, f32[512,1024]{1,0:T(8,128)S(1)}) custom-call(s32[3]{0:T(128)S(1)} %pad_add_fusion.place, bf16[1024,1024]{1,0:T(8,128)(2,1)S(1)} %get-tuple-element.58.load_weights, bf16[1024,1024]{1,0:T(8,128)(2,1)S(1)} %get-tuple-element.65.gain_weights, f32[512,8]{1,0:T(8,128)S(1)} %get-tuple-element.66.mask, ...), custom_call_target="tpu_custom_call" | custom-call | flops 536870912 | bytes 13123596 | tf_op jit(solution)/shard_map/pallas_call | solution.py:23
  78.2 0.0 collective-permute-done.10.refs_1_
  78.2 1.9 %shard_map.134 = bf16[512,1024]{1,0:T(8,128)(2,1)} custom-call(s32[3]{0:T(128)S(1)} %pad_add_fusion.place, bf16[1024,1024]{1,0:T(8,128)(2,1)S(1)} %get-tuple-element.58.load_weights, bf16[1024,1024]{1,0:T(8,128)(2,1)S(1)} %get-tuple-element.65.gain_weights, f32[512,8]{1,0:T(8,128)S(1)} %get-tuple-element.66.mask, ...), custom_call_target="tpu_custom_call" | custom-call | flops 268435456 | bytes 7618572 | tf_op jit(solution)/shard_map/pallas_call | solution.py:23
  80.2 2.1 %collective-permute-done.12.refs_0_ = bf16[1,512,128]{2,1,0:T(8,128)(2,1)S(1)} collective-permute-done((bf16[1,512,128]{2,1,0:T(8,128)(2,1)S(1)}, bf16[1,512,128]{2,1,0:T(8,128)(2,1)S(1)}, u32[]{:S(2)}, u32[]{:S(2)}) %collective-permute-start.12) | collective-permute-done | bytes 131104 | tf_op jit(solution)/shard_map/ppermute | solution.py:280
  82.3 0.9 collective-permute-start.13
  83.1 1.0 %collective-permute-done.13.refs_1_ = bf16[1,512,128]{2,1,0:T(8,128)(2,1)S(1)} collective-permute-done((bf16[1,512,128]{2,1,0:T(8,128)(2,1)S(1)}, bf16[1,512,128]{2,1,0:T(8,128)(2,1)S(1)}, u32[]{:S(2)}, u32[]{:S(2)}) %collective-permute-start.13) | collective-permute-done | bytes 131104 | tf_op jit(solution)/shard_map/ppermute | solution.py:351
  84.1 2.1 %shard_map.135 = bf16[512,1024]{1,0:T(8,128)(2,1)} custom-call(s32[3]{0:T(128)S(1)} %pad_add_fusion.place, bf16[1024,1024]{1,0:T(8,128)(2,1)S(1)} %get-tuple-element.58.load_weights, bf16[1024,1024]{1,0:T(8,128)(2,1)S(1)} %get-tuple-element.65.gain_weights, f32[512,8]{1,0:T(8,128)S(1)} %get-tuple-element.66.mask, ...), custom_call_target="tpu_custom_call" | custom-call | flops 268435456 | bytes 7618572 | tf_op jit(solution)/shard_map/pallas_call | solution.py:23
Async XLA Ops:
  4.4 6.5 %copy-start = (f32[128,4,128]{2,1,0:T(4,128)S(1)}, f32[128,4,128]{2,1,0:T(4,128)}, u32[]{:S(2)}) copy-start(f32[128,4,128]{2,1,0:T(4,128)} %param.19) | copy-start | bytes 786436
  4.4 6.5 %copy-start.1 = (f32[128,4,128]{2,1,0:T(4,128)S(1)}, f32[128,4,128]{2,1,0:T(4,128)}, u32[]{:S(2)}) copy-start(f32[128,4,128]{2,1,0:T(4,128)} %param.20) | copy-start | bytes 786436
  7.4 4.8 %collective-permute-start = (bf16[4,512,128]{2,1,0:T(8,128)(2,1)S(1)}, bf16[4,512,128]{2,1,0:T(8,128)(2,1)S(1)}, u32[]{:S(2)}, u32[]{:S(2)}) collective-permute-start(bf16[4,512,128]{2,1,0:T(8,128)(2,1)S(1)} %get-tuple-element.79), channel_id=1, source_target_pairs={{0,1},{1,0},{2,3},{3,2},{4,5},{5,4},{6,7},{7,6},{8,9},{9,8},{10,11... | collective-permute-start | bytes 1572872 | tf_op jit(solution)/shard_map/ppermute | solution.py:308
  10.7 2.3 %collective-permute-start.1 = (bf16[4,512,128]{2,1,0:T(8,128)(2,1)S(1)}, bf16[4,512,128]{2,1,0:T(8,128)(2,1)S(1)}, u32[]{:S(2)}, u32[]{:S(2)}) collective-permute-start(bf16[4,512,128]{2,1,0:T(8,128)(2,1)S(1)} %get-tuple-element.80), channel_id=1, source_target_pairs={{0,1},{1,0},{2,3},{3,2},{4,5},{5,4},{6,7},{7,6},{8,9},{9,8},{10,11... | collective-permute-start | bytes 1572872 | tf_op jit(solution)/shard_map/ppermute | solution.py:299
  13.6 7.6 %collective-permute-start.4 = (bf16[2,512,128]{2,1,0:T(8,128)(2,1)S(1)}, bf16[2,512,128]{2,1,0:T(8,128)(2,1)S(1)}, u32[]{:S(2)}, u32[]{:S(2)}) collective-permute-start(bf16[2,512,128]{2,1,0:T(8,128)(2,1)S(1)} %shard_map.128), channel_id=1, source_target_pairs={{0,6},{1,7},{2,0},{3,1},{4,2},{5,3},{6,4},{7,5},{8,14},{9,15},{10,... | collective-permute-start | bytes 786440 | tf_op jit(solution)/shard_map/ppermute | solution.py:280
  15.1 8.8 %collective-permute-start.3 = (bf16[2,512,128]{2,1,0:T(8,128)(2,1)S(1)}, bf16[2,512,128]{2,1,0:T(8,128)(2,1)S(1)}, u32[]{:S(2)}, u32[]{:S(2)}) collective-permute-start(bf16[2,512,128]{2,1,0:T(8,128)(2,1)S(1)} %shard_map.127), channel_id=1, source_target_pairs={{0,4},{1,5},{2,6},{3,7},{4,0},{5,1},{6,2},{7,3},{8,12},{9,13},{10,... | collective-permute-start | bytes 786440 | tf_op jit(solution)/shard_map/ppermute | solution.py:280
  16.3 14.2 %collective-permute-start.2 = (bf16[2,512,128]{2,1,0:T(8,128)(2,1)S(1)}, bf16[2,512,128]{2,1,0:T(8,128)(2,1)S(1)}, u32[]{:S(2)}, u32[]{:S(2)}) collective-permute-start(bf16[2,512,128]{2,1,0:T(8,128)(2,1)S(1)} %shard_map.126), channel_id=1, source_target_pairs={{0,2},{1,3},{2,4},{3,5},{4,6},{5,7},{6,0},{7,1},{8,10},{9,11},{10,... | collective-permute-start | bytes 786440 | tf_op jit(solution)/shard_map/ppermute | solution.py:280
  56.0 5.0 %collective-permute-start.5 = (bf16[2,512,128]{2,1,0:T(8,128)(2,1)S(1)}, bf16[2,512,128]{2,1,0:T(8,128)(2,1)S(1)}, u32[]{:S(2)}, u32[]{:S(2)}) collective-permute-start(bf16[2,512,128]{2,1,0:T(8,128)(2,1)S(1)} %get-tuple-element.94.refs_0_), channel_id=1, source_target_pairs={{0,1},{1,0},{2,3},{3,2},{4,5},{5,4},{6,7},{7,6},{8,9},{9,8},{10,11... | collective-permute-start | bytes 786440 | tf_op jit(solution)/shard_map/ppermute | solution.py:351
  58.4 9.0 %collective-permute-start.6 = (bf16[2,512,128]{2,1,0:T(8,128)(2,1)S(1)}, bf16[2,512,128]{2,1,0:T(8,128)(2,1)S(1)}, u32[]{:S(2)}, u32[]{:S(2)}) collective-permute-start(bf16[2,512,128]{2,1,0:T(8,128)(2,1)S(1)} %get-tuple-element.94.refs_0_), channel_id=1, source_target_pairs={{0,2},{1,3},{2,4},{3,5},{4,6},{5,7},{6,0},{7,1},{8,10},{9,11},{10,... | collective-permute-start | bytes 786440 | tf_op jit(solution)/shard_map/ppermute | solution.py:280
  58.4 9.9 %collective-permute-start.8 = (bf16[2,512,128]{2,1,0:T(8,128)(2,1)S(1)}, bf16[2,512,128]{2,1,0:T(8,128)(2,1)S(1)}, u32[]{:S(2)}, u32[]{:S(2)}) collective-permute-start(bf16[2,512,128]{2,1,0:T(8,128)(2,1)S(1)} %get-tuple-element.94.refs_0_), channel_id=1, source_target_pairs={{0,6},{1,7},{2,0},{3,1},{4,2},{5,3},{6,4},{7,5},{8,14},{9,15},{10,... | collective-permute-start | bytes 786440 | tf_op jit(solution)/shard_map/ppermute | solution.py:280
  67.3 2.1 %collective-permute-start.7 = (bf16[2,512,128]{2,1,0:T(8,128)(2,1)S(1)}, bf16[2,512,128]{2,1,0:T(8,128)(2,1)S(1)}, u32[]{:S(2)}, u32[]{:S(2)}) collective-permute-start(bf16[2,512,128]{2,1,0:T(8,128)(2,1)S(1)} %collective-permute-done.6.refs_0_), channel_id=1, source_target_pairs={{0,1},{1,0},{2,3},{3,2},{4,5},{5,4},{6,7},{7,6},{8,9},{9,8},{10,11... | collective-permute-start | bytes 786440 | tf_op jit(solution)/shard_map/ppermute | solution.py:351
  68.3 8.6 %collective-permute-start.11 = (bf16[2,512,128]{2,1,0:T(8,128)(2,1)S(1)}, bf16[2,512,128]{2,1,0:T(8,128)(2,1)S(1)}, u32[]{:S(2)}, u32[]{:S(2)}) collective-permute-start(bf16[2,512,128]{2,1,0:T(8,128)(2,1)S(1)} %collective-permute-done.8.refs_0_), channel_id=1, source_target_pairs={{0,1},{1,0},{2,3},{3,2},{4,5},{5,4},{6,7},{7,6},{8,9},{9,8},{10,11... | collective-permute-start | bytes 786440 | tf_op jit(solution)/shard_map/ppermute | solution.py:351
  68.3 6.1 %collective-permute-start.9 = (bf16[1,512,128]{2,1,0:T(8,128)(2,1)S(1)}, bf16[1,512,128]{2,1,0:T(8,128)(2,1)S(1)}, u32[]{:S(2)}, u32[]{:S(2)}) collective-permute-start(bf16[1,512,128]{2,1,0:T(8,128)(2,1)S(1)} %get-tuple-element.104), channel_id=1, source_target_pairs={{0,4},{1,5},{2,6},{3,7},{4,0},{5,1},{6,2},{7,3},{8,12},{9,13},{10,... | collective-permute-start | bytes 393224 | tf_op jit(solution)/shard_map/ppermute | solution.py:280
  74.3 3.9 %collective-permute-start.10 = (bf16[1,512,128]{2,1,0:T(8,128)(2,1)S(1)}, bf16[1,512,128]{2,1,0:T(8,128)(2,1)S(1)}, u32[]{:S(2)}, u32[]{:S(2)}) collective-permute-start(bf16[1,512,128]{2,1,0:T(8,128)(2,1)S(1)} %collective-permute-done.9.refs_0_), channel_id=1, source_target_pairs={{0,1},{1,0},{2,3},{3,2},{4,5},{5,4},{6,7},{7,6},{8,9},{9,8},{10,11... | collective-permute-start | bytes 393224 | tf_op jit(solution)/shard_map/ppermute | solution.py:351
  75.7 6.6 %collective-permute-start.12 = (bf16[1,512,128]{2,1,0:T(8,128)(2,1)S(1)}, bf16[1,512,128]{2,1,0:T(8,128)(2,1)S(1)}, u32[]{:S(2)}, u32[]{:S(2)}) collective-permute-start(bf16[1,512,128]{2,1,0:T(8,128)(2,1)S(1)} %get-tuple-element.110), channel_id=1, source_target_pairs={{0,4},{1,5},{2,6},{3,7},{4,0},{5,1},{6,2},{7,3},{8,12},{9,13},{10,... | collective-permute-start | bytes 393224 | tf_op jit(solution)/shard_map/ppermute | solution.py:280
  82.3 1.8 %collective-permute-start.13 = (bf16[1,512,128]{2,1,0:T(8,128)(2,1)S(1)}, bf16[1,512,128]{2,1,0:T(8,128)(2,1)S(1)}, u32[]{:S(2)}, u32[]{:S(2)}) collective-permute-start(bf16[1,512,128]{2,1,0:T(8,128)(2,1)S(1)} %collective-permute-done.12.refs_0_), channel_id=1, source_target_pairs={{0,1},{1,0},{2,3},{3,2},{4,5},{5,4},{6,7},{7,6},{8,9},{9,8},{10,11... | collective-permute-start | bytes 393224 | tf_op jit(solution)/shard_map/ppermute | solution.py:351

commit v3 on v1

--- a/solution.py
+++ b/solution.py
@@ -16,14 +16,14 @@
 NN = (((1,), (0,)), ((), ()))
 
 
-def call(kernel, outs, operands, scratch=(), smem=0, hbm=0, hbm_out=False, flops=0):
-    vmem, scalar = pl.BlockSpec(memory_space=pltpu.VMEM), pl.BlockSpec(memory_space=pltpu.SMEM)
+def call(kernel, outs, operands, scratch=(), hbm=0, hbm_out=False, flops=0):
+    vmem = pl.BlockSpec(memory_space=pltpu.VMEM)
     far = pl.BlockSpec(memory_space=pltpu.HBM)
     moved = sum(a.size * a.dtype.itemsize for a in (*operands, *outs))
     return pl.pallas_call(
         kernel,
         out_shape=outs,
-        in_specs=[scalar] * smem + [vmem] * (len(operands) - smem - hbm) + [far] * hbm,
+        in_specs=[vmem] * (len(operands) - hbm) + [far] * hbm,
         out_specs=tuple([far if hbm_out else vmem] * len(outs)),
         scratch_shapes=list(scratch),
         compiler_params=pltpu.CompilerParams(vmem_limit_bytes=VMEM),
@@ -39,70 +39,80 @@
     return jax.ShapeDtypeStruct(shape, dtype)
 
 
-def front_kernel(
-    place, pattern, load_far, cot_far, gain_far, available_far, readings_far, rows_far, enc_in_far, enc_out_far,
-    load_weights, gain_weights, keep, send, mask,
-    load, cotangent, gain, available, lhs, rows_in, enc_in, enc_out, sems,
+def here():
+    at = lax.axis_index("state")
+    return lax.div(at, 2), lax.rem(at, 2)
+
+
+def split(keep, send, at, total):
+    mine = here()[1] == 0
+    low, high = total[:, :BLK], total[:, BLK:]
+    keep[at] = jnp.where(mine, low, high)
+    send[at] = jnp.where(mine, high, low).astype(BF16)
+
+
+def window_of(at):
+    return slice(at * 2 * BLK, (at + 1) * 2 * BLK)
+
+
+def pull_kernel(
+    table_far, load_far, cot_far, rows_far, enc_in_far, enc_out_far, gain_far, available_far, readings_far,
+    weights, keep, send, rows_in, enc_in, enc_out, gain, available, readings,
+    pattern, load, cotangent, sems,
 ):
-    core = place[1]
     pairs = (
-        (load_far, load), (cot_far, cotangent), (gain_far, gain), (available_far, available),
-        (readings_far, lhs), (rows_far, rows_in), (enc_in_far, enc_in), (enc_out_far, enc_out),
+        (table_far, pattern),
+        (load_far, load), (cot_far, cotangent), (rows_far, rows_in), (enc_in_far, enc_in), (enc_out_far, enc_out),
+        (gain_far, gain), (available_far, available), (readings_far, readings),
     )
     copies = [pltpu.make_async_copy(far, near, sems.at[i]) for i, (far, near) in enumerate(pairs)]
     for copy in copies:
         copy.start()
-    load_weights[...] = jnp.zeros_like(load_weights)
-    gain_weights[...] = jnp.zeros_like(gain_weights)
-    traces, blocks, steps = available.shape
-    reads = pattern.shape[0]
-
-    def split(which, at, total):
-        low, high = total[:, :BLK], total[:, BLK:]
-        keep[at, which] = jnp.where(core == 0, low, high)
-        send[at, which] = jnp.where(core == 0, high, low).astype(BF16)
-
+    weights[...] = jnp.zeros_like(weights)
     copies[0].wait()
-    for q in range(blocks):
-        for k in range(reads):
+    copies[1].wait()
+    for q in range(load.shape[0]):
+        for k in range(load.shape[1]):
             row = pl.multiple_of(pattern[k, q] * BLK, BLK)
-            load_weights[pl.ds(row, BLK), q * BLK : (q + 1) * BLK] = load[q, k]
-    copies[1].wait()
-
-    def pull_columns(at, _):
-        window = pl.ds(pl.multiple_of(at * 2 * BLK, 2 * BLK), 2 * BLK)
-        split(1, at, lax.dot_general(cotangent[...], load_weights[window, :], NT, preferred_element_type=F32))
-        return 0
-
-    lax.fori_loop(0, 4, pull_columns, 0)
+            weights[pl.ds(row, BLK), q * BLK : (q + 1) * BLK] = load[q, k]
     copies[2].wait()
-    for q in range(blocks):
-        for k in range(reads):
-            column = pl.multiple_of(pattern[k, q] * BLK, BLK)
-            gain_weights[q * BLK : (q + 1) * BLK, pl.ds(column, BLK)] = gain[q, k]
+    for at in range(keep.shape[0]):
+        total = lax.dot_general(cotangent[...], weights[window_of(at), :], NT, preferred_element_type=F32)
+        split(keep, send, at, total)
     for copy in copies[3:]:
         copy.wait()
+
+
+def drive_kernel(
+    rows_in, enc_in, enc_out, gain, available, readings, table_far,
+    weights, keep, send, mask,
+    lhs, pattern, sem,
+):
+    fetch = pltpu.make_async_copy(table_far, pattern, sem)
+    fetch.start()
+    traces, blocks, steps = available.shape
+    hidden = jax.nn.gelu(jnp.dot(rows_in[...], enc_in[...], preferred_element_type=F32)).astype(BF16)
+    weights[...] = jnp.zeros_like(weights)
     for b in range(traces):
         mask[b * steps : (b + 1) * steps, :] = available[b].astype(F32).T
+    fetch.wait()
     for q in range(blocks):
-        lhs[:, q * BLK : (q + 1) * BLK] = lhs[:, q * BLK : (q + 1) * BLK] * mask[:, q : q + 1].astype(BF16)
-    hidden = jax.nn.gelu(jnp.dot(rows_in[...], enc_in[...], preferred_element_type=F32)).astype(BF16)
-
-    def drive_columns(at, _):
-        window = pl.ds(pl.multiple_of(at * 2 * BLK, 2 * BLK), 2 * BLK)
-        total = jnp.dot(lhs[...], gain_weights[:, window], preferred_element_type=F32)
-        total += jnp.dot(hidden, enc_out[:, window], preferred_element_type=F32)
-        split(0, at, total)
-        return 0
-
-    lax.fori_loop(0, 4, drive_columns, 0)
-
-
-def merge_kernel(place, keep, came, own, *pieces):
-    own[...] = keep[place[0]] + came[place[0]].astype(F32)
-    for k, piece in enumerate(pieces):
-        at = lax.rem(place[0] + k + 1, keep.shape[0])
-        piece[...] = (keep[at] + came[at].astype(F32)).astype(BF16)
+        for k in range(gain.shape[1]):
+            column = pl.multiple_of(pattern[k, q] * BLK, BLK)
+            weights[q * BLK : (q + 1) * BLK, pl.ds(column, BLK)] = gain[q, k]
+        lhs[:, q * BLK : (q + 1) * BLK] = readings[:, q * BLK : (q + 1) * BLK] * mask[:, q : q + 1].astype(BF16)
+    for at in range(keep.shape[0]):
+        total = jnp.dot(lhs[...], weights[:, window_of(at)], preferred_element_type=F32)
+        total += jnp.dot(hidden, enc_out[:, window_of(at)], preferred_element_type=F32)
+        split(keep, send, at, total)
+
+
+def merge_kernel(keep_a, keep_b, came_a, came_b, own, *pieces):
+    x, _ = here()
+    for which, (keep, came) in enumerate(((keep_a, came_a), (keep_b, came_b))):
+        for k, piece in enumerate((own, *pieces)):
+            at = lax.rem(x + k, keep.shape[0])
+            piece[which] = (keep[at] + came[at].astype(F32)).astype(piece.dtype)
 
 
 def rows_of(b, u, steps):
@@ -152,7 +162,7 @@
 
 
 def scan_kernel(
-    traces, steps, place,
+    traces, steps,
     own, one, two, three, keep_r, keep_s, root, seg_r, seg_s,
     states, grads, before, parcel,
     source, pull, ends,
@@ -189,7 +199,7 @@
             half, row = which // 2, (which % 2) * traces + b
             ends[half, 0, row : row + 1, :] = total[end : end + 1, :]
             ends[half, 1, row : row + 1, :] = whole[end : end + 1, :]
-    me = place[2]
+    me = lax.axis_index("tm")
     for target in range(parcel.shape[0]):
         onward = target > me
         parcel[target, :SEG] = jnp.where(onward, ends[0, 0], ends[1, 0])
@@ -197,12 +207,12 @@
 
 
 def settle_kernel(
-    traces, steps, place,
+    traces, steps,
     parcel, before, states, grads, root, ahead_p, filt_p, rise_p, fall_p,
     smoothed,
     sums, carry,
 ):
-    me, length = place[2], parcel.shape[0]
+    me, length = lax.axis_index("tm"), parcel.shape[0]
     onward = jnp.zeros((SEG, BLK), F32)
     back = onward
     for j in range(length):
@@ -223,11 +233,11 @@
     smoothed[...] = sums[...].astype(BF16)
 
 
-def project_kernel(shift, last, place, mine, partner, load_weights, gain_weights, mask, *refs):
+def project_kernel(shift, last, mine, partner, load_weights, gain_weights, mask, *refs):
     before, refs = ((), refs) if shift == 0 else (refs[:2], refs[2:])
     outs, lhs, *rest = refs[:2], *refs[2:]
-    core = place[1]
-    block = pl.multiple_of(2 * BLK * lax.rem(place[0] - shift + 4, 4), 2 * BLK)
+    x, core = here()
+    block = pl.multiple_of(2 * BLK * lax.rem(x - shift + 4, 4), 2 * BLK)
     states = pl.ds(block, 2 * BLK)
     copies = []
     for which in range(2):
@@ -252,10 +262,12 @@
                 if which == 1:
                     piece = piece * mask[:, q : q + 1]
                 stage[which, :, q * BLK : (q + 1) * BLK] = piece.astype(BF16)
-            copies.append(
-                pltpu.make_async_copy(stage.at[which, :, window], outs[which].at[:, window], sems.at[which, at])
-            )
-            copies[-1].start()
+            if at % 2:
+                window = slice((at - 1) * 2 * BLK, (at + 1) * 2 * BLK)
+                copies.append(
+                    pltpu.make_async_copy(stage.at[which, :, window], outs[which].at[:, window], sems.at[which, at // 2])
+                )
+                copies[-1].start()
     for copy in copies:
         copy.wait()
 
@@ -266,36 +278,47 @@
     sensors, blocks = readings.shape[2], available.shape[2]
     states = encoder_out.shape[1]
     axis, times = lax.axis_size("state"), lax.axis_size("tm")
-    at = lax.axis_index("state")
-    place = jnp.stack([at // 2, at % 2, lax.axis_index("tm")]).astype(jnp.int32)
     swap = [(i, i ^ 1) for i in range(axis)]
+
+    work = 2 * rows * sensors * states
+    both = struct((2, rows, BLK), BF16)
 
     def across(pieces):
         moved = {k: lax.ppermute(pieces[k - 1], "state", [(i, (i + 2 * k) % axis) for i in range(axis)]) for k in (1, 3, 2)}
         return [moved[k] for k in (1, 2, 3)]
 
-    work = 2 * rows * sensors * states
-
-    far = (
-        load, cotangent.reshape(rows, sensors), gain, available.transpose(0, 2, 1),
-        readings.reshape(rows, sensors), inputs.reshape(rows, features), encoder_in, encoder_out,
-    )
-    load_weights, gain_weights, keep, send, mask = call(
-        front_kernel,
-        (
-            struct((states, sensors), BF16),
-            struct((sensors, states), BF16),
-            struct((axis // 2, 2, rows, BLK), F32),
-            struct((axis // 2, 2, rows, BLK), BF16),
-            struct((rows, blocks), F32),
-        ),
-        (place, in_hbm(pattern.T), *far),
-        scratch=[pltpu.VMEM(a.shape, a.dtype) for a in far] + [pltpu.SemaphoreType.DMA((len(far),))],
-        smem=2,
-        hbm=len(far),
-        flops=2 * work,
-    )
-    came = lax.ppermute(send, "state", swap)
+    near = (
+        inputs.reshape(rows, features), encoder_in, encoder_out, gain, available.transpose(0, 2, 1),
+        readings.reshape(rows, sensors),
+    )
+    pulled_from = (load, cotangent.reshape(rows, sensors))
+    table = pattern.T
+    chips = axis // 2
+    parts = (struct((chips, rows, BLK), F32), struct((chips, rows, BLK), BF16))
+    load_weights, keep_b, send_b, *near = call(
+        pull_kernel,
+        (struct((states, sensors), BF16), *parts, *(struct(a.shape, a.dtype) for a in near)),
+        (table, *pulled_from, *near),
+        scratch=[pltpu.SMEM(table.shape, table.dtype)]
+        + [pltpu.VMEM(a.shape, a.dtype) for a in pulled_from]
+        + [pltpu.SemaphoreType.DMA((9,))],
+        hbm=9,
+        flops=work,
+    )
+    came_b = lax.ppermute(send_b, "state", swap)
+    gain_weights, keep_a, send_a, mask = call(
+        drive_kernel,
+        (struct((sensors, states), BF16), *parts, struct((rows, blocks), F32)),
+        (*near, table),
+        scratch=[
+            pltpu.VMEM((rows, sensors), BF16),
+            pltpu.SMEM(table.shape, table.dtype),
+            pltpu.SemaphoreType.DMA,
+        ],
+        hbm=1,
+        flops=work,
+    )
+    came_a = lax.ppermute(send_a, "state", swap)
     full, segments = struct((rows, BLK), F32), struct((traces, SEG, BLK), F32)
     keep_r, keep_s, root, ahead_p, filt_p, rise_p, fall_p, seg_r, seg_s = call(
         functools.partial(decay_kernel, traces, steps),
@@ -303,25 +326,25 @@
         (retain.reshape(-1, steps), smooth.reshape(-1, steps)),
     )
     decays = (keep_r, keep_s, root, ahead_p, filt_p, rise_p, fall_p, seg_r, seg_s)
-    keep, decays = lax.optimization_barrier((keep, decays))
+    keep_a, decays = lax.optimization_barrier((keep_a, decays))
     keep_r, keep_s, root, ahead_p, filt_p, rise_p, fall_p, seg_r, seg_s = decays
     both = struct((2, rows, BLK), BF16)
-    own, *sums = call(merge_kernel, (struct(both.shape, F32),) + (both,) * 3, (place, keep, came), smem=1)
+    own, *sums = call(
+        merge_kernel, (struct(both.shape, F32),) + (both,) * 3, (keep_a, keep_b, came_a, came_b)
+    )
     sums = across(sums)
     scanned, pulled, before, parcel = call(
         functools.partial(scan_kernel, traces, steps),
         (full, full, struct((4, traces, 2, SEG, BLK), F32), struct((times, 2 * SEG, BLK), F32)),
-        (place, own, *sums, keep_r, keep_s, root, seg_r, seg_s),
+        (own, *sums, keep_r, keep_s, root, seg_r, seg_s),
         scratch=[pltpu.VMEM((rows, BLK), F32)] * 2 + [pltpu.VMEM((2, 2, SEG, BLK), F32)],
-        smem=1,
     )
     parcel = lax.all_to_all(parcel, "tm", 0, 0)
     (smoothed,) = call(
         functools.partial(settle_kernel, traces, steps),
         (both,),
-        (place, parcel, before, scanned, pulled, root, ahead_p, filt_p, rise_p, fall_p),
+        (parcel, before, scanned, pulled, root, ahead_p, filt_p, rise_p, fall_p),
         scratch=[pltpu.VMEM((2, rows, BLK), F32), pltpu.VMEM((2, SEG, BLK), F32)],
-        smem=1,
     )
     same = [smoothed, *across([smoothed] * 3)]
     totals = ()
@@ -336,11 +359,10 @@
         totals = call(
             functools.partial(project_kernel, shift, last),
             (struct((rows, sensors), BF16 if last else F32),) * 2,
-            (place, same[shift], partner, load_weights, gain_weights, mask, *totals),
+            (same[shift], partner, load_weights, gain_weights, mask, *totals),
             scratch=[pltpu.VMEM((2, rows, 2 * BLK), BF16)]
-            + ([pltpu.VMEM((2, rows, sensors), BF16), pltpu.SemaphoreType.DMA((2, 4))] if last else []),
-            smem=1,
-            hbm_out=last,
+            + ([pltpu.VMEM((2, rows, sensors), BF16), pltpu.SemaphoreType.DMA((2, 2))] if last else []),
+                hbm_out=last,
             flops=work // 2,
         )
     predicted, sensor_grad = totals

time: 80.4 us -> 75.8 us (0.943)
  Pallas kernels: 18.2 us -> 12.1 us
  waiting for transfers between devices: 24.8 us -> 26.2 us
    pallas_call x9 -> x10, Pallas kernels: 18.2 us -> 12.1 us  [call(): pl.pallas_call(kernel, out_shape=outs, in_specs=[vmem] * (len(operands) -...]
    ppermute x6, waiting for transfers between devices: 23.1 us -> 24.2 us  [across(): lax.ppermute(pieces[k - 1], 'state', [(i, (i + 2 * k) % axis) for i in ra...]
    ppermute x1 -> x2, starting transfers between devices: 3.29 us -> 3.41 us  [the longest x1 3.31 us: local(): came_a = lax.ppermute(send_a, 'state', swap)]
    ppermute x1 -> x2, waiting for transfers between devices: 1.69 us -> 1.6 us  [the longest x1 0.85 us: local(): came_a = lax.ppermute(send_a, 'state', swap)]
  transfers between devices with their start and end apart: 11 -> 12, of which waited for: 6 -> 8; matrix products, arithmetic and copies ran while one was open for 0% -> 0% of each run, Pallas kernels for 6% -> 4%
where the time goes in v3:
time: 75.8 us; the launch traced here: 75.7 us
  waiting for transfers between devices  26.2 us (35%)
  blocking collectives  20.6 us (27%)
  starting transfers between devices  15.9 us (21%)
  Pallas kernels  12.1 us (16%)
  between operations  0.89 us (1%)
    ppermute x6, waiting for transfers between devices, across(): lax.ppermute(pieces[k - 1], 'state', [(i, (i + 2 * k) % axis) for i in ra...  24.2 us
    all_to_all x1, blocking collectives, local(): parcel = lax.all_to_all(parcel, 'tm', 0, 0)  20.6 us
    pallas_call x10, Pallas kernels, call(): pl.pallas_call(kernel, out_shape=outs, in_specs=[vmem] * (len(operands) -...  12.1 us
    ppermute x6, starting transfers between devices, across(): lax.ppermute(pieces[k - 1], 'state', [(i, (i + 2 * k) % axis) for i in ra...  7.12 us
    ppermute x4, starting transfers between devices, local(): partner = lax.ppermute(same[shift], 'state', swap)  5.37 us
    ppermute x1, starting transfers between devices, local(): came_a = lax.ppermute(send_a, 'state', swap)  3.31 us
  transfers between devices with their start and end apart: 12, of which 8 were waited for; matrix products, arithmetic and copies ran while one was open for 0% of the time, Pallas kernels for 4%

profile of v3, /device:TPU:1, one launch (start us, length us, event | category | flops | bytes accessed | tf_op | source)
XLA Modules:
  0.0 75.7 jit_solution(14507040185371543264)
XLA Ops:
  0.6 2.9 %shard_map.122 = (bf16[1024,1024]{1,0:T(8,128)(2,1)S(1)}, f32[4,512,128]{2,1,0:T(8,128)S(1)}, bf16[4,512,128]{2,1,0:T(8,128)(2,1)S(1)}, bf16[512,256]{1,0:T(8,12...) custom-call(s32[4,8]{1,0:T(4,128)} %bitcast.15, ...), custom_call_target="tpu_custom_call" | custom-call | flops 1073741824 | bytes 11829376 | tf_op jit(solution)/shard_map/pallas_call | solution.py:23
  3.6 0.0 copy-start
  3.6 0.0 copy-start.1
  3.6 2.6 %shard_map.123 = (bf16[1024,1024]{1,0:T(8,128)(2,1)S(1)}, f32[4,512,128]{2,1,0:T(8,128)S(1)}, bf16[4,512,128]{2,1,0:T(8,128)(2,1)S(1)}, f32[512,8]{1,0:T(8,128)S(1)}) custom-call(bf16[512,256]{1,0:T(8,128)(2,1)S(1)} %get-tuple-element.59.rows_in, bf16[256,256]{1,0:T(8,128)(2,1)S(1)} %get-tuple-element.60.enc_in, ...), custom_call_target="tpu_custom_call" | custom-call | flops 1073741824 | bytes 6717568 | tf_op jit(solution)/shard_map/pallas_call | solution.py:23
  6.2 3.3 %collective-permute-start = (bf16[4,512,128]{2,1,0:T(8,128)(2,1)S(1)}, bf16[4,512,128]{2,1,0:T(8,128)(2,1)S(1)}, u32[]{:S(2)}, u32[]{:S(2)}) collective-permute-start(bf16[4,512,128]{2,1,0:T(8,128)(2,1)S(1)} %get-tuple-element.77), channel_id=1, source_target_pairs={{0,1},{1,0},{2,3},{3,2},{4,5},{5,4},{6,7},{7,6},{8,9},{9,8},{10,11... | collective-permute-start | bytes 1572872 | tf_op jit(solution)/shard_map/ppermute | solution.py:321
  9.5 0.1 collective-permute-start.1
  9.6 0.0 copy-done
  9.6 0.0 copy-done.1
  9.6 0.6 shard_map.124
  10.2 0.9 %collective-permute-done.came_a = bf16[4,512,128]{2,1,0:T(8,128)(2,1)S(1)} collective-permute-done((bf16[4,512,128]{2,1,0:T(8,128)(2,1)S(1)}, bf16[4,512,128]{2,1,0:T(8,128)(2,1)S(1)}, u32[]{:S(2)}, u32[]{:S(2)}) %collective-permute-start) | collective-permute-done | bytes 524320 | tf_op jit(solution)/shard_map/ppermute | solution.py:321
  11.0 0.7 collective-permute-done.1.came_b
  11.8 0.2 shard_map.125
  12.0 0.1 collective-permute-start.2
  12.0 1.9 %collective-permute-start.3 = (bf16[2,512,128]{2,1,0:T(8,128)(2,1)S(1)}, bf16[2,512,128]{2,1,0:T(8,128)(2,1)S(1)}, u32[]{:S(2)}, u32[]{:S(2)}) collective-permute-start(bf16[2,512,128]{2,1,0:T(8,128)(2,1)S(1)} %get-tuple-element.81), channel_id=1, source_target_pairs={{0,4},{1,5},{2,6},{3,7},{4,0},{5,1},{6,2},{7,3},{8,12},{9,13},{10,... | collective-permute-start | bytes 786440 | tf_op jit(solution)/shard_map/ppermute | solution.py:287
  14.0 1.2 %collective-permute-start.4 = (bf16[2,512,128]{2,1,0:T(8,128)(2,1)S(1)}, bf16[2,512,128]{2,1,0:T(8,128)(2,1)S(1)}, u32[]{:S(2)}, u32[]{:S(2)}) collective-permute-start(bf16[2,512,128]{2,1,0:T(8,128)(2,1)S(1)} %get-tuple-element.82), channel_id=1, source_target_pairs={{0,6},{1,7},{2,0},{3,1},{4,2},{5,3},{6,4},{7,5},{8,14},{9,15},{10,... | collective-permute-start | bytes 786440 | tf_op jit(solution)/shard_map/ppermute | solution.py:287
  15.1 6.3 %collective-permute-done.2.one = bf16[2,512,128]{2,1,0:T(8,128)(2,1)S(1)} collective-permute-done((bf16[2,512,128]{2,1,0:T(8,128)(2,1)S(1)}, bf16[2,512,128]{2,1,0:T(8,128)(2,1)S(1)}, u32[]{:S(2)}, u32[]{:S(2)}) %collective-permute-start.2) | collective-permute-done | bytes 262176 | tf_op jit(solution)/shard_map/ppermute | solution.py:287
  21.4 4.2 %collective-permute-done.3.two = bf16[2,512,128]{2,1,0:T(8,128)(2,1)S(1)} collective-permute-done((bf16[2,512,128]{2,1,0:T(8,128)(2,1)S(1)}, bf16[2,512,128]{2,1,0:T(8,128)(2,1)S(1)}, u32[]{:S(2)}, u32[]{:S(2)}) %collective-permute-start.3) | collective-permute-done | bytes 262176 | tf_op jit(solution)/shard_map/ppermute | solution.py:287
  25.7 1.0 %collective-permute-done.4.three = bf16[2,512,128]{2,1,0:T(8,128)(2,1)S(1)} collective-permute-done((bf16[2,512,128]{2,1,0:T(8,128)(2,1)S(1)}, bf16[2,512,128]{2,1,0:T(8,128)(2,1)S(1)}, u32[]{:S(2)}, u32[]{:S(2)}) %collective-permute-start.4) | collective-permute-done | bytes 262176 | tf_op jit(solution)/shard_map/ppermute | solution.py:287
  26.7 1.1 %shard_map.126 = (f32[512,128]{1,0:T(8,128)S(1)}, f32[512,128]{1,0:T(8,128)S(1)}, f32[4,4,2,8,128]{4,3,2,1,0:T(8,128)S(1)}, f32[32,16,128]{2,1,0:T(8,128)S(1)}) custom-call(f32[2,512,128]{2,1,0:T(8,128)S(1)} %get-tuple-element.79.own, bf16[2,512,128]{2,1,0:T(8,128)(2,1)S(1)} %collective-permute-done.2.one, ...), custom_call_target="tpu_custom_call" | custom-call | bytes 3047424 | tf_op jit(solution)/shard_map/pallas_call | solution.py:23
  27.8 20.6 %all_to_all.5.parcel = f32[32,16,128]{2,1,0:T(8,128)S(1)} all-to-all(f32[32,16,128]{2,1,0:T(8,128)S(1)} %get-tuple-element.88), channel_id=1, replica_groups=mesh['tm'=32,'state'=8] {'tm'}, dimensions={0} | all-to-all | bytes 524288 | tf_op jit(solution)/shard_map/all_to_all | solution.py:342
  48.4 0.7 shard_map.127.mine
  49.1 3.3 %collective-permute-start.5 = (bf16[2,512,128]{2,1,0:T(8,128)(2,1)S(1)}, bf16[2,512,128]{2,1,0:T(8,128)(2,1)S(1)}, u32[]{:S(2)}, u32[]{:S(2)}) collective-permute-start(bf16[2,512,128]{2,1,0:T(8,128)(2,1)S(1)} %shard_map.127.mine), channel_id=1, source_target_pairs={{0,1},{1,0},{2,3},{3,2},{4,5},{5,4},{6,7},{7,6},{8,9},{9,8},{10,11... | collective-permute-start | bytes 786440 | tf_op jit(solution)/shard_map/ppermute | solution.py:358
  52.4 1.1 %collective-permute-start.6 = (bf16[2,512,128]{2,1,0:T(8,128)(2,1)S(1)}, bf16[2,512,128]{2,1,0:T(8,128)(2,1)S(1)}, u32[]{:S(2)}, u32[]{:S(2)}) collective-permute-start(bf16[2,512,128]{2,1,0:T(8,128)(2,1)S(1)} %shard_map.127.mine), channel_id=1, source_target_pairs={{0,2},{1,3},{2,4},{3,5},{4,6},{5,7},{6,0},{7,1},{8,10},{9,11},{10,... | collective-permute-start | bytes 786440 | tf_op jit(solution)/shard_map/ppermute | solution.py:287
  53.5 1.6 %collective-permute-start.8 = (bf16[2,512,128]{2,1,0:T(8,128)(2,1)S(1)}, bf16[2,512,128]{2,1,0:T(8,128)(2,1)S(1)}, u32[]{:S(2)}, u32[]{:S(2)}) collective-permute-start(bf16[2,512,128]{2,1,0:T(8,128)(2,1)S(1)} %shard_map.127.mine), channel_id=1, source_target_pairs={{0,6},{1,7},{2,0},{3,1},{4,2},{5,3},{6,4},{7,5},{8,14},{9,15},{10,... | collective-permute-start | bytes 786440 | tf_op jit(solution)/shard_map/ppermute | solution.py:287
  55.1 0.0 collective-permute-done.5.partner
  55.1 0.7 shard_map.128
  55.9 5.6 %collective-permute-done.6.mine = bf16[2,512,128]{2,1,0:T(8,128)(2,1)S(1)} collective-permute-done((bf16[2,512,128]{2,1,0:T(8,128)(2,1)S(1)}, bf16[2,512,128]{2,1,0:T(8,128)(2,1)S(1)}, u32[]{:S(2)}, u32[]{:S(2)}) %collective-permute-start.6) | collective-permute-done | bytes 262176 | tf_op jit(solution)/shard_map/ppermute | solution.py:287
  61.4 0.9 %collective-permute-start.7 = (bf16[2,512,128]{2,1,0:T(8,128)(2,1)S(1)}, bf16[2,512,128]{2,1,0:T(8,128)(2,1)S(1)}, u32[]{:S(2)}, u32[]{:S(2)}) collective-permute-start(bf16[2,512,128]{2,1,0:T(8,128)(2,1)S(1)} %collective-permute-done.6.mine), channel_id=1, source_target_pairs={{0,1},{1,0},{2,3},{3,2},{4,5},{5,4},{6,7},{7,6},{8,9},{9,8},{10,11... | collective-permute-start | bytes 786440 | tf_op jit(solution)/shard_map/ppermute | solution.py:358
  62.4 1.2 %collective-permute-start.9 = (bf16[2,512,128]{2,1,0:T(8,128)(2,1)S(1)}, bf16[2,512,128]{2,1,0:T(8,128)(2,1)S(1)}, u32[]{:S(2)}, u32[]{:S(2)}) collective-permute-start(bf16[2,512,128]{2,1,0:T(8,128)(2,1)S(1)} %shard_map.127.mine), channel_id=1, source_target_pairs={{0,4},{1,5},{2,6},{3,7},{4,0},{5,1},{6,2},{7,3},{8,12},{9,13},{10,... | collective-permute-start | bytes 786440 | tf_op jit(solution)/shard_map/ppermute | solution.py:287
  63.6 0.0 collective-permute-done.8.mine
  63.6 0.3 collective-permute-start.11
  63.9 0.0 collective-permute-done.7.partner
  63.9 0.8 %shard_map.129 = (f32[512,1024]{1,0:T(8,128)S(1)}, f32[512,1024]{1,0:T(8,128)S(1)}) custom-call(bf16[2,512,128]{2,1,0:T(8,128)(2,1)S(1)} %collective-permute-done.6.mine, bf16[2,512,128]{2,1,0:T(8,128)(2,1)S(1)} %collective-permute-done.7.partner, bf16[1024,1024]{1,0:T(8,128)(2,1)S(1)} %get-tuple-element.96.load_weights, ...), custom_call_target="tpu_custom_call" | custom-call | flops 536870912 | bytes 13123584 | tf_op jit(solution)/shard_map/pallas_call | solution.py:23
  64.7 7.1 %collective-permute-done.9.mine = bf16[2,512,128]{2,1,0:T(8,128)(2,1)S(1)} collective-permute-done((bf16[2,512,128]{2,1,0:T(8,128)(2,1)S(1)}, bf16[2,512,128]{2,1,0:T(8,128)(2,1)S(1)}, u32[]{:S(2)}, u32[]{:S(2)}) %collective-permute-start.9) | collective-permute-done | bytes 262176 | tf_op jit(solution)/shard_map/ppermute | solution.py:287
  71.7 0.9 %collective-permute-start.10 = (bf16[2,512,128]{2,1,0:T(8,128)(2,1)S(1)}, bf16[2,512,128]{2,1,0:T(8,128)(2,1)S(1)}, u32[]{:S(2)}, u32[]{:S(2)}) collective-permute-start(bf16[2,512,128]{2,1,0:T(8,128)(2,1)S(1)} %collective-permute-done.9.mine), channel_id=1, source_target_pairs={{0,1},{1,0},{2,3},{3,2},{4,5},{5,4},{6,7},{7,6},{8,9},{9,8},{10,11... | collective-permute-start | bytes 786440 | tf_op jit(solution)/shard_map/ppermute | solution.py:358
  72.6 0.0 collective-permute-done.11.partner
  72.6 0.8 shard_map.130
  73.4 0.4 collective-permute-done.10.partner
  73.8 1.7 %shard_map.131 = (bf16[512,1024]{1,0:T(8,128)(2,1)}, bf16[512,1024]{1,0:T(8,128)(2,1)}) custom-call(bf16[2,512,128]{2,1,0:T(8,128)(2,1)S(1)} %collective-permute-done.9.mine, bf16[2,512,128]{2,1,0:T(8,128)(2,1)S(1)} %collective-permute-done.10.partner, bf16[1024,1024]{1,0:T(8,128)(2,1)S(1)} %get-tuple-element.96.load_weights, ...), custom_call_target="tpu_custom_call" | custom-call | flops 536870912 | bytes 11026432 | tf_op jit(solution)/shard_map/pallas_call | solution.py:23
Async XLA Ops:
  3.6 6.0 %copy-start = (f32[128,4,128]{2,1,0:T(4,128)S(1)}, f32[128,4,128]{2,1,0:T(4,128)}, u32[]{:S(2)}) copy-start(f32[128,4,128]{2,1,0:T(4,128)} %param.19) | copy-start | bytes 786436
  3.6 6.0 %copy-start.1 = (f32[128,4,128]{2,1,0:T(4,128)S(1)}, f32[128,4,128]{2,1,0:T(4,128)}, u32[]{:S(2)}) copy-start(f32[128,4,128]{2,1,0:T(4,128)} %param.20) | copy-start | bytes 786436
  6.2 4.8 %collective-permute-start = (bf16[4,512,128]{2,1,0:T(8,128)(2,1)S(1)}, bf16[4,512,128]{2,1,0:T(8,128)(2,1)S(1)}, u32[]{:S(2)}, u32[]{:S(2)}) collective-permute-start(bf16[4,512,128]{2,1,0:T(8,128)(2,1)S(1)} %get-tuple-element.77), channel_id=1, source_target_pairs={{0,1},{1,0},{2,3},{3,2},{4,5},{5,4},{6,7},{7,6},{8,9},{9,8},{10,11... | collective-permute-start | bytes 1572872 | tf_op jit(solution)/shard_map/ppermute | solution.py:321
  9.5 2.3 %collective-permute-start.1 = (bf16[4,512,128]{2,1,0:T(8,128)(2,1)S(1)}, bf16[4,512,128]{2,1,0:T(8,128)(2,1)S(1)}, u32[]{:S(2)}, u32[]{:S(2)}) collective-permute-start(bf16[4,512,128]{2,1,0:T(8,128)(2,1)S(1)} %get-tuple-element.78), channel_id=1, source_target_pairs={{0,1},{1,0},{2,3},{3,2},{4,5},{5,4},{6,7},{7,6},{8,9},{9,8},{10,11... | collective-permute-start | bytes 1572872 | tf_op jit(solution)/shard_map/ppermute | solution.py:308
  12.0 9.5 %collective-permute-start.2 = (bf16[2,512,128]{2,1,0:T(8,128)(2,1)S(1)}, bf16[2,512,128]{2,1,0:T(8,128)(2,1)S(1)}, u32[]{:S(2)}, u32[]{:S(2)}) collective-permute-start(bf16[2,512,128]{2,1,0:T(8,128)(2,1)S(1)} %get-tuple-element.80), channel_id=1, source_target_pairs={{0,2},{1,3},{2,4},{3,5},{4,6},{5,7},{6,0},{7,1},{8,10},{9,11},{10,... | collective-permute-start | bytes 786440 | tf_op jit(solution)/shard_map/ppermute | solution.py:287
  12.0 13.6 %collective-permute-start.3 = (bf16[2,512,128]{2,1,0:T(8,128)(2,1)S(1)}, bf16[2,512,128]{2,1,0:T(8,128)(2,1)S(1)}, u32[]{:S(2)}, u32[]{:S(2)}) collective-permute-start(bf16[2,512,128]{2,1,0:T(8,128)(2,1)S(1)} %get-tuple-element.81), channel_id=1, source_target_pairs={{0,4},{1,5},{2,6},{3,7},{4,0},{5,1},{6,2},{7,3},{8,12},{9,13},{10,... | collective-permute-start | bytes 786440 | tf_op jit(solution)/shard_map/ppermute | solution.py:287
  14.0 12.7 %collective-permute-start.4 = (bf16[2,512,128]{2,1,0:T(8,128)(2,1)S(1)}, bf16[2,512,128]{2,1,0:T(8,128)(2,1)S(1)}, u32[]{:S(2)}, u32[]{:S(2)}) collective-permute-start(bf16[2,512,128]{2,1,0:T(8,128)(2,1)S(1)} %get-tuple-element.82), channel_id=1, source_target_pairs={{0,6},{1,7},{2,0},{3,1},{4,2},{5,3},{6,4},{7,5},{8,14},{9,15},{10,... | collective-permute-start | bytes 786440 | tf_op jit(solution)/shard_map/ppermute | solution.py:287
  49.1 6.0 %collective-permute-start.5 = (bf16[2,512,128]{2,1,0:T(8,128)(2,1)S(1)}, bf16[2,512,128]{2,1,0:T(8,128)(2,1)S(1)}, u32[]{:S(2)}, u32[]{:S(2)}) collective-permute-start(bf16[2,512,128]{2,1,0:T(8,128)(2,1)S(1)} %shard_map.127.mine), channel_id=1, source_target_pairs={{0,1},{1,0},{2,3},{3,2},{4,5},{5,4},{6,7},{7,6},{8,9},{9,8},{10,11... | collective-permute-start | bytes 786440 | tf_op jit(solution)/shard_map/ppermute | solution.py:358
  52.4 9.0 %collective-permute-start.6 = (bf16[2,512,128]{2,1,0:T(8,128)(2,1)S(1)}, bf16[2,512,128]{2,1,0:T(8,128)(2,1)S(1)}, u32[]{:S(2)}, u32[]{:S(2)}) collective-permute-start(bf16[2,512,128]{2,1,0:T(8,128)(2,1)S(1)} %shard_map.127.mine), channel_id=1, source_target_pairs={{0,2},{1,3},{2,4},{3,5},{4,6},{5,7},{6,0},{7,1},{8,10},{9,11},{10,... | collective-permute-start | bytes 786440 | tf_op jit(solution)/shard_map/ppermute | solution.py:287
  53.5 10.1 %collective-permute-start.8 = (bf16[2,512,128]{2,1,0:T(8,128)(2,1)S(1)}, bf16[2,512,128]{2,1,0:T(8,128)(2,1)S(1)}, u32[]{:S(2)}, u32[]{:S(2)}) collective-permute-start(bf16[2,512,128]{2,1,0:T(8,128)(2,1)S(1)} %shard_map.127.mine), channel_id=1, source_target_pairs={{0,6},{1,7},{2,0},{3,1},{4,2},{5,3},{6,4},{7,5},{8,14},{9,15},{10,... | collective-permute-start | bytes 786440 | tf_op jit(solution)/shard_map/ppermute | solution.py:287
  61.4 2.4 %collective-permute-start.7 = (bf16[2,512,128]{2,1,0:T(8,128)(2,1)S(1)}, bf16[2,512,128]{2,1,0:T(8,128)(2,1)S(1)}, u32[]{:S(2)}, u32[]{:S(2)}) collective-permute-start(bf16[2,512,128]{2,1,0:T(8,128)(2,1)S(1)} %collective-permute-done.6.mine), channel_id=1, source_target_pairs={{0,1},{1,0},{2,3},{3,2},{4,5},{5,4},{6,7},{7,6},{8,9},{9,8},{10,11... | collective-permute-start | bytes 786440 | tf_op jit(solution)/shard_map/ppermute | solution.py:358
  62.4 9.4 %collective-permute-start.9 = (bf16[2,512,128]{2,1,0:T(8,128)(2,1)S(1)}, bf16[2,512,128]{2,1,0:T(8,128)(2,1)S(1)}, u32[]{:S(2)}, u32[]{:S(2)}) collective-permute-start(bf16[2,512,128]{2,1,0:T(8,128)(2,1)S(1)} %shard_map.127.mine), channel_id=1, source_target_pairs={{0,4},{1,5},{2,6},{3,7},{4,0},{5,1},{6,2},{7,3},{8,12},{9,13},{10,... | collective-permute-start | bytes 786440 | tf_op jit(solution)/shard_map/ppermute | solution.py:287
  63.6 9.0 %collective-permute-start.11 = (bf16[2,512,128]{2,1,0:T(8,128)(2,1)S(1)}, bf16[2,512,128]{2,1,0:T(8,128)(2,1)S(1)}, u32[]{:S(2)}, u32[]{:S(2)}) collective-permute-start(bf16[2,512,128]{2,1,0:T(8,128)(2,1)S(1)} %collective-permute-done.8.mine), channel_id=1, source_target_pairs={{0,1},{1,0},{2,3},{3,2},{4,5},{5,4},{6,7},{7,6},{8,9},{9,8},{10,11... | collective-permute-start | bytes 786440 | tf_op jit(solution)/shard_map/ppermute | solution.py:358
  71.7 2.0 %collective-permute-start.10 = (bf16[2,512,128]{2,1,0:T(8,128)(2,1)S(1)}, bf16[2,512,128]{2,1,0:T(8,128)(2,1)S(1)}, u32[]{:S(2)}, u32[]{:S(2)}) collective-permute-start(bf16[2,512,128]{2,1,0:T(8,128)(2,1)S(1)} %collective-permute-done.9.mine), channel_id=1, source_target_pairs={{0,1},{1,0},{2,3},{3,2},{4,5},{5,4},{6,7},{7,6},{8,9},{9,8},{10,11... | collective-permute-start | bytes 786440 | tf_op jit(solution)/shard_map/ppermute | solution.py:358

commit v4 on v3

--- a/solution.py
+++ b/solution.py
@@ -16,7 +16,7 @@
 NN = (((1,), (0,)), ((), ()))
 
 
-def call(kernel, outs, operands, scratch=(), hbm=0, hbm_out=False, flops=0):
+def call(kernel, outs, operands, scratch=(), hbm=0, hbm_out=False, flops=0, alias=None):
     vmem = pl.BlockSpec(memory_space=pltpu.VMEM)
     far = pl.BlockSpec(memory_space=pltpu.HBM)
     moved = sum(a.size * a.dtype.itemsize for a in (*operands, *outs))
@@ -26,6 +26,7 @@
         in_specs=[vmem] * (len(operands) - hbm) + [far] * hbm,
         out_specs=tuple([far if hbm_out else vmem] * len(outs)),
         scratch_shapes=list(scratch),
+        input_output_aliases=alias or {},
         compiler_params=pltpu.CompilerParams(vmem_limit_bytes=VMEM),
         cost_estimate=pl.CostEstimate(flops=flops, bytes_accessed=moved, transcendentals=0),
     )(*operands[: len(operands) - hbm], *[in_hbm(a) for a in operands[len(operands) - hbm :]])
@@ -56,63 +57,66 @@
 
 
 def pull_kernel(
-    table_far, load_far, cot_far, rows_far, enc_in_far, enc_out_far, gain_far, available_far, readings_far,
-    weights, keep, send, rows_in, enc_in, enc_out, gain, available, readings,
-    pattern, load, cotangent, sems,
+    table_far, load_far, rows_far, enc_in_far, cot_far, enc_out_far, gain_far, available_far, readings_far,
+    weights, keep, send, gain_weights, hidden, enc_out, gain, available, readings,
+    pattern, load, rows_in, enc_in, cotangent, sems,
 ):
     pairs = (
-        (table_far, pattern),
-        (load_far, load), (cot_far, cotangent), (rows_far, rows_in), (enc_in_far, enc_in), (enc_out_far, enc_out),
-        (gain_far, gain), (available_far, available), (readings_far, readings),
+        (table_far, pattern), (load_far, load), (rows_far, rows_in), (enc_in_far, enc_in), (cot_far, cotangent),
+        (enc_out_far, enc_out), (gain_far, gain), (available_far, available), (readings_far, readings),
     )
     copies = [pltpu.make_async_copy(far, near, sems.at[i]) for i, (far, near) in enumerate(pairs)]
-    for copy in copies:
+    for copy in copies[:5]:
         copy.start()
     weights[...] = jnp.zeros_like(weights)
     copies[0].wait()
     copies[1].wait()
+    for copy in copies[5:]:
+        copy.start()
     for q in range(load.shape[0]):
         for k in range(load.shape[1]):
             row = pl.multiple_of(pattern[k, q] * BLK, BLK)
             weights[pl.ds(row, BLK), q * BLK : (q + 1) * BLK] = load[q, k]
     copies[2].wait()
+    copies[3].wait()
+    hidden[...] = jax.nn.gelu(jnp.dot(rows_in[...], enc_in[...], preferred_element_type=F32)).astype(BF16)
+    gain_weights[...] = jnp.zeros_like(gain_weights)
+    copies[4].wait()
     for at in range(keep.shape[0]):
         total = lax.dot_general(cotangent[...], weights[window_of(at), :], NT, preferred_element_type=F32)
         split(keep, send, at, total)
-    for copy in copies[3:]:
+    for copy in copies[5:]:
         copy.wait()
 
 
 def drive_kernel(
-    rows_in, enc_in, enc_out, gain, available, readings, table_far,
+    cleared, hidden, enc_out, gain, available, readings, table_far,
     weights, keep, send, mask,
     lhs, pattern, sem,
 ):
     fetch = pltpu.make_async_copy(table_far, pattern, sem)
     fetch.start()
     traces, blocks, steps = available.shape
-    hidden = jax.nn.gelu(jnp.dot(rows_in[...], enc_in[...], preferred_element_type=F32)).astype(BF16)
-    weights[...] = jnp.zeros_like(weights)
     for b in range(traces):
         mask[b * steps : (b + 1) * steps, :] = available[b].astype(F32).T
+    for q in range(blocks):
+        lhs[:, q * BLK : (q + 1) * BLK] = readings[:, q * BLK : (q + 1) * BLK] * mask[:, q : q + 1].astype(BF16)
     fetch.wait()
     for q in range(blocks):
         for k in range(gain.shape[1]):
             column = pl.multiple_of(pattern[k, q] * BLK, BLK)
             weights[q * BLK : (q + 1) * BLK, pl.ds(column, BLK)] = gain[q, k]
-        lhs[:, q * BLK : (q + 1) * BLK] = readings[:, q * BLK : (q + 1) * BLK] * mask[:, q : q + 1].astype(BF16)
     for at in range(keep.shape[0]):
         total = jnp.dot(lhs[...], weights[:, window_of(at)], preferred_element_type=F32)
-        total += jnp.dot(hidden, enc_out[:, window_of(at)], preferred_element_type=F32)
+        total += jnp.dot(hidden[...], enc_out[:, window_of(at)], preferred_element_type=F32)
         split(keep, send, at, total)
 
 
-def merge_kernel(keep_a, keep_b, came_a, came_b, own, *pieces):
+def merge_kernel(keep, came, own, *pieces):
     x, _ = here()
-    for which, (keep, came) in enumerate(((keep_a, came_a), (keep_b, came_b))):
-        for k, piece in enumerate((own, *pieces)):
-            at = lax.rem(x + k, keep.shape[0])
-            piece[which] = (keep[at] + came[at].astype(F32)).astype(piece.dtype)
+    for k, piece in enumerate((own, *pieces)):
+        at = lax.rem(x + k, keep.shape[0])
+        piece[...] = (keep[at] + came[at].astype(F32)).astype(piece.dtype)
 
 
 def rows_of(b, u, steps):
@@ -163,13 +167,12 @@
 
 def scan_kernel(
     traces, steps,
-    own, one, two, three, keep_r, keep_s, root, seg_r, seg_s,
+    own_a, own_b, a1, a2, a3, b1, b2, b3, keep_r, keep_s, root, seg_r, seg_s,
     states, grads, before, parcel,
     source, pull, ends,
 ):
-    pieces = (one, two, three)
-    source[...] = root[...] * (own[0] + sum(piece[0].astype(F32) for piece in pieces))
-    pull[...] = own[1] + sum(piece[1].astype(F32) for piece in pieces)
+    source[...] = root[...] * (own_a[...] + a1[...].astype(F32) + a2[...].astype(F32) + a3[...].astype(F32))
+    pull[...] = own_b[...] + b1[...].astype(F32) + b2[...].astype(F32) + b3[...].astype(F32)
     for b in range(traces):
         filt = jnp.zeros((SEG, BLK), F32)
         rise, ahead, fall = filt, filt, filt
@@ -287,20 +290,19 @@
         moved = {k: lax.ppermute(pieces[k - 1], "state", [(i, (i + 2 * k) % axis) for i in range(axis)]) for k in (1, 3, 2)}
         return [moved[k] for k in (1, 2, 3)]
 
-    near = (
-        inputs.reshape(rows, features), encoder_in, encoder_out, gain, available.transpose(0, 2, 1),
-        readings.reshape(rows, sensors),
-    )
-    pulled_from = (load, cotangent.reshape(rows, sensors))
+    fetched = (encoder_out, gain, available.transpose(0, 2, 1), readings.reshape(rows, sensors))
+    staged = (load, inputs.reshape(rows, features), encoder_in, cotangent.reshape(rows, sensors))
     table = pattern.T
-    chips = axis // 2
-    parts = (struct((chips, rows, BLK), F32), struct((chips, rows, BLK), BF16))
-    load_weights, keep_b, send_b, *near = call(
+    parts = (struct((axis // 2, rows, BLK), F32), struct((axis // 2, rows, BLK), BF16))
+    load_weights, keep_b, send_b, cleared, hidden, *fetched = call(
         pull_kernel,
-        (struct((states, sensors), BF16), *parts, *(struct(a.shape, a.dtype) for a in near)),
-        (table, *pulled_from, *near),
+        (
+            struct((states, sensors), BF16), *parts, struct((sensors, states), BF16),
+            struct((rows, encoder_in.shape[1]), BF16), *(struct(a.shape, a.dtype) for a in fetched),
+        ),
+        (table, *staged, *fetched),
         scratch=[pltpu.SMEM(table.shape, table.dtype)]
-        + [pltpu.VMEM(a.shape, a.dtype) for a in pulled_from]
+        + [pltpu.VMEM(a.shape, a.dtype) for a in staged]
         + [pltpu.SemaphoreType.DMA((9,))],
         hbm=9,
         flops=work,
@@ -309,7 +311,7 @@
     gain_weights, keep_a, send_a, mask = call(
         drive_kernel,
         (struct((sensors, states), BF16), *parts, struct((rows, blocks), F32)),
-        (*near, table),
+        (cleared, hidden, *fetched, table),
         scratch=[
             pltpu.VMEM((rows, sensors), BF16),
             pltpu.SMEM(table.shape, table.dtype),
@@ -317,26 +319,26 @@
         ],
         hbm=1,
         flops=work,
+        alias={0: 0},
     )
     came_a = lax.ppermute(send_a, "state", swap)
+    piece = struct((rows, BLK), BF16)
+    pieces = (struct((rows, BLK), F32),) + (piece,) * 3
+    own_b, *sums_b = call(merge_kernel, pieces, (keep_b, came_b))
+    sums_b = across(sums_b)
+    keep_a, own_b = lax.optimization_barrier((keep_a, own_b))
+    own_a, *sums_a = call(merge_kernel, pieces, (keep_a, came_a))
+    sums_a = across(sums_a)
     full, segments = struct((rows, BLK), F32), struct((traces, SEG, BLK), F32)
     keep_r, keep_s, root, ahead_p, filt_p, rise_p, fall_p, seg_r, seg_s = call(
         functools.partial(decay_kernel, traces, steps),
         (full,) * 7 + (segments,) * 2,
         (retain.reshape(-1, steps), smooth.reshape(-1, steps)),
     )
-    decays = (keep_r, keep_s, root, ahead_p, filt_p, rise_p, fall_p, seg_r, seg_s)
-    keep_a, decays = lax.optimization_barrier((keep_a, decays))
-    keep_r, keep_s, root, ahead_p, filt_p, rise_p, fall_p, seg_r, seg_s = decays
-    both = struct((2, rows, BLK), BF16)
-    own, *sums = call(
-        merge_kernel, (struct(both.shape, F32),) + (both,) * 3, (keep_a, keep_b, came_a, came_b)
-    )
-    sums = across(sums)
     scanned, pulled, before, parcel = call(
         functools.partial(scan_kernel, traces, steps),
         (full, full, struct((4, traces, 2, SEG, BLK), F32), struct((times, 2 * SEG, BLK), F32)),
-        (own, *sums, keep_r, keep_s, root, seg_r, seg_s),
+        (own_a, own_b, *sums_a, *sums_b, keep_r, keep_s, root, seg_r, seg_s),
         scratch=[pltpu.VMEM((rows, BLK), F32)] * 2 + [pltpu.VMEM((2, 2, SEG, BLK), F32)],
     )
     parcel = lax.all_to_all(parcel, "tm", 0, 0)

time: 75.8 us -> 75.9 us (level)
  waiting for transfers between devices: 26.2 us -> 24.1 us
  starting transfers between devices: 15.9 us -> 17.3 us
    ppermute x1, starting transfers between devices: 3.31 us -> 0.11 us  [local(): came_a = lax.ppermute(send_a, 'state', swap)]
    ppermute x1, starting transfers between devices: 0.1 us -> 3.29 us  [local(): came_b = lax.ppermute(send_b, 'state', swap)]
    ppermute x6 -> x9, waiting for transfers between devices: 24.2 us -> 22 us  [across(): lax.ppermute(pieces[k - 1], 'state', [(i, (i + 2 * k) % axis) for i in ra...]
    ppermute x6 -> x9, starting transfers between devices: 7.12 us -> 8.97 us  [across(): lax.ppermute(pieces[k - 1], 'state', [(i, (i + 2 * k) % axis) for i in ra...]
    ppermute x1, waiting for transfers between devices: 0.85 us -> 1.78 us  [local(): came_a = lax.ppermute(send_a, 'state', swap)]
    pallas_call x10 -> x11, Pallas kernels: 12.1 us -> 12.4 us  [call(): pl.pallas_call(kernel, out_shape=outs, in_specs=[vmem] * (len(operands) -...]
  transfers between devices with their start and end apart: 12 -> 15, of which waited for: 8 -> 9; matrix products, arithmetic and copies ran while one was open for 0% -> 0% of each run, Pallas kernels for 4% -> 7%
where the time goes in v4:
time: 75.9 us; the launch traced here: 75.8 us
  waiting for transfers between devices  24.1 us (32%)
  blocking collectives  20.9 us (28%)
  starting transfers between devices  17.3 us (23%)
  Pallas kernels  12.4 us (16%)
  between operations  0.91 us (1%)
    ppermute x9, waiting for transfers between devices, across(): lax.ppermute(pieces[k - 1], 'state', [(i, (i + 2 * k) % axis) for i in ra...  22 us
    all_to_all x1, blocking collectives, local(): parcel = lax.all_to_all(parcel, 'tm', 0, 0)  20.9 us
    pallas_call x11, Pallas kernels, call(): pl.pallas_call(kernel, out_shape=outs, in_specs=[vmem] * (len(operands) -...  12.4 us
    ppermute x9, starting transfers between devices, across(): lax.ppermute(pieces[k - 1], 'state', [(i, (i + 2 * k) % axis) for i in ra...  8.97 us
    ppermute x4, starting transfers between devices, local(): partner = lax.ppermute(same[shift], 'state', swap)  4.98 us
    ppermute x1, starting transfers between devices, local(): came_b = lax.ppermute(send_b, 'state', swap)  3.29 us
    ppermute x1, waiting for transfers between devices, local(): came_a = lax.ppermute(send_a, 'state', swap)  1.78 us
  transfers between devices with their start and end apart: 15, of which 9 were waited for; matrix products, arithmetic and copies ran while one was open for 0% of the time, Pallas kernels for 7%

profile of v4, /device:TPU:1, one launch (start us, length us, event | category | flops | bytes accessed | tf_op | source)
XLA Modules:
  0.0 75.8 jit_solution(11893015150802671398)
XLA Ops:
  0.6 3.4 %shard_map.122 = (bf16[1024,1024]{1,0:T(8,128)(2,1)S(1)}, f32[4,512,128]{2,1,0:T(8,128)S(1)}, bf16[4,512,128]{2,1,0:T(8,128)(2,1)S(1)}, bf16[1024,1024]{1,0:T(8,...) custom-call(s32[4,8]{1,0:T(4,128)} %bitcast.15, ...), custom_call_target="tpu_custom_call" | custom-call | flops 1073741824 | bytes 13795456 | tf_op jit(solution)/shard_map/pallas_call | solution.py:23
  4.0 3.3 %collective-permute-start = (bf16[4,512,128]{2,1,0:T(8,128)(2,1)S(1)}, bf16[4,512,128]{2,1,0:T(8,128)(2,1)S(1)}, u32[]{:S(2)}, u32[]{:S(2)}) collective-permute-start(bf16[4,512,128]{2,1,0:T(8,128)(2,1)S(1)} %get-tuple-element.63), channel_id=1, source_target_pairs={{0,1},{1,0},{2,3},{3,2},{4,5},{5,4},{6,7},{7,6},{8,9},{9,8},{10,11... | collective-permute-start | bytes 1572872 | tf_op jit(solution)/shard_map/ppermute | solution.py:310
  7.3 2.4 %shard_map.123 = (bf16[1024,1024]{1,0:T(8,128)(2,1)S(1)}, f32[4,512,128]{2,1,0:T(8,128)S(1)}, bf16[4,512,128]{2,1,0:T(8,128)(2,1)S(1)}, f32[512,8]{1,0:T(8,128)S(1)}) custom-call(bf16[1024,1024]{1,0:T(8,128)(2,1)S(1)} %get-tuple-element.55.cleared, bf16[512,256]{1,0:T(8,128)(2,1)S(1)} %get-tuple-element.56.hidden, ...), custom_call_target="tpu_custom_call", output_to_operand_aliasing={{0}: (0, {})} | custom-call | flops 1073741824 | bytes 8683648 | tf_op jit(solution)/shard_map/pallas_call | solution.py:23
  9.8 0.0 copy-start
  9.8 0.0 copy-start.1
  9.8 0.1 collective-permute-start.1
  9.9 0.0 collective-permute-done.came
  9.9 0.1 shard_map.124
  10.0 1.8 %collective-permute-done.1.came = bf16[4,512,128]{2,1,0:T(8,128)(2,1)S(1)} collective-permute-done((bf16[4,512,128]{2,1,0:T(8,128)(2,1)S(1)}, bf16[4,512,128]{2,1,0:T(8,128)(2,1)S(1)}, u32[]{:S(2)}, u32[]{:S(2)}) %collective-permute-start.1) | collective-permute-done | bytes 524320 | tf_op jit(solution)/shard_map/ppermute | solution.py:324
  11.8 0.1 shard_map.125
  11.9 0.1 collective-permute-start.2
  12.0 1.9 %collective-permute-start.3 = (bf16[512,128]{1,0:T(8,128)(2,1)S(1)}, bf16[512,128]{1,0:T(8,128)(2,1)S(1)}, u32[]{:S(2)}, u32[]{:S(2)}) collective-permute-start(bf16[512,128]{1,0:T(8,128)(2,1)S(1)} %get-tuple-element.70), channel_id=1, source_target_pairs={{0,4},{1,5},{2,6},{3,7},{4,0},{5,1},{6,2},{7,3},{8,12},{9,13},{10,... | collective-permute-start | bytes 393224 | tf_op jit(solution)/shard_map/ppermute | solution.py:290
  13.9 1.1 %collective-permute-start.4 = (bf16[512,128]{1,0:T(8,128)(2,1)S(1)}, bf16[512,128]{1,0:T(8,128)(2,1)S(1)}, u32[]{:S(2)}, u32[]{:S(2)}) collective-permute-start(bf16[512,128]{1,0:T(8,128)(2,1)S(1)} %get-tuple-element.71), channel_id=1, source_target_pairs={{0,6},{1,7},{2,0},{3,1},{4,2},{5,3},{6,4},{7,5},{8,14},{9,15},{10,... | collective-permute-start | bytes 393224 | tf_op jit(solution)/shard_map/ppermute | solution.py:290
  15.1 0.3 collective-permute-start.5
  15.4 1.6 %collective-permute-start.6 = (bf16[512,128]{1,0:T(8,128)(2,1)S(1)}, bf16[512,128]{1,0:T(8,128)(2,1)S(1)}, u32[]{:S(2)}, u32[]{:S(2)}) collective-permute-start(bf16[512,128]{1,0:T(8,128)(2,1)S(1)} %get-tuple-element.73), channel_id=1, source_target_pairs={{0,4},{1,5},{2,6},{3,7},{4,0},{5,1},{6,2},{7,3},{8,12},{9,13},{10,... | collective-permute-start | bytes 393224 | tf_op jit(solution)/shard_map/ppermute | solution.py:290
  17.0 3.4 %collective-permute-done.2.a1 = bf16[512,128]{1,0:T(8,128)(2,1)S(1)} collective-permute-done((bf16[512,128]{1,0:T(8,128)(2,1)S(1)}, bf16[512,128]{1,0:T(8,128)(2,1)S(1)}, u32[]{:S(2)}, u32[]{:S(2)}) %collective-permute-start.2) | collective-permute-done | bytes 131104 | tf_op jit(solution)/shard_map/ppermute | solution.py:290
  20.4 0.0 collective-permute-start.7
  20.4 0.0 copy-done
  20.4 0.0 copy-done.1
  20.4 0.6 shard_map.126
  21.0 0.0 collective-permute-done.3.a2
  21.0 0.2 collective-permute-done.4.a3
  21.2 3.1 %collective-permute-done.5.b1 = bf16[512,128]{1,0:T(8,128)(2,1)S(1)} collective-permute-done((bf16[512,128]{1,0:T(8,128)(2,1)S(1)}, bf16[512,128]{1,0:T(8,128)(2,1)S(1)}, u32[]{:S(2)}, u32[]{:S(2)}) %collective-permute-start.5) | collective-permute-done | bytes 131104 | tf_op jit(solution)/shard_map/ppermute | solution.py:290
  24.3 1.6 %collective-permute-done.6.b2 = bf16[512,128]{1,0:T(8,128)(2,1)S(1)} collective-permute-done((bf16[512,128]{1,0:T(8,128)(2,1)S(1)}, bf16[512,128]{1,0:T(8,128)(2,1)S(1)}, u32[]{:S(2)}, u32[]{:S(2)}) %collective-permute-start.6) | collective-permute-done | bytes 131104 | tf_op jit(solution)/shard_map/ppermute | solution.py:290
  25.9 1.0 %collective-permute-done.7.b3 = bf16[512,128]{1,0:T(8,128)(2,1)S(1)} collective-permute-done((bf16[512,128]{1,0:T(8,128)(2,1)S(1)}, bf16[512,128]{1,0:T(8,128)(2,1)S(1)}, u32[]{:S(2)}, u32[]{:S(2)}) %collective-permute-start.7) | collective-permute-done | bytes 131104 | tf_op jit(solution)/shard_map/ppermute | solution.py:290
  26.9 1.1 %shard_map.127 = (f32[512,128]{1,0:T(8,128)S(1)}, f32[512,128]{1,0:T(8,128)S(1)}, f32[4,4,2,8,128]{4,3,2,1,0:T(8,128)S(1)}, f32[32,16,128]{2,1,0:T(8,128)S(1)}) custom-call(f32[512,128]{1,0:T(8,128)S(1)} %get-tuple-element.67.own_a, f32[512,128]{1,0:T(8,128)S(1)} %get-tuple-element.68.own_b, bf16[512,128]{1,0:T(8,128)(2,1)S(1)} %collective-permute-done.2.a1, ...), custom_call_target="tpu_custom_call" | custom-call | bytes 3047424 | tf_op jit(solution)/shard_map/pallas_call | solution.py:23
  28.0 20.9 %all_to_all.5.parcel = f32[32,16,128]{2,1,0:T(8,128)S(1)} all-to-all(f32[32,16,128]{2,1,0:T(8,128)S(1)} %get-tuple-element.80), channel_id=1, replica_groups=mesh['tm'=32,'state'=8] {'tm'}, dimensions={0} | all-to-all | bytes 524288 | tf_op jit(solution)/shard_map/all_to_all | solution.py:344
  48.9 0.7 shard_map.128.mine
  49.6 2.9 %collective-permute-start.8 = (bf16[2,512,128]{2,1,0:T(8,128)(2,1)S(1)}, bf16[2,512,128]{2,1,0:T(8,128)(2,1)S(1)}, u32[]{:S(2)}, u32[]{:S(2)}) collective-permute-start(bf16[2,512,128]{2,1,0:T(8,128)(2,1)S(1)} %shard_map.128.mine), channel_id=1, source_target_pairs={{0,1},{1,0},{2,3},{3,2},{4,5},{5,4},{6,7},{7,6},{8,9},{9,8},{10,11... | collective-permute-start | bytes 786440 | tf_op jit(solution)/shard_map/ppermute | solution.py:360
  52.5 1.0 %collective-permute-start.9 = (bf16[2,512,128]{2,1,0:T(8,128)(2,1)S(1)}, bf16[2,512,128]{2,1,0:T(8,128)(2,1)S(1)}, u32[]{:S(2)}, u32[]{:S(2)}) collective-permute-start(bf16[2,512,128]{2,1,0:T(8,128)(2,1)S(1)} %shard_map.128.mine), channel_id=1, source_target_pairs={{0,2},{1,3},{2,4},{3,5},{4,6},{5,7},{6,0},{7,1},{8,10},{9,11},{10,... | collective-permute-start | bytes 786440 | tf_op jit(solution)/shard_map/ppermute | solution.py:290
  53.6 1.7 %collective-permute-start.11 = (bf16[2,512,128]{2,1,0:T(8,128)(2,1)S(1)}, bf16[2,512,128]{2,1,0:T(8,128)(2,1)S(1)}, u32[]{:S(2)}, u32[]{:S(2)}) collective-permute-start(bf16[2,512,128]{2,1,0:T(8,128)(2,1)S(1)} %shard_map.128.mine), channel_id=1, source_target_pairs={{0,6},{1,7},{2,0},{3,1},{4,2},{5,3},{6,4},{7,5},{8,14},{9,15},{10,... | collective-permute-start | bytes 786440 | tf_op jit(solution)/shard_map/ppermute | solution.py:290
  55.2 0.0 collective-permute-done.8.partner
  55.2 0.7 shard_map.129
  56.0 5.6 %collective-permute-done.9.mine = bf16[2,512,128]{2,1,0:T(8,128)(2,1)S(1)} collective-permute-done((bf16[2,512,128]{2,1,0:T(8,128)(2,1)S(1)}, bf16[2,512,128]{2,1,0:T(8,128)(2,1)S(1)}, u32[]{:S(2)}, u32[]{:S(2)}) %collective-permute-start.9) | collective-permute-done | bytes 262176 | tf_op jit(solution)/shard_map/ppermute | solution.py:290
  61.5 0.9 %collective-permute-start.10 = (bf16[2,512,128]{2,1,0:T(8,128)(2,1)S(1)}, bf16[2,512,128]{2,1,0:T(8,128)(2,1)S(1)}, u32[]{:S(2)}, u32[]{:S(2)}) collective-permute-start(bf16[2,512,128]{2,1,0:T(8,128)(2,1)S(1)} %collective-permute-done.9.mine), channel_id=1, source_target_pairs={{0,1},{1,0},{2,3},{3,2},{4,5},{5,4},{6,7},{7,6},{8,9},{9,8},{10,11... | collective-permute-start | bytes 786440 | tf_op jit(solution)/shard_map/ppermute | solution.py:360
  62.5 1.2 %collective-permute-start.12 = (bf16[2,512,128]{2,1,0:T(8,128)(2,1)S(1)}, bf16[2,512,128]{2,1,0:T(8,128)(2,1)S(1)}, u32[]{:S(2)}, u32[]{:S(2)}) collective-permute-start(bf16[2,512,128]{2,1,0:T(8,128)(2,1)S(1)} %shard_map.128.mine), channel_id=1, source_target_pairs={{0,4},{1,5},{2,6},{3,7},{4,0},{5,1},{6,2},{7,3},{8,12},{9,13},{10,... | collective-permute-start | bytes 786440 | tf_op jit(solution)/shard_map/ppermute | solution.py:290
  63.6 0.0 collective-permute-done.11.mine
  63.6 0.3 collective-permute-start.14
  63.9 0.0 collective-permute-done.10.partner
  63.9 0.8 %shard_map.130 = (f32[512,1024]{1,0:T(8,128)S(1)}, f32[512,1024]{1,0:T(8,128)S(1)}) custom-call(bf16[2,512,128]{2,1,0:T(8,128)(2,1)S(1)} %collective-permute-done.9.mine, bf16[2,512,128]{2,1,0:T(8,128)(2,1)S(1)} %collective-permute-done.10.partner, bf16[1024,1024]{1,0:T(8,128)(2,1)S(1)} %get-tuple-element.88.load_weights, ...), custom_call_target="tpu_custom_call" | custom-call | flops 536870912 | bytes 13123584 | tf_op jit(solution)/shard_map/pallas_call | solution.py:23
  64.7 7.1 %collective-permute-done.12.mine = bf16[2,512,128]{2,1,0:T(8,128)(2,1)S(1)} collective-permute-done((bf16[2,512,128]{2,1,0:T(8,128)(2,1)S(1)}, bf16[2,512,128]{2,1,0:T(8,128)(2,1)S(1)}, u32[]{:S(2)}, u32[]{:S(2)}) %collective-permute-start.12) | collective-permute-done | bytes 262176 | tf_op jit(solution)/shard_map/ppermute | solution.py:290
  71.8 0.9 %collective-permute-start.13 = (bf16[2,512,128]{2,1,0:T(8,128)(2,1)S(1)}, bf16[2,512,128]{2,1,0:T(8,128)(2,1)S(1)}, u32[]{:S(2)}, u32[]{:S(2)}) collective-permute-start(bf16[2,512,128]{2,1,0:T(8,128)(2,1)S(1)} %collective-permute-done.12.mine), channel_id=1, source_target_pairs={{0,1},{1,0},{2,3},{3,2},{4,5},{5,4},{6,7},{7,6},{8,9},{9,8},{10,11... | collective-permute-start | bytes 786440 | tf_op jit(solution)/shard_map/ppermute | solution.py:360
  72.7 0.0 collective-permute-done.14.partner
  72.7 0.8 shard_map.131
  73.5 0.4 collective-permute-done.13.partner
  73.9 1.8 %shard_map.132 = (bf16[512,1024]{1,0:T(8,128)(2,1)}, bf16[512,1024]{1,0:T(8,128)(2,1)}) custom-call(bf16[2,512,128]{2,1,0:T(8,128)(2,1)S(1)} %collective-permute-done.12.mine, bf16[2,512,128]{2,1,0:T(8,128)(2,1)S(1)} %collective-permute-done.13.partner, bf16[1024,1024]{1,0:T(8,128)(2,1)S(1)} %get-tuple-element.88.load_weights, ...), custom_call_target="tpu_custom_call" | custom-call | flops 536870912 | bytes 11026432 | tf_op jit(solution)/shard_map/pallas_call | solution.py:23
Async XLA Ops:
  4.0 5.9 %collective-permute-start = (bf16[4,512,128]{2,1,0:T(8,128)(2,1)S(1)}, bf16[4,512,128]{2,1,0:T(8,128)(2,1)S(1)}, u32[]{:S(2)}, u32[]{:S(2)}) collective-permute-start(bf16[4,512,128]{2,1,0:T(8,128)(2,1)S(1)} %get-tuple-element.63), channel_id=1, source_target_pairs={{0,1},{1,0},{2,3},{3,2},{4,5},{5,4},{6,7},{7,6},{8,9},{9,8},{10,11... | collective-permute-start | bytes 1572872 | tf_op jit(solution)/shard_map/ppermute | solution.py:310
  9.8 10.6 %copy-start = (f32[128,4,128]{2,1,0:T(4,128)S(1)}, f32[128,4,128]{2,1,0:T(4,128)}, u32[]{:S(2)}) copy-start(f32[128,4,128]{2,1,0:T(4,128)} %param.19) | copy-start | bytes 786436
  9.8 10.6 %copy-start.1 = (f32[128,4,128]{2,1,0:T(4,128)S(1)}, f32[128,4,128]{2,1,0:T(4,128)}, u32[]{:S(2)}) copy-start(f32[128,4,128]{2,1,0:T(4,128)} %param.20) | copy-start | bytes 786436
  9.8 2.0 %collective-permute-start.1 = (bf16[4,512,128]{2,1,0:T(8,128)(2,1)S(1)}, bf16[4,512,128]{2,1,0:T(8,128)(2,1)S(1)}, u32[]{:S(2)}, u32[]{:S(2)}) collective-permute-start(bf16[4,512,128]{2,1,0:T(8,128)(2,1)S(1)} %get-tuple-element.66), channel_id=1, source_target_pairs={{0,1},{1,0},{2,3},{3,2},{4,5},{5,4},{6,7},{7,6},{8,9},{9,8},{10,11... | collective-permute-start | bytes 1572872 | tf_op jit(solution)/shard_map/ppermute | solution.py:324
  11.9 8.5 %collective-permute-start.2 = (bf16[512,128]{1,0:T(8,128)(2,1)S(1)}, bf16[512,128]{1,0:T(8,128)(2,1)S(1)}, u32[]{:S(2)}, u32[]{:S(2)}) collective-permute-start(bf16[512,128]{1,0:T(8,128)(2,1)S(1)} %get-tuple-element.69), channel_id=1, source_target_pairs={{0,2},{1,3},{2,4},{3,5},{4,6},{5,7},{6,0},{7,1},{8,10},{9,11},{10,... | collective-permute-start | bytes 393224 | tf_op jit(solution)/shard_map/ppermute | solution.py:290
  12.0 9.0 %collective-permute-start.3 = (bf16[512,128]{1,0:T(8,128)(2,1)S(1)}, bf16[512,128]{1,0:T(8,128)(2,1)S(1)}, u32[]{:S(2)}, u32[]{:S(2)}) collective-permute-start(bf16[512,128]{1,0:T(8,128)(2,1)S(1)} %get-tuple-element.70), channel_id=1, source_target_pairs={{0,4},{1,5},{2,6},{3,7},{4,0},{5,1},{6,2},{7,3},{8,12},{9,13},{10,... | collective-permute-start | bytes 393224 | tf_op jit(solution)/shard_map/ppermute | solution.py:290
  13.9 7.3 %collective-permute-start.4 = (bf16[512,128]{1,0:T(8,128)(2,1)S(1)}, bf16[512,128]{1,0:T(8,128)(2,1)S(1)}, u32[]{:S(2)}, u32[]{:S(2)}) collective-permute-start(bf16[512,128]{1,0:T(8,128)(2,1)S(1)} %get-tuple-element.71), channel_id=1, source_target_pairs={{0,6},{1,7},{2,0},{3,1},{4,2},{5,3},{6,4},{7,5},{8,14},{9,15},{10,... | collective-permute-start | bytes 393224 | tf_op jit(solution)/shard_map/ppermute | solution.py:290
  15.1 9.2 %collective-permute-start.5 = (bf16[512,128]{1,0:T(8,128)(2,1)S(1)}, bf16[512,128]{1,0:T(8,128)(2,1)S(1)}, u32[]{:S(2)}, u32[]{:S(2)}) collective-permute-start(bf16[512,128]{1,0:T(8,128)(2,1)S(1)} %get-tuple-element.72), channel_id=1, source_target_pairs={{0,2},{1,3},{2,4},{3,5},{4,6},{5,7},{6,0},{7,1},{8,10},{9,11},{10,... | collective-permute-start | bytes 393224 | tf_op jit(solution)/shard_map/ppermute | solution.py:290
  15.4 10.5 %collective-permute-start.6 = (bf16[512,128]{1,0:T(8,128)(2,1)S(1)}, bf16[512,128]{1,0:T(8,128)(2,1)S(1)}, u32[]{:S(2)}, u32[]{:S(2)}) collective-permute-start(bf16[512,128]{1,0:T(8,128)(2,1)S(1)} %get-tuple-element.73), channel_id=1, source_target_pairs={{0,4},{1,5},{2,6},{3,7},{4,0},{5,1},{6,2},{7,3},{8,12},{9,13},{10,... | collective-permute-start | bytes 393224 | tf_op jit(solution)/shard_map/ppermute | solution.py:290
  20.4 6.5 %collective-permute-start.7 = (bf16[512,128]{1,0:T(8,128)(2,1)S(1)}, bf16[512,128]{1,0:T(8,128)(2,1)S(1)}, u32[]{:S(2)}, u32[]{:S(2)}) collective-permute-start(bf16[512,128]{1,0:T(8,128)(2,1)S(1)} %get-tuple-element.74), channel_id=1, source_target_pairs={{0,6},{1,7},{2,0},{3,1},{4,2},{5,3},{6,4},{7,5},{8,14},{9,15},{10,... | collective-permute-start | bytes 393224 | tf_op jit(solution)/shard_map/ppermute | solution.py:290
  49.6 5.6 %collective-permute-start.8 = (bf16[2,512,128]{2,1,0:T(8,128)(2,1)S(1)}, bf16[2,512,128]{2,1,0:T(8,128)(2,1)S(1)}, u32[]{:S(2)}, u32[]{:S(2)}) collective-permute-start(bf16[2,512,128]{2,1,0:T(8,128)(2,1)S(1)} %shard_map.128.mine), channel_id=1, source_target_pairs={{0,1},{1,0},{2,3},{3,2},{4,5},{5,4},{6,7},{7,6},{8,9},{9,8},{10,11... | collective-permute-start | bytes 786440 | tf_op jit(solution)/shard_map/ppermute | solution.py:360
  52.5 9.0 %collective-permute-start.9 = (bf16[2,512,128]{2,1,0:T(8,128)(2,1)S(1)}, bf16[2,512,128]{2,1,0:T(8,128)(2,1)S(1)}, u32[]{:S(2)}, u32[]{:S(2)}) collective-permute-start(bf16[2,512,128]{2,1,0:T(8,128)(2,1)S(1)} %shard_map.128.mine), channel_id=1, source_target_pairs={{0,2},{1,3},{2,4},{3,5},{4,6},{5,7},{6,0},{7,1},{8,10},{9,11},{10,... | collective-permute-start | bytes 786440 | tf_op jit(solution)/shard_map/ppermute | solution.py:290
  53.6 10.1 %collective-permute-start.11 = (bf16[2,512,128]{2,1,0:T(8,128)(2,1)S(1)}, bf16[2,512,128]{2,1,0:T(8,128)(2,1)S(1)}, u32[]{:S(2)}, u32[]{:S(2)}) collective-permute-start(bf16[2,512,128]{2,1,0:T(8,128)(2,1)S(1)} %shard_map.128.mine), channel_id=1, source_target_pairs={{0,6},{1,7},{2,0},{3,1},{4,2},{5,3},{6,4},{7,5},{8,14},{9,15},{10,... | collective-permute-start | bytes 786440 | tf_op jit(solution)/shard_map/ppermute | solution.py:290
  61.5 2.4 %collective-permute-start.10 = (bf16[2,512,128]{2,1,0:T(8,128)(2,1)S(1)}, bf16[2,512,128]{2,1,0:T(8,128)(2,1)S(1)}, u32[]{:S(2)}, u32[]{:S(2)}) collective-permute-start(bf16[2,512,128]{2,1,0:T(8,128)(2,1)S(1)} %collective-permute-done.9.mine), channel_id=1, source_target_pairs={{0,1},{1,0},{2,3},{3,2},{4,5},{5,4},{6,7},{7,6},{8,9},{9,8},{10,11... | collective-permute-start | bytes 786440 | tf_op jit(solution)/shard_map/ppermute | solution.py:360
  62.5 9.4 %collective-permute-start.12 = (bf16[2,512,128]{2,1,0:T(8,128)(2,1)S(1)}, bf16[2,512,128]{2,1,0:T(8,128)(2,1)S(1)}, u32[]{:S(2)}, u32[]{:S(2)}) collective-permute-start(bf16[2,512,128]{2,1,0:T(8,128)(2,1)S(1)} %shard_map.128.mine), channel_id=1, source_target_pairs={{0,4},{1,5},{2,6},{3,7},{4,0},{5,1},{6,2},{7,3},{8,12},{9,13},{10,... | collective-permute-start | bytes 786440 | tf_op jit(solution)/shard_map/ppermute | solution.py:290
  63.6 9.0 %collective-permute-start.14 = (bf16[2,512,128]{2,1,0:T(8,128)(2,1)S(1)}, bf16[2,512,128]{2,1,0:T(8,128)(2,1)S(1)}, u32[]{:S(2)}, u32[]{:S(2)}) collective-permute-start(bf16[2,512,128]{2,1,0:T(8,128)(2,1)S(1)} %collective-permute-done.11.mine), channel_id=1, source_target_pairs={{0,1},{1,0},{2,3},{3,2},{4,5},{5,4},{6,7},{7,6},{8,9},{9,8},{10,11... | collective-permute-start | bytes 786440 | tf_op jit(solution)/shard_map/ppermute | solution.py:360
  71.8 2.0 %collective-permute-start.13 = (bf16[2,512,128]{2,1,0:T(8,128)(2,1)S(1)}, bf16[2,512,128]{2,1,0:T(8,128)(2,1)S(1)}, u32[]{:S(2)}, u32[]{:S(2)}) collective-permute-start(bf16[2,512,128]{2,1,0:T(8,128)(2,1)S(1)} %collective-permute-done.12.mine), channel_id=1, source_target_pairs={{0,1},{1,0},{2,3},{3,2},{4,5},{5,4},{6,7},{7,6},{8,9},{9,8},{10,11... | collective-permute-start | bytes 786440 | tf_op jit(solution)/shard_map/ppermute | solution.py:360

commit v5 on v4

--- a/solution.py
+++ b/solution.py
@@ -57,46 +57,44 @@
 
 
 def pull_kernel(
-    table_far, load_far, rows_far, enc_in_far, cot_far, enc_out_far, gain_far, available_far, readings_far,
-    weights, keep, send, gain_weights, hidden, enc_out, gain, available, readings,
-    pattern, load, rows_in, enc_in, cotangent, sems,
+    table_far, load_far, cot_far, rows_far, enc_in_far, enc_out_far, gain_far, available_far, readings_far,
+    weights, keep, send, gain_weights, rows_in, enc_in, enc_out, gain, available, readings,
+    pattern, load, cotangent, sems,
 ):
     pairs = (
-        (table_far, pattern), (load_far, load), (rows_far, rows_in), (enc_in_far, enc_in), (cot_far, cotangent),
+        (table_far, pattern), (load_far, load), (cot_far, cotangent), (rows_far, rows_in), (enc_in_far, enc_in),
         (enc_out_far, enc_out), (gain_far, gain), (available_far, available), (readings_far, readings),
     )
     copies = [pltpu.make_async_copy(far, near, sems.at[i]) for i, (far, near) in enumerate(pairs)]
-    for copy in copies[:5]:
+    for copy in copies[:3]:
         copy.start()
     weights[...] = jnp.zeros_like(weights)
+    gain_weights[...] = jnp.zeros_like(gain_weights)
     copies[0].wait()
     copies[1].wait()
-    for copy in copies[5:]:
+    for copy in copies[3:]:
         copy.start()
     for q in range(load.shape[0]):
         for k in range(load.shape[1]):
             row = pl.multiple_of(pattern[k, q] * BLK, BLK)
             weights[pl.ds(row, BLK), q * BLK : (q + 1) * BLK] = load[q, k]
     copies[2].wait()
-    copies[3].wait()
-    hidden[...] = jax.nn.gelu(jnp.dot(rows_in[...], enc_in[...], preferred_element_type=F32)).astype(BF16)
-    gain_weights[...] = jnp.zeros_like(gain_weights)
-    copies[4].wait()
     for at in range(keep.shape[0]):
         total = lax.dot_general(cotangent[...], weights[window_of(at), :], NT, preferred_element_type=F32)
         split(keep, send, at, total)
-    for copy in copies[5:]:
+    for copy in copies[3:]:
         copy.wait()
 
 
 def drive_kernel(
-    cleared, hidden, enc_out, gain, available, readings, table_far,
+    cleared, rows_in, enc_in, enc_out, gain, available, readings, table_far,
     weights, keep, send, mask,
     lhs, pattern, sem,
 ):
     fetch = pltpu.make_async_copy(table_far, pattern, sem)
     fetch.start()
     traces, blocks, steps = available.shape
+    hidden = jax.nn.gelu(jnp.dot(rows_in[...], enc_in[...], preferred_element_type=F32)).astype(BF16)
     for b in range(traces):
         mask[b * steps : (b + 1) * steps, :] = available[b].astype(F32).T
     for q in range(blocks):
@@ -108,7 +106,7 @@
             weights[q * BLK : (q + 1) * BLK, pl.ds(column, BLK)] = gain[q, k]
     for at in range(keep.shape[0]):
         total = jnp.dot(lhs[...], weights[:, window_of(at)], preferred_element_type=F32)
-        total += jnp.dot(hidden[...], enc_out[:, window_of(at)], preferred_element_type=F32)
+        total += jnp.dot(hidden, enc_out[:, window_of(at)], preferred_element_type=F32)
         split(keep, send, at, total)
 
 
@@ -200,13 +198,11 @@
             before[which, b, 1] = value_before
             end = 0 if backward else SEG - 1
             half, row = which // 2, (which % 2) * traces + b
-            ends[half, 0, row : row + 1, :] = total[end : end + 1, :]
-            ends[half, 1, row : row + 1, :] = whole[end : end + 1, :]
+            ends[half, row : row + 1, :] = total[end : end + 1, :]
+            ends[half, SEG + row : SEG + row + 1, :] = -jnp.log(jnp.maximum(whole[end : end + 1, :], 1e-37))
     me = lax.axis_index("tm")
     for target in range(parcel.shape[0]):
-        onward = target > me
-        parcel[target, :SEG] = jnp.where(onward, ends[0, 0], ends[1, 0])
-        parcel[target, SEG:] = jnp.where(onward, ends[0, 1], ends[1, 1])
+        parcel[target] = jnp.where(target > me, ends[0], ends[1]).astype(BF16)
 
 
 def settle_kernel(
@@ -218,10 +214,18 @@
     me, length = lax.axis_index("tm"), parcel.shape[0]
     onward = jnp.zeros((SEG, BLK), F32)
     back = onward
+
+    def pair(j):
+        both = parcel[j].astype(F32)
+        return jnp.exp(-both[SEG:]), both[:SEG]
+
+    pairs = [pair(j) for j in range(length)]
     for j in range(length):
-        onward = jnp.where(j < me, parcel[j, SEG:] * onward + parcel[j, :SEG], onward)
+        factor, value = pairs[j]
+        onward = jnp.where(j < me, factor * onward + value, onward)
         i = length - 1 - j
-        back = jnp.where(i > me, parcel[i, SEG:] * back + parcel[i, :SEG], back)
+        factor, value = pairs[i]
+        back = jnp.where(i > me, factor * back + value, back)
     carry[0] = onward
     carry[1] = back
     for b in range(traces):
@@ -265,10 +269,10 @@
                 if which == 1:
                     piece = piece * mask[:, q : q + 1]
                 stage[which, :, q * BLK : (q + 1) * BLK] = piece.astype(BF16)
-            if at % 2:
-                window = slice((at - 1) * 2 * BLK, (at + 1) * 2 * BLK)
+            if which == 1 or at % 2:
+                window = window if which == 1 else slice((at - 1) * 2 * BLK, (at + 1) * 2 * BLK)
                 copies.append(
-                    pltpu.make_async_copy(stage.at[which, :, window], outs[which].at[:, window], sems.at[which, at // 2])
+                    pltpu.make_async_copy(stage.at[which, :, window], outs[which].at[:, window], sems.at[which, at])
                 )
                 copies[-1].start()
     for copy in copies:
@@ -290,15 +294,18 @@
         moved = {k: lax.ppermute(pieces[k - 1], "state", [(i, (i + 2 * k) % axis) for i in range(axis)]) for k in (1, 3, 2)}
         return [moved[k] for k in (1, 2, 3)]
 
-    fetched = (encoder_out, gain, available.transpose(0, 2, 1), readings.reshape(rows, sensors))
-    staged = (load, inputs.reshape(rows, features), encoder_in, cotangent.reshape(rows, sensors))
+    fetched = (
+        inputs.reshape(rows, features), encoder_in, encoder_out, gain, available.transpose(0, 2, 1),
+        readings.reshape(rows, sensors),
+    )
+    staged = (load, cotangent.reshape(rows, sensors))
     table = pattern.T
     parts = (struct((axis // 2, rows, BLK), F32), struct((axis // 2, rows, BLK), BF16))
-    load_weights, keep_b, send_b, cleared, hidden, *fetched = call(
+    load_weights, keep_b, send_b, cleared, *fetched = call(
         pull_kernel,
         (
             struct((states, sensors), BF16), *parts, struct((sensors, states), BF16),
-            struct((rows, encoder_in.shape[1]), BF16), *(struct(a.shape, a.dtype) for a in fetched),
+            *(struct(a.shape, a.dtype) for a in fetched),
         ),
         (table, *staged, *fetched),
         scratch=[pltpu.SMEM(table.shape, table.dtype)]
@@ -311,7 +318,7 @@
     gain_weights, keep_a, send_a, mask = call(
         drive_kernel,
         (struct((sensors, states), BF16), *parts, struct((rows, blocks), F32)),
-        (cleared, hidden, *fetched, table),
+        (cleared, *fetched, table),
         scratch=[
             pltpu.VMEM((rows, sensors), BF16),
             pltpu.SMEM(table.shape, table.dtype),
@@ -337,9 +344,9 @@
     )
     scanned, pulled, before, parcel = call(
         functools.partial(scan_kernel, traces, steps),
-        (full, full, struct((4, traces, 2, SEG, BLK), F32), struct((times, 2 * SEG, BLK), F32)),
+        (full, full, struct((4, traces, 2, SEG, BLK), F32), struct((times, 2 * SEG, BLK), BF16)),
         (own_a, own_b, *sums_a, *sums_b, keep_r, keep_s, root, seg_r, seg_s),
-        scratch=[pltpu.VMEM((rows, BLK), F32)] * 2 + [pltpu.VMEM((2, 2, SEG, BLK), F32)],
+        scratch=[pltpu.VMEM((rows, BLK), F32)] * 2 + [pltpu.VMEM((2, 2 * SEG, BLK), F32)],
     )
     parcel = lax.all_to_all(parcel, "tm", 0, 0)
     (smoothed,) = call(
@@ -363,7 +370,7 @@
             (struct((rows, sensors), BF16 if last else F32),) * 2,
             (same[shift], partner, load_weights, gain_weights, mask, *totals),
             scratch=[pltpu.VMEM((2, rows, 2 * BLK), BF16)]
-            + ([pltpu.VMEM((2, rows, sensors), BF16), pltpu.SemaphoreType.DMA((2, 2))] if last else []),
+            + ([pltpu.VMEM((2, rows, sensors), BF16), pltpu.SemaphoreType.DMA((2, 4))] if last else []),
                 hbm_out=last,
             flops=work // 2,
         )

time: 75.9 us -> 74.2 us (0.978)
  blocking collectives: 20.9 us -> 19.3 us
    all_to_all x1, blocking collectives: 20.9 us -> 19.3 us  [local(): parcel = lax.all_to_all(parcel, 'tm', 0, 0)]
where the time goes in v5:
time: 74.2 us; the launch traced here: 74 us
  waiting for transfers between devices  24.1 us (32%)
  blocking collectives  19.3 us (26%)
  starting transfers between devices  17.2 us (23%)
  Pallas kernels  12.5 us (17%)
  between operations  0.91 us (1%)
    ppermute x9, waiting for transfers between devices, across(): lax.ppermute(pieces[k - 1], 'state', [(i, (i + 2 * k) % axis) for i in ra...  21.9 us
    all_to_all x1, blocking collectives, local(): parcel = lax.all_to_all(parcel, 'tm', 0, 0)  19.3 us
    pallas_call x11, Pallas kernels, call(): pl.pallas_call(kernel, out_shape=outs, in_specs=[vmem] * (len(operands) -...  12.5 us
    ppermute x9, starting transfers between devices, across(): lax.ppermute(pieces[k - 1], 'state', [(i, (i + 2 * k) % axis) for i in ra...  9 us
    ppermute x4, starting transfers between devices, local(): partner = lax.ppermute(same[shift], 'state', swap)  4.76 us
    ppermute x1, starting transfers between devices, local(): came_b = lax.ppermute(send_b, 'state', swap)  3.29 us
    ppermute x1, waiting for transfers between devices, local(): came_a = lax.ppermute(send_a, 'state', swap)  1.78 us
  transfers between devices with their start and end apart: 15, of which 9 were waited for; matrix products, arithmetic and copies ran while one was open for 0% of the time, Pallas kernels for 7%

profile of v5, /device:TPU:1, one launch (start us, length us, event | category | flops | bytes accessed | tf_op | source)
XLA Modules:
  0.0 74.0 jit_solution(17635948509283468378)
XLA Ops:
  0.6 3.4 %shard_map.122 = (bf16[1024,1024]{1,0:T(8,128)(2,1)S(1)}, f32[4,512,128]{2,1,0:T(8,128)S(1)}, bf16[4,512,128]{2,1,0:T(8,128)(2,1)S(1)}, bf16[1024,1024]{1,0:T(8,...) custom-call(s32[4,8]{1,0:T(4,128)} %bitcast.15, ...), custom_call_target="tpu_custom_call" | custom-call | flops 1073741824 | bytes 13926528 | tf_op jit(solution)/shard_map/pallas_call | solution.py:23
  4.1 3.3 %collective-permute-start = (bf16[4,512,128]{2,1,0:T(8,128)(2,1)S(1)}, bf16[4,512,128]{2,1,0:T(8,128)(2,1)S(1)}, u32[]{:S(2)}, u32[]{:S(2)}) collective-permute-start(bf16[4,512,128]{2,1,0:T(8,128)(2,1)S(1)} %get-tuple-element.65), channel_id=1, source_target_pairs={{0,1},{1,0},{2,3},{3,2},{4,5},{5,4},{6,7},{7,6},{8,9},{9,8},{10,11... | collective-permute-start | bytes 1572872 | tf_op jit(solution)/shard_map/ppermute | solution.py:317
  7.3 2.4 %shard_map.123 = (bf16[1024,1024]{1,0:T(8,128)(2,1)S(1)}, f32[4,512,128]{2,1,0:T(8,128)S(1)}, bf16[4,512,128]{2,1,0:T(8,128)(2,1)S(1)}, f32[512,8]{1,0:T(8,128)S(1)}) custom-call(bf16[1024,1024]{1,0:T(8,128)(2,1)S(1)} %get-tuple-element.56.cleared, bf16[512,256]{1,0:T(8,128)(2,1)S(1)} %get-tuple-element.57.rows_in, ...), custom_call_target="tpu_custom_call", output_to_operand_aliasing={{0}: (0, {})} | custom-call | flops 1073741824 | bytes 8814720 | tf_op jit(solution)/shard_map/pallas_call | solution.py:23
  9.7 0.0 copy-start
  9.7 0.0 copy-start.1
  9.7 0.1 collective-permute-start.1
  9.9 0.0 collective-permute-done.came
  9.9 0.1 shard_map.124
  10.0 1.8 %collective-permute-done.1.came = bf16[4,512,128]{2,1,0:T(8,128)(2,1)S(1)} collective-permute-done((bf16[4,512,128]{2,1,0:T(8,128)(2,1)S(1)}, bf16[4,512,128]{2,1,0:T(8,128)(2,1)S(1)}, u32[]{:S(2)}, u32[]{:S(2)}) %collective-permute-start.1) | collective-permute-done | bytes 524320 | tf_op jit(solution)/shard_map/ppermute | solution.py:331
  11.7 0.1 shard_map.125
  11.8 0.1 collective-permute-start.2
  11.9 1.9 %collective-permute-start.3 = (bf16[512,128]{1,0:T(8,128)(2,1)S(1)}, bf16[512,128]{1,0:T(8,128)(2,1)S(1)}, u32[]{:S(2)}, u32[]{:S(2)}) collective-permute-start(bf16[512,128]{1,0:T(8,128)(2,1)S(1)} %get-tuple-element.72), channel_id=1, source_target_pairs={{0,4},{1,5},{2,6},{3,7},{4,0},{5,1},{6,2},{7,3},{8,12},{9,13},{10,... | collective-permute-start | bytes 393224 | tf_op jit(solution)/shard_map/ppermute | solution.py:294
  13.9 1.2 %collective-permute-start.4 = (bf16[512,128]{1,0:T(8,128)(2,1)S(1)}, bf16[512,128]{1,0:T(8,128)(2,1)S(1)}, u32[]{:S(2)}, u32[]{:S(2)}) collective-permute-start(bf16[512,128]{1,0:T(8,128)(2,1)S(1)} %get-tuple-element.73), channel_id=1, source_target_pairs={{0,6},{1,7},{2,0},{3,1},{4,2},{5,3},{6,4},{7,5},{8,14},{9,15},{10,... | collective-permute-start | bytes 393224 | tf_op jit(solution)/shard_map/ppermute | solution.py:294
  15.0 0.3 collective-permute-start.5
  15.3 1.6 %collective-permute-start.6 = (bf16[512,128]{1,0:T(8,128)(2,1)S(1)}, bf16[512,128]{1,0:T(8,128)(2,1)S(1)}, u32[]{:S(2)}, u32[]{:S(2)}) collective-permute-start(bf16[512,128]{1,0:T(8,128)(2,1)S(1)} %get-tuple-element.75), channel_id=1, source_target_pairs={{0,4},{1,5},{2,6},{3,7},{4,0},{5,1},{6,2},{7,3},{8,12},{9,13},{10,... | collective-permute-start | bytes 393224 | tf_op jit(solution)/shard_map/ppermute | solution.py:294
  17.0 3.4 %collective-permute-done.2.a1 = bf16[512,128]{1,0:T(8,128)(2,1)S(1)} collective-permute-done((bf16[512,128]{1,0:T(8,128)(2,1)S(1)}, bf16[512,128]{1,0:T(8,128)(2,1)S(1)}, u32[]{:S(2)}, u32[]{:S(2)}) %collective-permute-start.2) | collective-permute-done | bytes 131104 | tf_op jit(solution)/shard_map/ppermute | solution.py:294
  20.3 0.0 collective-permute-start.7
  20.3 0.0 copy-done
  20.3 0.0 copy-done.1
  20.3 0.6 shard_map.126
  20.9 0.0 collective-permute-done.3.a2
  20.9 0.2 collective-permute-done.4.a3
  21.2 3.1 %collective-permute-done.5.b1 = bf16[512,128]{1,0:T(8,128)(2,1)S(1)} collective-permute-done((bf16[512,128]{1,0:T(8,128)(2,1)S(1)}, bf16[512,128]{1,0:T(8,128)(2,1)S(1)}, u32[]{:S(2)}, u32[]{:S(2)}) %collective-permute-start.5) | collective-permute-done | bytes 131104 | tf_op jit(solution)/shard_map/ppermute | solution.py:294
  24.3 1.6 %collective-permute-done.6.b2 = bf16[512,128]{1,0:T(8,128)(2,1)S(1)} collective-permute-done((bf16[512,128]{1,0:T(8,128)(2,1)S(1)}, bf16[512,128]{1,0:T(8,128)(2,1)S(1)}, u32[]{:S(2)}, u32[]{:S(2)}) %collective-permute-start.6) | collective-permute-done | bytes 131104 | tf_op jit(solution)/shard_map/ppermute | solution.py:294
  25.8 1.0 %collective-permute-done.7.b3 = bf16[512,128]{1,0:T(8,128)(2,1)S(1)} collective-permute-done((bf16[512,128]{1,0:T(8,128)(2,1)S(1)}, bf16[512,128]{1,0:T(8,128)(2,1)S(1)}, u32[]{:S(2)}, u32[]{:S(2)}) %collective-permute-start.7) | collective-permute-done | bytes 131104 | tf_op jit(solution)/shard_map/ppermute | solution.py:294
  26.8 1.1 %shard_map.127 = (f32[512,128]{1,0:T(8,128)S(1)}, f32[512,128]{1,0:T(8,128)S(1)}, f32[4,4,2,8,128]{4,3,2,1,0:T(8,128)S(1)}, bf16[32,16,128]{2,1,0:T(8,128)(2,1)S(1)}) custom-call(f32[512,128]{1,0:T(8,128)S(1)} %get-tuple-element.69.own_a, f32[512,128]{1,0:T(8,128)S(1)} %get-tuple-element.70.own_b, bf16[512,128]{1,0:T(8,128)(2,1)S(1)} %collective-permute-done.2.a1, ...), custom_call_target="tpu_custom_call" | custom-call | bytes 2916352 | tf_op jit(solution)/shard_map/pallas_call | solution.py:23
  28.0 19.3 %all_to_all.5.parcel = bf16[32,16,128]{2,1,0:T(8,128)(2,1)S(1)} all-to-all(bf16[32,16,128]{2,1,0:T(8,128)(2,1)S(1)} %get-tuple-element.82), channel_id=1, replica_groups=mesh['tm'=32,'state'=8] {'tm'}, dimensions={0} | all-to-all | bytes 262144 | tf_op jit(solution)/shard_map/all_to_all | solution.py:351
  47.3 0.7 shard_map.128.mine
  48.0 2.7 %collective-permute-start.8 = (bf16[2,512,128]{2,1,0:T(8,128)(2,1)S(1)}, bf16[2,512,128]{2,1,0:T(8,128)(2,1)S(1)}, u32[]{:S(2)}, u32[]{:S(2)}) collective-permute-start(bf16[2,512,128]{2,1,0:T(8,128)(2,1)S(1)} %shard_map.128.mine), channel_id=1, source_target_pairs={{0,1},{1,0},{2,3},{3,2},{4,5},{5,4},{6,7},{7,6},{8,9},{9,8},{10,11... | collective-permute-start | bytes 786440 | tf_op jit(solution)/shard_map/ppermute | solution.py:367
  50.7 1.1 %collective-permute-start.9 = (bf16[2,512,128]{2,1,0:T(8,128)(2,1)S(1)}, bf16[2,512,128]{2,1,0:T(8,128)(2,1)S(1)}, u32[]{:S(2)}, u32[]{:S(2)}) collective-permute-start(bf16[2,512,128]{2,1,0:T(8,128)(2,1)S(1)} %shard_map.128.mine), channel_id=1, source_target_pairs={{0,2},{1,3},{2,4},{3,5},{4,6},{5,7},{6,0},{7,1},{8,10},{9,11},{10,... | collective-permute-start | bytes 786440 | tf_op jit(solution)/shard_map/ppermute | solution.py:294
  51.7 1.6 %collective-permute-start.11 = (bf16[2,512,128]{2,1,0:T(8,128)(2,1)S(1)}, bf16[2,512,128]{2,1,0:T(8,128)(2,1)S(1)}, u32[]{:S(2)}, u32[]{:S(2)}) collective-permute-start(bf16[2,512,128]{2,1,0:T(8,128)(2,1)S(1)} %shard_map.128.mine), channel_id=1, source_target_pairs={{0,6},{1,7},{2,0},{3,1},{4,2},{5,3},{6,4},{7,5},{8,14},{9,15},{10,... | collective-permute-start | bytes 786440 | tf_op jit(solution)/shard_map/ppermute | solution.py:294
  53.4 0.0 collective-permute-done.8.partner
  53.4 0.7 %shard_map.129 = (f32[512,1024]{1,0:T(8,128)S(1)}, f32[512,1024]{1,0:T(8,128)S(1)}) custom-call(bf16[2,512,128]{2,1,0:T(8,128)(2,1)S(1)} %shard_map.128.mine, bf16[2,512,128]{2,1,0:T(8,128)(2,1)S(1)} %collective-permute-done.8.partner, bf16[1024,1024]{1,0:T(8,128)(2,1)S(1)} %get-tuple-element.90.load_weights, ...), custom_call_target="tpu_custom_call" | custom-call | flops 536870912 | bytes 8929280 | tf_op jit(solution)/shard_map/pallas_call | solution.py:23
  54.1 5.6 %collective-permute-done.9.mine = bf16[2,512,128]{2,1,0:T(8,128)(2,1)S(1)} collective-permute-done((bf16[2,512,128]{2,1,0:T(8,128)(2,1)S(1)}, bf16[2,512,128]{2,1,0:T(8,128)(2,1)S(1)}, u32[]{:S(2)}, u32[]{:S(2)}) %collective-permute-start.9) | collective-permute-done | bytes 262176 | tf_op jit(solution)/shard_map/ppermute | solution.py:294
  59.7 0.9 %collective-permute-start.10 = (bf16[2,512,128]{2,1,0:T(8,128)(2,1)S(1)}, bf16[2,512,128]{2,1,0:T(8,128)(2,1)S(1)}, u32[]{:S(2)}, u32[]{:S(2)}) collective-permute-start(bf16[2,512,128]{2,1,0:T(8,128)(2,1)S(1)} %collective-permute-done.9.mine), channel_id=1, source_target_pairs={{0,1},{1,0},{2,3},{3,2},{4,5},{5,4},{6,7},{7,6},{8,9},{9,8},{10,11... | collective-permute-start | bytes 786440 | tf_op jit(solution)/shard_map/ppermute | solution.py:367
  60.6 1.2 %collective-permute-start.12 = (bf16[2,512,128]{2,1,0:T(8,128)(2,1)S(1)}, bf16[2,512,128]{2,1,0:T(8,128)(2,1)S(1)}, u32[]{:S(2)}, u32[]{:S(2)}) collective-permute-start(bf16[2,512,128]{2,1,0:T(8,128)(2,1)S(1)} %shard_map.128.mine), channel_id=1, source_target_pairs={{0,4},{1,5},{2,6},{3,7},{4,0},{5,1},{6,2},{7,3},{8,12},{9,13},{10,... | collective-permute-start | bytes 786440 | tf_op jit(solution)/shard_map/ppermute | solution.py:294
  61.8 0.0 collective-permute-done.11.mine
  61.8 0.3 collective-permute-start.14
  62.1 0.0 collective-permute-done.10.partner
  62.1 0.8 %shard_map.130 = (f32[512,1024]{1,0:T(8,128)S(1)}, f32[512,1024]{1,0:T(8,128)S(1)}) custom-call(bf16[2,512,128]{2,1,0:T(8,128)(2,1)S(1)} %collective-permute-done.9.mine, bf16[2,512,128]{2,1,0:T(8,128)(2,1)S(1)} %collective-permute-done.10.partner, bf16[1024,1024]{1,0:T(8,128)(2,1)S(1)} %get-tuple-element.90.load_weights, ...), custom_call_target="tpu_custom_call" | custom-call | flops 536870912 | bytes 13123584 | tf_op jit(solution)/shard_map/pallas_call | solution.py:23
  62.9 7.1 %collective-permute-done.12.mine = bf16[2,512,128]{2,1,0:T(8,128)(2,1)S(1)} collective-permute-done((bf16[2,512,128]{2,1,0:T(8,128)(2,1)S(1)}, bf16[2,512,128]{2,1,0:T(8,128)(2,1)S(1)}, u32[]{:S(2)}, u32[]{:S(2)}) %collective-permute-start.12) | collective-permute-done | bytes 262176 | tf_op jit(solution)/shard_map/ppermute | solution.py:294
  70.0 0.9 %collective-permute-start.13 = (bf16[2,512,128]{2,1,0:T(8,128)(2,1)S(1)}, bf16[2,512,128]{2,1,0:T(8,128)(2,1)S(1)}, u32[]{:S(2)}, u32[]{:S(2)}) collective-permute-start(bf16[2,512,128]{2,1,0:T(8,128)(2,1)S(1)} %collective-permute-done.12.mine), channel_id=1, source_target_pairs={{0,1},{1,0},{2,3},{3,2},{4,5},{5,4},{6,7},{7,6},{8,9},{9,8},{10,11... | collective-permute-start | bytes 786440 | tf_op jit(solution)/shard_map/ppermute | solution.py:367
  70.8 0.0 collective-permute-done.14.partner
  70.9 0.8 %shard_map.131 = (f32[512,1024]{1,0:T(8,128)S(1)}, f32[512,1024]{1,0:T(8,128)S(1)}) custom-call(bf16[2,512,128]{2,1,0:T(8,128)(2,1)S(1)} %collective-permute-done.11.mine, bf16[2,512,128]{2,1,0:T(8,128)(2,1)S(1)} %collective-permute-done.14.partner, bf16[1024,1024]{1,0:T(8,128)(2,1)S(1)} %get-tuple-element.90.load_weights, ...), custom_call_target="tpu_custom_call" | custom-call | flops 536870912 | bytes 13123584 | tf_op jit(solution)/shard_map/pallas_call | solution.py:23
  71.6 0.4 collective-permute-done.13.partner
  72.0 1.8 %shard_map.132 = (bf16[512,1024]{1,0:T(8,128)(2,1)}, bf16[512,1024]{1,0:T(8,128)(2,1)}) custom-call(bf16[2,512,128]{2,1,0:T(8,128)(2,1)S(1)} %collective-permute-done.12.mine, bf16[2,512,128]{2,1,0:T(8,128)(2,1)S(1)} %collective-permute-done.13.partner, bf16[1024,1024]{1,0:T(8,128)(2,1)S(1)} %get-tuple-element.90.load_weights, ...), custom_call_target="tpu_custom_call" | custom-call | flops 536870912 | bytes 11026432 | tf_op jit(solution)/shard_map/pallas_call | solution.py:23
Async XLA Ops:
  4.1 5.8 %collective-permute-start = (bf16[4,512,128]{2,1,0:T(8,128)(2,1)S(1)}, bf16[4,512,128]{2,1,0:T(8,128)(2,1)S(1)}, u32[]{:S(2)}, u32[]{:S(2)}) collective-permute-start(bf16[4,512,128]{2,1,0:T(8,128)(2,1)S(1)} %get-tuple-element.65), channel_id=1, source_target_pairs={{0,1},{1,0},{2,3},{3,2},{4,5},{5,4},{6,7},{7,6},{8,9},{9,8},{10,11... | collective-permute-start | bytes 1572872 | tf_op jit(solution)/shard_map/ppermute | solution.py:317
  9.7 10.6 %copy-start = (f32[128,4,128]{2,1,0:T(4,128)S(1)}, f32[128,4,128]{2,1,0:T(4,128)}, u32[]{:S(2)}) copy-start(f32[128,4,128]{2,1,0:T(4,128)} %param.19) | copy-start | bytes 786436
  9.7 10.6 %copy-start.1 = (f32[128,4,128]{2,1,0:T(4,128)S(1)}, f32[128,4,128]{2,1,0:T(4,128)}, u32[]{:S(2)}) copy-start(f32[128,4,128]{2,1,0:T(4,128)} %param.20) | copy-start | bytes 786436
  9.7 2.0 %collective-permute-start.1 = (bf16[4,512,128]{2,1,0:T(8,128)(2,1)S(1)}, bf16[4,512,128]{2,1,0:T(8,128)(2,1)S(1)}, u32[]{:S(2)}, u32[]{:S(2)}) collective-permute-start(bf16[4,512,128]{2,1,0:T(8,128)(2,1)S(1)} %get-tuple-element.68), channel_id=1, source_target_pairs={{0,1},{1,0},{2,3},{3,2},{4,5},{5,4},{6,7},{7,6},{8,9},{9,8},{10,11... | collective-permute-start | bytes 1572872 | tf_op jit(solution)/shard_map/ppermute | solution.py:331
  11.8 8.5 %collective-permute-start.2 = (bf16[512,128]{1,0:T(8,128)(2,1)S(1)}, bf16[512,128]{1,0:T(8,128)(2,1)S(1)}, u32[]{:S(2)}, u32[]{:S(2)}) collective-permute-start(bf16[512,128]{1,0:T(8,128)(2,1)S(1)} %get-tuple-element.71), channel_id=1, source_target_pairs={{0,2},{1,3},{2,4},{3,5},{4,6},{5,7},{6,0},{7,1},{8,10},{9,11},{10,... | collective-permute-start | bytes 393224 | tf_op jit(solution)/shard_map/ppermute | solution.py:294
  11.9 9.0 %collective-permute-start.3 = (bf16[512,128]{1,0:T(8,128)(2,1)S(1)}, bf16[512,128]{1,0:T(8,128)(2,1)S(1)}, u32[]{:S(2)}, u32[]{:S(2)}) collective-permute-start(bf16[512,128]{1,0:T(8,128)(2,1)S(1)} %get-tuple-element.72), channel_id=1, source_target_pairs={{0,4},{1,5},{2,6},{3,7},{4,0},{5,1},{6,2},{7,3},{8,12},{9,13},{10,... | collective-permute-start | bytes 393224 | tf_op jit(solution)/shard_map/ppermute | solution.py:294
  13.9 7.3 %collective-permute-start.4 = (bf16[512,128]{1,0:T(8,128)(2,1)S(1)}, bf16[512,128]{1,0:T(8,128)(2,1)S(1)}, u32[]{:S(2)}, u32[]{:S(2)}) collective-permute-start(bf16[512,128]{1,0:T(8,128)(2,1)S(1)} %get-tuple-element.73), channel_id=1, source_target_pairs={{0,6},{1,7},{2,0},{3,1},{4,2},{5,3},{6,4},{7,5},{8,14},{9,15},{10,... | collective-permute-start | bytes 393224 | tf_op jit(solution)/shard_map/ppermute | solution.py:294
  15.0 9.2 %collective-permute-start.5 = (bf16[512,128]{1,0:T(8,128)(2,1)S(1)}, bf16[512,128]{1,0:T(8,128)(2,1)S(1)}, u32[]{:S(2)}, u32[]{:S(2)}) collective-permute-start(bf16[512,128]{1,0:T(8,128)(2,1)S(1)} %get-tuple-element.74), channel_id=1, source_target_pairs={{0,2},{1,3},{2,4},{3,5},{4,6},{5,7},{6,0},{7,1},{8,10},{9,11},{10,... | collective-permute-start | bytes 393224 | tf_op jit(solution)/shard_map/ppermute | solution.py:294
  15.3 10.5 %collective-permute-start.6 = (bf16[512,128]{1,0:T(8,128)(2,1)S(1)}, bf16[512,128]{1,0:T(8,128)(2,1)S(1)}, u32[]{:S(2)}, u32[]{:S(2)}) collective-permute-start(bf16[512,128]{1,0:T(8,128)(2,1)S(1)} %get-tuple-element.75), channel_id=1, source_target_pairs={{0,4},{1,5},{2,6},{3,7},{4,0},{5,1},{6,2},{7,3},{8,12},{9,13},{10,... | collective-permute-start | bytes 393224 | tf_op jit(solution)/shard_map/ppermute | solution.py:294
  20.3 6.5 %collective-permute-start.7 = (bf16[512,128]{1,0:T(8,128)(2,1)S(1)}, bf16[512,128]{1,0:T(8,128)(2,1)S(1)}, u32[]{:S(2)}, u32[]{:S(2)}) collective-permute-start(bf16[512,128]{1,0:T(8,128)(2,1)S(1)} %get-tuple-element.76), channel_id=1, source_target_pairs={{0,6},{1,7},{2,0},{3,1},{4,2},{5,3},{6,4},{7,5},{8,14},{9,15},{10,... | collective-permute-start | bytes 393224 | tf_op jit(solution)/shard_map/ppermute | solution.py:294
  48.0 5.3 %collective-permute-start.8 = (bf16[2,512,128]{2,1,0:T(8,128)(2,1)S(1)}, bf16[2,512,128]{2,1,0:T(8,128)(2,1)S(1)}, u32[]{:S(2)}, u32[]{:S(2)}) collective-permute-start(bf16[2,512,128]{2,1,0:T(8,128)(2,1)S(1)} %shard_map.128.mine), channel_id=1, source_target_pairs={{0,1},{1,0},{2,3},{3,2},{4,5},{5,4},{6,7},{7,6},{8,9},{9,8},{10,11... | collective-permute-start | bytes 786440 | tf_op jit(solution)/shard_map/ppermute | solution.py:367
  50.7 9.0 %collective-permute-start.9 = (bf16[2,512,128]{2,1,0:T(8,128)(2,1)S(1)}, bf16[2,512,128]{2,1,0:T(8,128)(2,1)S(1)}, u32[]{:S(2)}, u32[]{:S(2)}) collective-permute-start(bf16[2,512,128]{2,1,0:T(8,128)(2,1)S(1)} %shard_map.128.mine), channel_id=1, source_target_pairs={{0,2},{1,3},{2,4},{3,5},{4,6},{5,7},{6,0},{7,1},{8,10},{9,11},{10,... | collective-permute-start | bytes 786440 | tf_op jit(solution)/shard_map/ppermute | solution.py:294
  51.7 10.1 %collective-permute-start.11 = (bf16[2,512,128]{2,1,0:T(8,128)(2,1)S(1)}, bf16[2,512,128]{2,1,0:T(8,128)(2,1)S(1)}, u32[]{:S(2)}, u32[]{:S(2)}) collective-permute-start(bf16[2,512,128]{2,1,0:T(8,128)(2,1)S(1)} %shard_map.128.mine), channel_id=1, source_target_pairs={{0,6},{1,7},{2,0},{3,1},{4,2},{5,3},{6,4},{7,5},{8,14},{9,15},{10,... | collective-permute-start | bytes 786440 | tf_op jit(solution)/shard_map/ppermute | solution.py:294
  59.7 2.5 %collective-permute-start.10 = (bf16[2,512,128]{2,1,0:T(8,128)(2,1)S(1)}, bf16[2,512,128]{2,1,0:T(8,128)(2,1)S(1)}, u32[]{:S(2)}, u32[]{:S(2)}) collective-permute-start(bf16[2,512,128]{2,1,0:T(8,128)(2,1)S(1)} %collective-permute-done.9.mine), channel_id=1, source_target_pairs={{0,1},{1,0},{2,3},{3,2},{4,5},{5,4},{6,7},{7,6},{8,9},{9,8},{10,11... | collective-permute-start | bytes 786440 | tf_op jit(solution)/shard_map/ppermute | solution.py:367
  60.6 9.4 %collective-permute-start.12 = (bf16[2,512,128]{2,1,0:T(8,128)(2,1)S(1)}, bf16[2,512,128]{2,1,0:T(8,128)(2,1)S(1)}, u32[]{:S(2)}, u32[]{:S(2)}) collective-permute-start(bf16[2,512,128]{2,1,0:T(8,128)(2,1)S(1)} %shard_map.128.mine), channel_id=1, source_target_pairs={{0,4},{1,5},{2,6},{3,7},{4,0},{5,1},{6,2},{7,3},{8,12},{9,13},{10,... | collective-permute-start | bytes 786440 | tf_op jit(solution)/shard_map/ppermute | solution.py:294
  61.8 9.0 %collective-permute-start.14 = (bf16[2,512,128]{2,1,0:T(8,128)(2,1)S(1)}, bf16[2,512,128]{2,1,0:T(8,128)(2,1)S(1)}, u32[]{:S(2)}, u32[]{:S(2)}) collective-permute-start(bf16[2,512,128]{2,1,0:T(8,128)(2,1)S(1)} %collective-permute-done.11.mine), channel_id=1, source_target_pairs={{0,1},{1,0},{2,3},{3,2},{4,5},{5,4},{6,7},{7,6},{8,9},{9,8},{10,11... | collective-permute-start | bytes 786440 | tf_op jit(solution)/shard_map/ppermute | solution.py:367
  70.0 2.0 %collective-permute-start.13 = (bf16[2,512,128]{2,1,0:T(8,128)(2,1)S(1)}, bf16[2,512,128]{2,1,0:T(8,128)(2,1)S(1)}, u32[]{:S(2)}, u32[]{:S(2)}) collective-permute-start(bf16[2,512,128]{2,1,0:T(8,128)(2,1)S(1)} %collective-permute-done.12.mine), channel_id=1, source_target_pairs={{0,1},{1,0},{2,3},{3,2},{4,5},{5,4},{6,7},{7,6},{8,9},{9,8},{10,11... | collective-permute-start | bytes 786440 | tf_op jit(solution)/shard_map/ppermute | solution.py:367

commit v6 on v5

--- a/solution.py
+++ b/solution.py
@@ -66,14 +66,12 @@
         (enc_out_far, enc_out), (gain_far, gain), (available_far, available), (readings_far, readings),
     )
     copies = [pltpu.make_async_copy(far, near, sems.at[i]) for i, (far, near) in enumerate(pairs)]
-    for copy in copies[:3]:
+    for copy in copies:
         copy.start()
     weights[...] = jnp.zeros_like(weights)
     gain_weights[...] = jnp.zeros_like(gain_weights)
     copies[0].wait()
     copies[1].wait()
-    for copy in copies[3:]:
-        copy.start()
     for q in range(load.shape[0]):
         for k in range(load.shape[1]):
             row = pl.multiple_of(pattern[k, q] * BLK, BLK)
@@ -269,10 +267,10 @@
                 if which == 1:
                     piece = piece * mask[:, q : q + 1]
                 stage[which, :, q * BLK : (q + 1) * BLK] = piece.astype(BF16)
-            if which == 1 or at % 2:
-                window = window if which == 1 else slice((at - 1) * 2 * BLK, (at + 1) * 2 * BLK)
+            if at % 2:
+                window = slice((at - 1) * 2 * BLK, (at + 1) * 2 * BLK)
                 copies.append(
-                    pltpu.make_async_copy(stage.at[which, :, window], outs[which].at[:, window], sems.at[which, at])
+                    pltpu.make_async_copy(stage.at[which, :, window], outs[which].at[:, window], sems.at[which, at // 2])
                 )
                 copies[-1].start()
     for copy in copies:
@@ -291,7 +289,9 @@
     both = struct((2, rows, BLK), BF16)
 
     def across(pieces):
-        moved = {k: lax.ppermute(pieces[k - 1], "state", [(i, (i + 2 * k) % axis) for i in range(axis)]) for k in (1, 3, 2)}
+        moved = {}
+        for k in (1, 3, 2):
+            moved[k] = lax.ppermute(pieces[k - 1], "state", [(i, (i + 2 * k) % axis) for i in range(axis)])
         return [moved[k] for k in (1, 2, 3)]
 
     fetched = (
@@ -370,7 +370,7 @@
             (struct((rows, sensors), BF16 if last else F32),) * 2,
             (same[shift], partner, load_weights, gain_weights, mask, *totals),
             scratch=[pltpu.VMEM((2, rows, 2 * BLK), BF16)]
-            + ([pltpu.VMEM((2, rows, sensors), BF16), pltpu.SemaphoreType.DMA((2, 4))] if last else []),
+            + ([pltpu.VMEM((2, rows, sensors), BF16), pltpu.SemaphoreType.DMA((2, 2))] if last else []),
                 hbm_out=last,
             flops=work // 2,
         )

time: 74.2 us -> 73.6 us (level)
  no operation moved by 1% of the time
where the time goes in v6:
time: 73.6 us; the launch traced here: 73.4 us
  waiting for transfers between devices  24.1 us (33%)
  blocking collectives  19.3 us (26%)
  starting transfers between devices  17.2 us (23%)
  Pallas kernels  11.9 us (16%)
  between operations  0.91 us (1%)
    ppermute x9, waiting for transfers between devices, across(): lax.ppermute(pieces[k - 1], 'state', [(i, (i + 2 * k) % axis) for i in ra...  21.9 us
    all_to_all x1, blocking collectives, local(): parcel = lax.all_to_all(parcel, 'tm', 0, 0)  19.3 us
    pallas_call x11, Pallas kernels, call(): pl.pallas_call(kernel, out_shape=outs, in_specs=[vmem] * (len(operands) -...  11.9 us
    ppermute x9, starting transfers between devices, across(): lax.ppermute(pieces[k - 1], 'state', [(i, (i + 2 * k) % axis) for i in ra...  9 us
    ppermute x4, starting transfers between devices, local(): partner = lax.ppermute(same[shift], 'state', swap)  4.76 us
    ppermute x1, starting transfers between devices, local(): came_b = lax.ppermute(send_b, 'state', swap)  3.29 us
    ppermute x1, waiting for transfers between devices, local(): came_a = lax.ppermute(send_a, 'state', swap)  1.78 us
  transfers between devices with their start and end apart: 15, of which 9 were waited for; matrix products, arithmetic and copies ran while one was open for 0% of the time, Pallas kernels for 7%

profile of v6, /device:TPU:1, one launch (start us, length us, event | category | flops | bytes accessed | tf_op | source)
XLA Modules:
  0.0 73.4 jit_solution(17430725735274863737)
XLA Ops:
  0.6 2.9 %shard_map.122 = (bf16[1024,1024]{1,0:T(8,128)(2,1)S(1)}, f32[4,512,128]{2,1,0:T(8,128)S(1)}, bf16[4,512,128]{2,1,0:T(8,128)(2,1)S(1)}, bf16[1024,1024]{1,0:T(8,...) custom-call(s32[4,8]{1,0:T(4,128)} %bitcast.15, ...), custom_call_target="tpu_custom_call" | custom-call | flops 1073741824 | bytes 13926528 | tf_op jit(solution)/shard_map/pallas_call | solution.py:23
  3.6 3.3 %collective-permute-start = (bf16[4,512,128]{2,1,0:T(8,128)(2,1)S(1)}, bf16[4,512,128]{2,1,0:T(8,128)(2,1)S(1)}, u32[]{:S(2)}, u32[]{:S(2)}) collective-permute-start(bf16[4,512,128]{2,1,0:T(8,128)(2,1)S(1)} %get-tuple-element.65), channel_id=1, source_target_pairs={{0,1},{1,0},{2,3},{3,2},{4,5},{5,4},{6,7},{7,6},{8,9},{9,8},{10,11... | collective-permute-start | bytes 1572872 | tf_op jit(solution)/shard_map/ppermute | solution.py:317
  6.9 2.4 %shard_map.123 = (bf16[1024,1024]{1,0:T(8,128)(2,1)S(1)}, f32[4,512,128]{2,1,0:T(8,128)S(1)}, bf16[4,512,128]{2,1,0:T(8,128)(2,1)S(1)}, f32[512,8]{1,0:T(8,128)S(1)}) custom-call(bf16[1024,1024]{1,0:T(8,128)(2,1)S(1)} %get-tuple-element.56.cleared, bf16[512,256]{1,0:T(8,128)(2,1)S(1)} %get-tuple-element.57.rows_in, ...), custom_call_target="tpu_custom_call", output_to_operand_aliasing={{0}: (0, {})} | custom-call | flops 1073741824 | bytes 8814720 | tf_op jit(solution)/shard_map/pallas_call | solution.py:23
  9.2 0.0 copy-start
  9.3 0.0 copy-start.1
  9.3 0.1 collective-permute-start.1
  9.4 0.0 collective-permute-done.came
  9.4 0.1 shard_map.124
  9.5 1.8 %collective-permute-done.1.came = bf16[4,512,128]{2,1,0:T(8,128)(2,1)S(1)} collective-permute-done((bf16[4,512,128]{2,1,0:T(8,128)(2,1)S(1)}, bf16[4,512,128]{2,1,0:T(8,128)(2,1)S(1)}, u32[]{:S(2)}, u32[]{:S(2)}) %collective-permute-start.1) | collective-permute-done | bytes 524320 | tf_op jit(solution)/shard_map/ppermute | solution.py:331
  11.3 0.1 shard_map.125
  11.4 0.1 collective-permute-start.2
  11.4 1.9 %collective-permute-start.3 = (bf16[512,128]{1,0:T(8,128)(2,1)S(1)}, bf16[512,128]{1,0:T(8,128)(2,1)S(1)}, u32[]{:S(2)}, u32[]{:S(2)}) collective-permute-start(bf16[512,128]{1,0:T(8,128)(2,1)S(1)} %get-tuple-element.72), channel_id=1, source_target_pairs={{0,4},{1,5},{2,6},{3,7},{4,0},{5,1},{6,2},{7,3},{8,12},{9,13},{10,... | collective-permute-start | bytes 393224 | tf_op jit(solution)/shard_map/ppermute | solution.py:294
  13.4 1.2 %collective-permute-start.4 = (bf16[512,128]{1,0:T(8,128)(2,1)S(1)}, bf16[512,128]{1,0:T(8,128)(2,1)S(1)}, u32[]{:S(2)}, u32[]{:S(2)}) collective-permute-start(bf16[512,128]{1,0:T(8,128)(2,1)S(1)} %get-tuple-element.73), channel_id=1, source_target_pairs={{0,6},{1,7},{2,0},{3,1},{4,2},{5,3},{6,4},{7,5},{8,14},{9,15},{10,... | collective-permute-start | bytes 393224 | tf_op jit(solution)/shard_map/ppermute | solution.py:294
  14.5 0.3 collective-permute-start.5
  14.9 1.6 %collective-permute-start.6 = (bf16[512,128]{1,0:T(8,128)(2,1)S(1)}, bf16[512,128]{1,0:T(8,128)(2,1)S(1)}, u32[]{:S(2)}, u32[]{:S(2)}) collective-permute-start(bf16[512,128]{1,0:T(8,128)(2,1)S(1)} %get-tuple-element.75), channel_id=1, source_target_pairs={{0,4},{1,5},{2,6},{3,7},{4,0},{5,1},{6,2},{7,3},{8,12},{9,13},{10,... | collective-permute-start | bytes 393224 | tf_op jit(solution)/shard_map/ppermute | solution.py:294
  16.5 3.4 %collective-permute-done.2.a1 = bf16[512,128]{1,0:T(8,128)(2,1)S(1)} collective-permute-done((bf16[512,128]{1,0:T(8,128)(2,1)S(1)}, bf16[512,128]{1,0:T(8,128)(2,1)S(1)}, u32[]{:S(2)}, u32[]{:S(2)}) %collective-permute-start.2) | collective-permute-done | bytes 131104 | tf_op jit(solution)/shard_map/ppermute | solution.py:294
  19.9 0.0 collective-permute-start.7
  19.9 0.0 copy-done
  19.9 0.0 copy-done.1
  19.9 0.6 shard_map.126
  20.4 0.0 collective-permute-done.3.a2
  20.5 0.2 collective-permute-done.4.a3
  20.7 3.1 %collective-permute-done.5.b1 = bf16[512,128]{1,0:T(8,128)(2,1)S(1)} collective-permute-done((bf16[512,128]{1,0:T(8,128)(2,1)S(1)}, bf16[512,128]{1,0:T(8,128)(2,1)S(1)}, u32[]{:S(2)}, u32[]{:S(2)}) %collective-permute-start.5) | collective-permute-done | bytes 131104 | tf_op jit(solution)/shard_map/ppermute | solution.py:294
  23.8 1.6 %collective-permute-done.6.b2 = bf16[512,128]{1,0:T(8,128)(2,1)S(1)} collective-permute-done((bf16[512,128]{1,0:T(8,128)(2,1)S(1)}, bf16[512,128]{1,0:T(8,128)(2,1)S(1)}, u32[]{:S(2)}, u32[]{:S(2)}) %collective-permute-start.6) | collective-permute-done | bytes 131104 | tf_op jit(solution)/shard_map/ppermute | solution.py:294
  25.4 1.0 %collective-permute-done.7.b3 = bf16[512,128]{1,0:T(8,128)(2,1)S(1)} collective-permute-done((bf16[512,128]{1,0:T(8,128)(2,1)S(1)}, bf16[512,128]{1,0:T(8,128)(2,1)S(1)}, u32[]{:S(2)}, u32[]{:S(2)}) %collective-permute-start.7) | collective-permute-done | bytes 131104 | tf_op jit(solution)/shard_map/ppermute | solution.py:294
  26.4 1.1 %shard_map.127 = (f32[512,128]{1,0:T(8,128)S(1)}, f32[512,128]{1,0:T(8,128)S(1)}, f32[4,4,2,8,128]{4,3,2,1,0:T(8,128)S(1)}, bf16[32,16,128]{2,1,0:T(8,128)(2,1)S(1)}) custom-call(f32[512,128]{1,0:T(8,128)S(1)} %get-tuple-element.69.own_a, f32[512,128]{1,0:T(8,128)S(1)} %get-tuple-element.70.own_b, bf16[512,128]{1,0:T(8,128)(2,1)S(1)} %collective-permute-done.2.a1, ...), custom_call_target="tpu_custom_call" | custom-call | bytes 2916352 | tf_op jit(solution)/shard_map/pallas_call | solution.py:23
  27.5 19.3 %all_to_all.5.parcel = bf16[32,16,128]{2,1,0:T(8,128)(2,1)S(1)} all-to-all(bf16[32,16,128]{2,1,0:T(8,128)(2,1)S(1)} %get-tuple-element.82), channel_id=1, replica_groups=mesh['tm'=32,'state'=8] {'tm'}, dimensions={0} | all-to-all | bytes 262144 | tf_op jit(solution)/shard_map/all_to_all | solution.py:351
  46.8 0.7 shard_map.128.mine
  47.5 2.7 %collective-permute-start.8 = (bf16[2,512,128]{2,1,0:T(8,128)(2,1)S(1)}, bf16[2,512,128]{2,1,0:T(8,128)(2,1)S(1)}, u32[]{:S(2)}, u32[]{:S(2)}) collective-permute-start(bf16[2,512,128]{2,1,0:T(8,128)(2,1)S(1)} %shard_map.128.mine), channel_id=1, source_target_pairs={{0,1},{1,0},{2,3},{3,2},{4,5},{5,4},{6,7},{7,6},{8,9},{9,8},{10,11... | collective-permute-start | bytes 786440 | tf_op jit(solution)/shard_map/ppermute | solution.py:367
  50.2 1.1 %collective-permute-start.9 = (bf16[2,512,128]{2,1,0:T(8,128)(2,1)S(1)}, bf16[2,512,128]{2,1,0:T(8,128)(2,1)S(1)}, u32[]{:S(2)}, u32[]{:S(2)}) collective-permute-start(bf16[2,512,128]{2,1,0:T(8,128)(2,1)S(1)} %shard_map.128.mine), channel_id=1, source_target_pairs={{0,2},{1,3},{2,4},{3,5},{4,6},{5,7},{6,0},{7,1},{8,10},{9,11},{10,... | collective-permute-start | bytes 786440 | tf_op jit(solution)/shard_map/ppermute | solution.py:294
  51.3 1.6 %collective-permute-start.11 = (bf16[2,512,128]{2,1,0:T(8,128)(2,1)S(1)}, bf16[2,512,128]{2,1,0:T(8,128)(2,1)S(1)}, u32[]{:S(2)}, u32[]{:S(2)}) collective-permute-start(bf16[2,512,128]{2,1,0:T(8,128)(2,1)S(1)} %shard_map.128.mine), channel_id=1, source_target_pairs={{0,6},{1,7},{2,0},{3,1},{4,2},{5,3},{6,4},{7,5},{8,14},{9,15},{10,... | collective-permute-start | bytes 786440 | tf_op jit(solution)/shard_map/ppermute | solution.py:294
  52.9 0.0 collective-permute-done.8.partner
  52.9 0.7 %shard_map.129 = (f32[512,1024]{1,0:T(8,128)S(1)}, f32[512,1024]{1,0:T(8,128)S(1)}) custom-call(bf16[2,512,128]{2,1,0:T(8,128)(2,1)S(1)} %shard_map.128.mine, bf16[2,512,128]{2,1,0:T(8,128)(2,1)S(1)} %collective-permute-done.8.partner, bf16[1024,1024]{1,0:T(8,128)(2,1)S(1)} %get-tuple-element.90.load_weights, ...), custom_call_target="tpu_custom_call" | custom-call | flops 536870912 | bytes 8929280 | tf_op jit(solution)/shard_map/pallas_call | solution.py:23
  53.6 5.6 %collective-permute-done.9.mine = bf16[2,512,128]{2,1,0:T(8,128)(2,1)S(1)} collective-permute-done((bf16[2,512,128]{2,1,0:T(8,128)(2,1)S(1)}, bf16[2,512,128]{2,1,0:T(8,128)(2,1)S(1)}, u32[]{:S(2)}, u32[]{:S(2)}) %collective-permute-start.9) | collective-permute-done | bytes 262176 | tf_op jit(solution)/shard_map/ppermute | solution.py:294
  59.2 0.9 %collective-permute-start.10 = (bf16[2,512,128]{2,1,0:T(8,128)(2,1)S(1)}, bf16[2,512,128]{2,1,0:T(8,128)(2,1)S(1)}, u32[]{:S(2)}, u32[]{:S(2)}) collective-permute-start(bf16[2,512,128]{2,1,0:T(8,128)(2,1)S(1)} %collective-permute-done.9.mine), channel_id=1, source_target_pairs={{0,1},{1,0},{2,3},{3,2},{4,5},{5,4},{6,7},{7,6},{8,9},{9,8},{10,11... | collective-permute-start | bytes 786440 | tf_op jit(solution)/shard_map/ppermute | solution.py:367
  60.1 1.2 %collective-permute-start.12 = (bf16[2,512,128]{2,1,0:T(8,128)(2,1)S(1)}, bf16[2,512,128]{2,1,0:T(8,128)(2,1)S(1)}, u32[]{:S(2)}, u32[]{:S(2)}) collective-permute-start(bf16[2,512,128]{2,1,0:T(8,128)(2,1)S(1)} %shard_map.128.mine), channel_id=1, source_target_pairs={{0,4},{1,5},{2,6},{3,7},{4,0},{5,1},{6,2},{7,3},{8,12},{9,13},{10,... | collective-permute-start | bytes 786440 | tf_op jit(solution)/shard_map/ppermute | solution.py:294
  61.4 0.0 collective-permute-done.11.mine
  61.4 0.3 collective-permute-start.14
  61.6 0.0 collective-permute-done.10.partner
  61.6 0.8 %shard_map.130 = (f32[512,1024]{1,0:T(8,128)S(1)}, f32[512,1024]{1,0:T(8,128)S(1)}) custom-call(bf16[2,512,128]{2,1,0:T(8,128)(2,1)S(1)} %collective-permute-done.9.mine, bf16[2,512,128]{2,1,0:T(8,128)(2,1)S(1)} %collective-permute-done.10.partner, bf16[1024,1024]{1,0:T(8,128)(2,1)S(1)} %get-tuple-element.90.load_weights, ...), custom_call_target="tpu_custom_call" | custom-call | flops 536870912 | bytes 13123584 | tf_op jit(solution)/shard_map/pallas_call | solution.py:23
  62.4 7.1 %collective-permute-done.12.mine = bf16[2,512,128]{2,1,0:T(8,128)(2,1)S(1)} collective-permute-done((bf16[2,512,128]{2,1,0:T(8,128)(2,1)S(1)}, bf16[2,512,128]{2,1,0:T(8,128)(2,1)S(1)}, u32[]{:S(2)}, u32[]{:S(2)}) %collective-permute-start.12) | collective-permute-done | bytes 262176 | tf_op jit(solution)/shard_map/ppermute | solution.py:294
  69.5 0.9 %collective-permute-start.13 = (bf16[2,512,128]{2,1,0:T(8,128)(2,1)S(1)}, bf16[2,512,128]{2,1,0:T(8,128)(2,1)S(1)}, u32[]{:S(2)}, u32[]{:S(2)}) collective-permute-start(bf16[2,512,128]{2,1,0:T(8,128)(2,1)S(1)} %collective-permute-done.12.mine), channel_id=1, source_target_pairs={{0,1},{1,0},{2,3},{3,2},{4,5},{5,4},{6,7},{7,6},{8,9},{9,8},{10,11... | collective-permute-start | bytes 786440 | tf_op jit(solution)/shard_map/ppermute | solution.py:367
  70.4 0.0 collective-permute-done.14.partner
  70.4 0.8 %shard_map.131 = (f32[512,1024]{1,0:T(8,128)S(1)}, f32[512,1024]{1,0:T(8,128)S(1)}) custom-call(bf16[2,512,128]{2,1,0:T(8,128)(2,1)S(1)} %collective-permute-done.11.mine, bf16[2,512,128]{2,1,0:T(8,128)(2,1)S(1)} %collective-permute-done.14.partner, bf16[1024,1024]{1,0:T(8,128)(2,1)S(1)} %get-tuple-element.90.load_weights, ...), custom_call_target="tpu_custom_call" | custom-call | flops 536870912 | bytes 13123584 | tf_op jit(solution)/shard_map/pallas_call | solution.py:23
  71.1 0.4 collective-permute-done.13.partner
  71.5 1.7 %shard_map.132 = (bf16[512,1024]{1,0:T(8,128)(2,1)}, bf16[512,1024]{1,0:T(8,128)(2,1)}) custom-call(bf16[2,512,128]{2,1,0:T(8,128)(2,1)S(1)} %collective-permute-done.12.mine, bf16[2,512,128]{2,1,0:T(8,128)(2,1)S(1)} %collective-permute-done.13.partner, bf16[1024,1024]{1,0:T(8,128)(2,1)S(1)} %get-tuple-element.90.load_weights, ...), custom_call_target="tpu_custom_call" | custom-call | flops 536870912 | bytes 11026432 | tf_op jit(solution)/shard_map/pallas_call | solution.py:23
Async XLA Ops:
  3.6 5.8 %collective-permute-start = (bf16[4,512,128]{2,1,0:T(8,128)(2,1)S(1)}, bf16[4,512,128]{2,1,0:T(8,128)(2,1)S(1)}, u32[]{:S(2)}, u32[]{:S(2)}) collective-permute-start(bf16[4,512,128]{2,1,0:T(8,128)(2,1)S(1)} %get-tuple-element.65), channel_id=1, source_target_pairs={{0,1},{1,0},{2,3},{3,2},{4,5},{5,4},{6,7},{7,6},{8,9},{9,8},{10,11... | collective-permute-start | bytes 1572872 | tf_op jit(solution)/shard_map/ppermute | solution.py:317
  9.2 10.6 %copy-start = (f32[128,4,128]{2,1,0:T(4,128)S(1)}, f32[128,4,128]{2,1,0:T(4,128)}, u32[]{:S(2)}) copy-start(f32[128,4,128]{2,1,0:T(4,128)} %param.19) | copy-start | bytes 786436
  9.3 10.6 %copy-start.1 = (f32[128,4,128]{2,1,0:T(4,128)S(1)}, f32[128,4,128]{2,1,0:T(4,128)}, u32[]{:S(2)}) copy-start(f32[128,4,128]{2,1,0:T(4,128)} %param.20) | copy-start | bytes 786436
  9.3 2.0 %collective-permute-start.1 = (bf16[4,512,128]{2,1,0:T(8,128)(2,1)S(1)}, bf16[4,512,128]{2,1,0:T(8,128)(2,1)S(1)}, u32[]{:S(2)}, u32[]{:S(2)}) collective-permute-start(bf16[4,512,128]{2,1,0:T(8,128)(2,1)S(1)} %get-tuple-element.68), channel_id=1, source_target_pairs={{0,1},{1,0},{2,3},{3,2},{4,5},{5,4},{6,7},{7,6},{8,9},{9,8},{10,11... | collective-permute-start | bytes 1572872 | tf_op jit(solution)/shard_map/ppermute | solution.py:331
  11.4 8.5 %collective-permute-start.2 = (bf16[512,128]{1,0:T(8,128)(2,1)S(1)}, bf16[512,128]{1,0:T(8,128)(2,1)S(1)}, u32[]{:S(2)}, u32[]{:S(2)}) collective-permute-start(bf16[512,128]{1,0:T(8,128)(2,1)S(1)} %get-tuple-element.71), channel_id=1, source_target_pairs={{0,2},{1,3},{2,4},{3,5},{4,6},{5,7},{6,0},{7,1},{8,10},{9,11},{10,... | collective-permute-start | bytes 393224 | tf_op jit(solution)/shard_map/ppermute | solution.py:294
  11.4 9.0 %collective-permute-start.3 = (bf16[512,128]{1,0:T(8,128)(2,1)S(1)}, bf16[512,128]{1,0:T(8,128)(2,1)S(1)}, u32[]{:S(2)}, u32[]{:S(2)}) collective-permute-start(bf16[512,128]{1,0:T(8,128)(2,1)S(1)} %get-tuple-element.72), channel_id=1, source_target_pairs={{0,4},{1,5},{2,6},{3,7},{4,0},{5,1},{6,2},{7,3},{8,12},{9,13},{10,... | collective-permute-start | bytes 393224 | tf_op jit(solution)/shard_map/ppermute | solution.py:294
  13.4 7.3 %collective-permute-start.4 = (bf16[512,128]{1,0:T(8,128)(2,1)S(1)}, bf16[512,128]{1,0:T(8,128)(2,1)S(1)}, u32[]{:S(2)}, u32[]{:S(2)}) collective-permute-start(bf16[512,128]{1,0:T(8,128)(2,1)S(1)} %get-tuple-element.73), channel_id=1, source_target_pairs={{0,6},{1,7},{2,0},{3,1},{4,2},{5,3},{6,4},{7,5},{8,14},{9,15},{10,... | collective-permute-start | bytes 393224 | tf_op jit(solution)/shard_map/ppermute | solution.py:294
  14.5 9.2 %collective-permute-start.5 = (bf16[512,128]{1,0:T(8,128)(2,1)S(1)}, bf16[512,128]{1,0:T(8,128)(2,1)S(1)}, u32[]{:S(2)}, u32[]{:S(2)}) collective-permute-start(bf16[512,128]{1,0:T(8,128)(2,1)S(1)} %get-tuple-element.74), channel_id=1, source_target_pairs={{0,2},{1,3},{2,4},{3,5},{4,6},{5,7},{6,0},{7,1},{8,10},{9,11},{10,... | collective-permute-start | bytes 393224 | tf_op jit(solution)/shard_map/ppermute | solution.py:294
  14.9 10.5 %collective-permute-start.6 = (bf16[512,128]{1,0:T(8,128)(2,1)S(1)}, bf16[512,128]{1,0:T(8,128)(2,1)S(1)}, u32[]{:S(2)}, u32[]{:S(2)}) collective-permute-start(bf16[512,128]{1,0:T(8,128)(2,1)S(1)} %get-tuple-element.75), channel_id=1, source_target_pairs={{0,4},{1,5},{2,6},{3,7},{4,0},{5,1},{6,2},{7,3},{8,12},{9,13},{10,... | collective-permute-start | bytes 393224 | tf_op jit(solution)/shard_map/ppermute | solution.py:294
  19.9 6.5 %collective-permute-start.7 = (bf16[512,128]{1,0:T(8,128)(2,1)S(1)}, bf16[512,128]{1,0:T(8,128)(2,1)S(1)}, u32[]{:S(2)}, u32[]{:S(2)}) collective-permute-start(bf16[512,128]{1,0:T(8,128)(2,1)S(1)} %get-tuple-element.76), channel_id=1, source_target_pairs={{0,6},{1,7},{2,0},{3,1},{4,2},{5,3},{6,4},{7,5},{8,14},{9,15},{10,... | collective-permute-start | bytes 393224 | tf_op jit(solution)/shard_map/ppermute | solution.py:294
  47.5 5.3 %collective-permute-start.8 = (bf16[2,512,128]{2,1,0:T(8,128)(2,1)S(1)}, bf16[2,512,128]{2,1,0:T(8,128)(2,1)S(1)}, u32[]{:S(2)}, u32[]{:S(2)}) collective-permute-start(bf16[2,512,128]{2,1,0:T(8,128)(2,1)S(1)} %shard_map.128.mine), channel_id=1, source_target_pairs={{0,1},{1,0},{2,3},{3,2},{4,5},{5,4},{6,7},{7,6},{8,9},{9,8},{10,11... | collective-permute-start | bytes 786440 | tf_op jit(solution)/shard_map/ppermute | solution.py:367
  50.2 9.0 %collective-permute-start.9 = (bf16[2,512,128]{2,1,0:T(8,128)(2,1)S(1)}, bf16[2,512,128]{2,1,0:T(8,128)(2,1)S(1)}, u32[]{:S(2)}, u32[]{:S(2)}) collective-permute-start(bf16[2,512,128]{2,1,0:T(8,128)(2,1)S(1)} %shard_map.128.mine), channel_id=1, source_target_pairs={{0,2},{1,3},{2,4},{3,5},{4,6},{5,7},{6,0},{7,1},{8,10},{9,11},{10,... | collective-permute-start | bytes 786440 | tf_op jit(solution)/shard_map/ppermute | solution.py:294
  51.3 10.1 %collective-permute-start.11 = (bf16[2,512,128]{2,1,0:T(8,128)(2,1)S(1)}, bf16[2,512,128]{2,1,0:T(8,128)(2,1)S(1)}, u32[]{:S(2)}, u32[]{:S(2)}) collective-permute-start(bf16[2,512,128]{2,1,0:T(8,128)(2,1)S(1)} %shard_map.128.mine), channel_id=1, source_target_pairs={{0,6},{1,7},{2,0},{3,1},{4,2},{5,3},{6,4},{7,5},{8,14},{9,15},{10,... | collective-permute-start | bytes 786440 | tf_op jit(solution)/shard_map/ppermute | solution.py:294
  59.2 2.4 %collective-permute-start.10 = (bf16[2,512,128]{2,1,0:T(8,128)(2,1)S(1)}, bf16[2,512,128]{2,1,0:T(8,128)(2,1)S(1)}, u32[]{:S(2)}, u32[]{:S(2)}) collective-permute-start(bf16[2,512,128]{2,1,0:T(8,128)(2,1)S(1)} %collective-permute-done.9.mine), channel_id=1, source_target_pairs={{0,1},{1,0},{2,3},{3,2},{4,5},{5,4},{6,7},{7,6},{8,9},{9,8},{10,11... | collective-permute-start | bytes 786440 | tf_op jit(solution)/shard_map/ppermute | solution.py:367
  60.1 9.4 %collective-permute-start.12 = (bf16[2,512,128]{2,1,0:T(8,128)(2,1)S(1)}, bf16[2,512,128]{2,1,0:T(8,128)(2,1)S(1)}, u32[]{:S(2)}, u32[]{:S(2)}) collective-permute-start(bf16[2,512,128]{2,1,0:T(8,128)(2,1)S(1)} %shard_map.128.mine), channel_id=1, source_target_pairs={{0,4},{1,5},{2,6},{3,7},{4,0},{5,1},{6,2},{7,3},{8,12},{9,13},{10,... | collective-permute-start | bytes 786440 | tf_op jit(solution)/shard_map/ppermute | solution.py:294
  61.4 9.0 %collective-permute-start.14 = (bf16[2,512,128]{2,1,0:T(8,128)(2,1)S(1)}, bf16[2,512,128]{2,1,0:T(8,128)(2,1)S(1)}, u32[]{:S(2)}, u32[]{:S(2)}) collective-permute-start(bf16[2,512,128]{2,1,0:T(8,128)(2,1)S(1)} %collective-permute-done.11.mine), channel_id=1, source_target_pairs={{0,1},{1,0},{2,3},{3,2},{4,5},{5,4},{6,7},{7,6},{8,9},{9,8},{10,11... | collective-permute-start | bytes 786440 | tf_op jit(solution)/shard_map/ppermute | solution.py:367
  69.5 2.0 %collective-permute-start.13 = (bf16[2,512,128]{2,1,0:T(8,128)(2,1)S(1)}, bf16[2,512,128]{2,1,0:T(8,128)(2,1)S(1)}, u32[]{:S(2)}, u32[]{:S(2)}) collective-permute-start(bf16[2,512,128]{2,1,0:T(8,128)(2,1)S(1)} %collective-permute-done.12.mine), channel_id=1, source_target_pairs={{0,1},{1,0},{2,3},{3,2},{4,5},{5,4},{6,7},{7,6},{8,9},{9,8},{10,11... | collective-permute-start | bytes 786440 | tf_op jit(solution)/shard_map/ppermute | solution.py:367

commit v7 on v6

--- a/solution.py
+++ b/solution.py
@@ -210,20 +210,22 @@
     sums, carry,
 ):
     me, length = lax.axis_index("tm"), parcel.shape[0]
-    onward = jnp.zeros((SEG, BLK), F32)
-    back = onward
 
     def pair(j):
         both = parcel[j].astype(F32)
         return jnp.exp(-both[SEG:]), both[:SEG]
 
+    def tree(items):
+        while len(items) > 1:
+            odd = items[len(items) // 2 * 2 :]
+            items = [
+                (first[0] * then[0], then[0] * first[1] + then[1]) for first, then in zip(items[::2], items[1::2])
+            ] + odd
+        return items[0][1]
+
     pairs = [pair(j) for j in range(length)]
-    for j in range(length):
-        factor, value = pairs[j]
-        onward = jnp.where(j < me, factor * onward + value, onward)
-        i = length - 1 - j
-        factor, value = pairs[i]
-        back = jnp.where(i > me, factor * back + value, back)
+    onward = tree([(jnp.where(j < me, f, 1.0), jnp.where(j < me, v, 0.0)) for j, (f, v) in enumerate(pairs)])
+    back = tree([(jnp.where(j > me, f, 1.0), jnp.where(j > me, v, 0.0)) for j, (f, v) in enumerate(pairs)][::-1])
     carry[0] = onward
     carry[1] = back
     for b in range(traces):

time: 73.6 us -> 73.6 us (level)
  no operation moved by 1% of the time
where the time goes in v7:
time: 73.6 us; the launch traced here: 73.4 us
  waiting for transfers between devices  24.1 us (33%)
  blocking collectives  19.3 us (26%)
  starting transfers between devices  17.2 us (23%)
  Pallas kernels  11.9 us (16%)
  between operations  0.91 us (1%)
    ppermute x9, waiting for transfers between devices, across(): lax.ppermute(pieces[k - 1], 'state', [(i, (i + 2 * k) % axis) for i in ra...  21.9 us
    all_to_all x1, blocking collectives, local(): parcel = lax.all_to_all(parcel, 'tm', 0, 0)  19.3 us
    pallas_call x11, Pallas kernels, call(): pl.pallas_call(kernel, out_shape=outs, in_specs=[vmem] * (len(operands) -...  11.9 us
    ppermute x9, starting transfers between devices, across(): lax.ppermute(pieces[k - 1], 'state', [(i, (i + 2 * k) % axis) for i in ra...  9 us
    ppermute x4, starting transfers between devices, local(): partner = lax.ppermute(same[shift], 'state', swap)  4.76 us
    ppermute x1, starting transfers between devices, local(): came_b = lax.ppermute(send_b, 'state', swap)  3.29 us
    ppermute x1, waiting for transfers between devices, local(): came_a = lax.ppermute(send_a, 'state', swap)  1.78 us
  transfers between devices with their start and end apart: 15, of which 9 were waited for; matrix products, arithmetic and copies ran while one was open for 0% of the time, Pallas kernels for 7%

profile of v7, /device:TPU:1, one launch (start us, length us, event | category | flops | bytes accessed | tf_op | source)
XLA Modules:
  0.0 73.4 jit_solution(8199822736708634750)
XLA Ops:
  0.6 2.9 %shard_map.122 = (bf16[1024,1024]{1,0:T(8,128)(2,1)S(1)}, f32[4,512,128]{2,1,0:T(8,128)S(1)}, bf16[4,512,128]{2,1,0:T(8,128)(2,1)S(1)}, bf16[1024,1024]{1,0:T(8,...) custom-call(s32[4,8]{1,0:T(4,128)} %bitcast.15, ...), custom_call_target="tpu_custom_call" | custom-call | flops 1073741824 | bytes 13926528 | tf_op jit(solution)/shard_map/pallas_call | solution.py:23
  3.6 3.3 %collective-permute-start = (bf16[4,512,128]{2,1,0:T(8,128)(2,1)S(1)}, bf16[4,512,128]{2,1,0:T(8,128)(2,1)S(1)}, u32[]{:S(2)}, u32[]{:S(2)}) collective-permute-start(bf16[4,512,128]{2,1,0:T(8,128)(2,1)S(1)} %get-tuple-element.65), channel_id=1, source_target_pairs={{0,1},{1,0},{2,3},{3,2},{4,5},{5,4},{6,7},{7,6},{8,9},{9,8},{10,11... | collective-permute-start | bytes 1572872 | tf_op jit(solution)/shard_map/ppermute | solution.py:319
  6.9 2.4 %shard_map.123 = (bf16[1024,1024]{1,0:T(8,128)(2,1)S(1)}, f32[4,512,128]{2,1,0:T(8,128)S(1)}, bf16[4,512,128]{2,1,0:T(8,128)(2,1)S(1)}, f32[512,8]{1,0:T(8,128)S(1)}) custom-call(bf16[1024,1024]{1,0:T(8,128)(2,1)S(1)} %get-tuple-element.56.cleared, bf16[512,256]{1,0:T(8,128)(2,1)S(1)} %get-tuple-element.57.rows_in, ...), custom_call_target="tpu_custom_call", output_to_operand_aliasing={{0}: (0, {})} | custom-call | flops 1073741824 | bytes 8814720 | tf_op jit(solution)/shard_map/pallas_call | solution.py:23
  9.2 0.0 copy-start
  9.3 0.0 copy-start.1
  9.3 0.1 collective-permute-start.1
  9.4 0.0 collective-permute-done.came
  9.4 0.1 shard_map.124
  9.5 1.8 %collective-permute-done.1.came = bf16[4,512,128]{2,1,0:T(8,128)(2,1)S(1)} collective-permute-done((bf16[4,512,128]{2,1,0:T(8,128)(2,1)S(1)}, bf16[4,512,128]{2,1,0:T(8,128)(2,1)S(1)}, u32[]{:S(2)}, u32[]{:S(2)}) %collective-permute-start.1) | collective-permute-done | bytes 524320 | tf_op jit(solution)/shard_map/ppermute | solution.py:333
  11.3 0.1 shard_map.125
  11.4 0.1 collective-permute-start.2
  11.4 1.9 %collective-permute-start.3 = (bf16[512,128]{1,0:T(8,128)(2,1)S(1)}, bf16[512,128]{1,0:T(8,128)(2,1)S(1)}, u32[]{:S(2)}, u32[]{:S(2)}) collective-permute-start(bf16[512,128]{1,0:T(8,128)(2,1)S(1)} %get-tuple-element.72), channel_id=1, source_target_pairs={{0,4},{1,5},{2,6},{3,7},{4,0},{5,1},{6,2},{7,3},{8,12},{9,13},{10,... | collective-permute-start | bytes 393224 | tf_op jit(solution)/shard_map/ppermute | solution.py:296
  13.4 1.2 %collective-permute-start.4 = (bf16[512,128]{1,0:T(8,128)(2,1)S(1)}, bf16[512,128]{1,0:T(8,128)(2,1)S(1)}, u32[]{:S(2)}, u32[]{:S(2)}) collective-permute-start(bf16[512,128]{1,0:T(8,128)(2,1)S(1)} %get-tuple-element.73), channel_id=1, source_target_pairs={{0,6},{1,7},{2,0},{3,1},{4,2},{5,3},{6,4},{7,5},{8,14},{9,15},{10,... | collective-permute-start | bytes 393224 | tf_op jit(solution)/shard_map/ppermute | solution.py:296
  14.5 0.3 collective-permute-start.5
  14.9 1.6 %collective-permute-start.6 = (bf16[512,128]{1,0:T(8,128)(2,1)S(1)}, bf16[512,128]{1,0:T(8,128)(2,1)S(1)}, u32[]{:S(2)}, u32[]{:S(2)}) collective-permute-start(bf16[512,128]{1,0:T(8,128)(2,1)S(1)} %get-tuple-element.75), channel_id=1, source_target_pairs={{0,4},{1,5},{2,6},{3,7},{4,0},{5,1},{6,2},{7,3},{8,12},{9,13},{10,... | collective-permute-start | bytes 393224 | tf_op jit(solution)/shard_map/ppermute | solution.py:296
  16.5 3.4 %collective-permute-done.2.a1 = bf16[512,128]{1,0:T(8,128)(2,1)S(1)} collective-permute-done((bf16[512,128]{1,0:T(8,128)(2,1)S(1)}, bf16[512,128]{1,0:T(8,128)(2,1)S(1)}, u32[]{:S(2)}, u32[]{:S(2)}) %collective-permute-start.2) | collective-permute-done | bytes 131104 | tf_op jit(solution)/shard_map/ppermute | solution.py:296
  19.9 0.0 collective-permute-start.7
  19.9 0.0 copy-done
  19.9 0.0 copy-done.1
  19.9 0.6 shard_map.126
  20.4 0.0 collective-permute-done.3.a2
  20.5 0.2 collective-permute-done.4.a3
  20.7 3.1 %collective-permute-done.5.b1 = bf16[512,128]{1,0:T(8,128)(2,1)S(1)} collective-permute-done((bf16[512,128]{1,0:T(8,128)(2,1)S(1)}, bf16[512,128]{1,0:T(8,128)(2,1)S(1)}, u32[]{:S(2)}, u32[]{:S(2)}) %collective-permute-start.5) | collective-permute-done | bytes 131104 | tf_op jit(solution)/shard_map/ppermute | solution.py:296
  23.8 1.6 %collective-permute-done.6.b2 = bf16[512,128]{1,0:T(8,128)(2,1)S(1)} collective-permute-done((bf16[512,128]{1,0:T(8,128)(2,1)S(1)}, bf16[512,128]{1,0:T(8,128)(2,1)S(1)}, u32[]{:S(2)}, u32[]{:S(2)}) %collective-permute-start.6) | collective-permute-done | bytes 131104 | tf_op jit(solution)/shard_map/ppermute | solution.py:296
  25.4 1.0 %collective-permute-done.7.b3 = bf16[512,128]{1,0:T(8,128)(2,1)S(1)} collective-permute-done((bf16[512,128]{1,0:T(8,128)(2,1)S(1)}, bf16[512,128]{1,0:T(8,128)(2,1)S(1)}, u32[]{:S(2)}, u32[]{:S(2)}) %collective-permute-start.7) | collective-permute-done | bytes 131104 | tf_op jit(solution)/shard_map/ppermute | solution.py:296
  26.4 1.1 %shard_map.127 = (f32[512,128]{1,0:T(8,128)S(1)}, f32[512,128]{1,0:T(8,128)S(1)}, f32[4,4,2,8,128]{4,3,2,1,0:T(8,128)S(1)}, bf16[32,16,128]{2,1,0:T(8,128)(2,1)S(1)}) custom-call(f32[512,128]{1,0:T(8,128)S(1)} %get-tuple-element.69.own_a, f32[512,128]{1,0:T(8,128)S(1)} %get-tuple-element.70.own_b, bf16[512,128]{1,0:T(8,128)(2,1)S(1)} %collective-permute-done.2.a1, ...), custom_call_target="tpu_custom_call" | custom-call | bytes 2916352 | tf_op jit(solution)/shard_map/pallas_call | solution.py:23
  27.5 19.3 %all_to_all.5.parcel = bf16[32,16,128]{2,1,0:T(8,128)(2,1)S(1)} all-to-all(bf16[32,16,128]{2,1,0:T(8,128)(2,1)S(1)} %get-tuple-element.82), channel_id=1, replica_groups=mesh['tm'=32,'state'=8] {'tm'}, dimensions={0} | all-to-all | bytes 262144 | tf_op jit(solution)/shard_map/all_to_all | solution.py:353
  46.8 0.7 shard_map.128.mine
  47.5 2.7 %collective-permute-start.8 = (bf16[2,512,128]{2,1,0:T(8,128)(2,1)S(1)}, bf16[2,512,128]{2,1,0:T(8,128)(2,1)S(1)}, u32[]{:S(2)}, u32[]{:S(2)}) collective-permute-start(bf16[2,512,128]{2,1,0:T(8,128)(2,1)S(1)} %shard_map.128.mine), channel_id=1, source_target_pairs={{0,1},{1,0},{2,3},{3,2},{4,5},{5,4},{6,7},{7,6},{8,9},{9,8},{10,11... | collective-permute-start | bytes 786440 | tf_op jit(solution)/shard_map/ppermute | solution.py:369
  50.2 1.1 %collective-permute-start.9 = (bf16[2,512,128]{2,1,0:T(8,128)(2,1)S(1)}, bf16[2,512,128]{2,1,0:T(8,128)(2,1)S(1)}, u32[]{:S(2)}, u32[]{:S(2)}) collective-permute-start(bf16[2,512,128]{2,1,0:T(8,128)(2,1)S(1)} %shard_map.128.mine), channel_id=1, source_target_pairs={{0,2},{1,3},{2,4},{3,5},{4,6},{5,7},{6,0},{7,1},{8,10},{9,11},{10,... | collective-permute-start | bytes 786440 | tf_op jit(solution)/shard_map/ppermute | solution.py:296
  51.3 1.6 %collective-permute-start.11 = (bf16[2,512,128]{2,1,0:T(8,128)(2,1)S(1)}, bf16[2,512,128]{2,1,0:T(8,128)(2,1)S(1)}, u32[]{:S(2)}, u32[]{:S(2)}) collective-permute-start(bf16[2,512,128]{2,1,0:T(8,128)(2,1)S(1)} %shard_map.128.mine), channel_id=1, source_target_pairs={{0,6},{1,7},{2,0},{3,1},{4,2},{5,3},{6,4},{7,5},{8,14},{9,15},{10,... | collective-permute-start | bytes 786440 | tf_op jit(solution)/shard_map/ppermute | solution.py:296
  52.9 0.0 collective-permute-done.8.partner
  52.9 0.7 %shard_map.129 = (f32[512,1024]{1,0:T(8,128)S(1)}, f32[512,1024]{1,0:T(8,128)S(1)}) custom-call(bf16[2,512,128]{2,1,0:T(8,128)(2,1)S(1)} %shard_map.128.mine, bf16[2,512,128]{2,1,0:T(8,128)(2,1)S(1)} %collective-permute-done.8.partner, bf16[1024,1024]{1,0:T(8,128)(2,1)S(1)} %get-tuple-element.90.load_weights, ...), custom_call_target="tpu_custom_call" | custom-call | flops 536870912 | bytes 8929280 | tf_op jit(solution)/shard_map/pallas_call | solution.py:23
  53.6 5.6 %collective-permute-done.9.mine = bf16[2,512,128]{2,1,0:T(8,128)(2,1)S(1)} collective-permute-done((bf16[2,512,128]{2,1,0:T(8,128)(2,1)S(1)}, bf16[2,512,128]{2,1,0:T(8,128)(2,1)S(1)}, u32[]{:S(2)}, u32[]{:S(2)}) %collective-permute-start.9) | collective-permute-done | bytes 262176 | tf_op jit(solution)/shard_map/ppermute | solution.py:296
  59.2 0.9 %collective-permute-start.10 = (bf16[2,512,128]{2,1,0:T(8,128)(2,1)S(1)}, bf16[2,512,128]{2,1,0:T(8,128)(2,1)S(1)}, u32[]{:S(2)}, u32[]{:S(2)}) collective-permute-start(bf16[2,512,128]{2,1,0:T(8,128)(2,1)S(1)} %collective-permute-done.9.mine), channel_id=1, source_target_pairs={{0,1},{1,0},{2,3},{3,2},{4,5},{5,4},{6,7},{7,6},{8,9},{9,8},{10,11... | collective-permute-start | bytes 786440 | tf_op jit(solution)/shard_map/ppermute | solution.py:369
  60.1 1.2 %collective-permute-start.12 = (bf16[2,512,128]{2,1,0:T(8,128)(2,1)S(1)}, bf16[2,512,128]{2,1,0:T(8,128)(2,1)S(1)}, u32[]{:S(2)}, u32[]{:S(2)}) collective-permute-start(bf16[2,512,128]{2,1,0:T(8,128)(2,1)S(1)} %shard_map.128.mine), channel_id=1, source_target_pairs={{0,4},{1,5},{2,6},{3,7},{4,0},{5,1},{6,2},{7,3},{8,12},{9,13},{10,... | collective-permute-start | bytes 786440 | tf_op jit(solution)/shard_map/ppermute | solution.py:296
  61.3 0.0 collective-permute-done.11.mine
  61.3 0.3 collective-permute-start.14
  61.6 0.0 collective-permute-done.10.partner
  61.6 0.8 %shard_map.130 = (f32[512,1024]{1,0:T(8,128)S(1)}, f32[512,1024]{1,0:T(8,128)S(1)}) custom-call(bf16[2,512,128]{2,1,0:T(8,128)(2,1)S(1)} %collective-permute-done.9.mine, bf16[2,512,128]{2,1,0:T(8,128)(2,1)S(1)} %collective-permute-done.10.partner, bf16[1024,1024]{1,0:T(8,128)(2,1)S(1)} %get-tuple-element.90.load_weights, ...), custom_call_target="tpu_custom_call" | custom-call | flops 536870912 | bytes 13123584 | tf_op jit(solution)/shard_map/pallas_call | solution.py:23
  62.4 7.1 %collective-permute-done.12.mine = bf16[2,512,128]{2,1,0:T(8,128)(2,1)S(1)} collective-permute-done((bf16[2,512,128]{2,1,0:T(8,128)(2,1)S(1)}, bf16[2,512,128]{2,1,0:T(8,128)(2,1)S(1)}, u32[]{:S(2)}, u32[]{:S(2)}) %collective-permute-start.12) | collective-permute-done | bytes 262176 | tf_op jit(solution)/shard_map/ppermute | solution.py:296
  69.5 0.9 %collective-permute-start.13 = (bf16[2,512,128]{2,1,0:T(8,128)(2,1)S(1)}, bf16[2,512,128]{2,1,0:T(8,128)(2,1)S(1)}, u32[]{:S(2)}, u32[]{:S(2)}) collective-permute-start(bf16[2,512,128]{2,1,0:T(8,128)(2,1)S(1)} %collective-permute-done.12.mine), channel_id=1, source_target_pairs={{0,1},{1,0},{2,3},{3,2},{4,5},{5,4},{6,7},{7,6},{8,9},{9,8},{10,11... | collective-permute-start | bytes 786440 | tf_op jit(solution)/shard_map/ppermute | solution.py:369
  70.4 0.0 collective-permute-done.14.partner
  70.4 0.8 %shard_map.131 = (f32[512,1024]{1,0:T(8,128)S(1)}, f32[512,1024]{1,0:T(8,128)S(1)}) custom-call(bf16[2,512,128]{2,1,0:T(8,128)(2,1)S(1)} %collective-permute-done.11.mine, bf16[2,512,128]{2,1,0:T(8,128)(2,1)S(1)} %collective-permute-done.14.partner, bf16[1024,1024]{1,0:T(8,128)(2,1)S(1)} %get-tuple-element.90.load_weights, ...), custom_call_target="tpu_custom_call" | custom-call | flops 536870912 | bytes 13123584 | tf_op jit(solution)/shard_map/pallas_call | solution.py:23
  71.1 0.4 collective-permute-done.13.partner
  71.5 1.7 %shard_map.132 = (bf16[512,1024]{1,0:T(8,128)(2,1)}, bf16[512,1024]{1,0:T(8,128)(2,1)}) custom-call(bf16[2,512,128]{2,1,0:T(8,128)(2,1)S(1)} %collective-permute-done.12.mine, bf16[2,512,128]{2,1,0:T(8,128)(2,1)S(1)} %collective-permute-done.13.partner, bf16[1024,1024]{1,0:T(8,128)(2,1)S(1)} %get-tuple-element.90.load_weights, ...), custom_call_target="tpu_custom_call" | custom-call | flops 536870912 | bytes 11026432 | tf_op jit(solution)/shard_map/pallas_call | solution.py:23
Async XLA Ops:
  3.6 5.8 %collective-permute-start = (bf16[4,512,128]{2,1,0:T(8,128)(2,1)S(1)}, bf16[4,512,128]{2,1,0:T(8,128)(2,1)S(1)}, u32[]{:S(2)}, u32[]{:S(2)}) collective-permute-start(bf16[4,512,128]{2,1,0:T(8,128)(2,1)S(1)} %get-tuple-element.65), channel_id=1, source_target_pairs={{0,1},{1,0},{2,3},{3,2},{4,5},{5,4},{6,7},{7,6},{8,9},{9,8},{10,11... | collective-permute-start | bytes 1572872 | tf_op jit(solution)/shard_map/ppermute | solution.py:319
  9.2 10.6 %copy-start = (f32[128,4,128]{2,1,0:T(4,128)S(1)}, f32[128,4,128]{2,1,0:T(4,128)}, u32[]{:S(2)}) copy-start(f32[128,4,128]{2,1,0:T(4,128)} %param.19) | copy-start | bytes 786436
  9.3 10.6 %copy-start.1 = (f32[128,4,128]{2,1,0:T(4,128)S(1)}, f32[128,4,128]{2,1,0:T(4,128)}, u32[]{:S(2)}) copy-start(f32[128,4,128]{2,1,0:T(4,128)} %param.20) | copy-start | bytes 786436
  9.3 2.0 %collective-permute-start.1 = (bf16[4,512,128]{2,1,0:T(8,128)(2,1)S(1)}, bf16[4,512,128]{2,1,0:T(8,128)(2,1)S(1)}, u32[]{:S(2)}, u32[]{:S(2)}) collective-permute-start(bf16[4,512,128]{2,1,0:T(8,128)(2,1)S(1)} %get-tuple-element.68), channel_id=1, source_target_pairs={{0,1},{1,0},{2,3},{3,2},{4,5},{5,4},{6,7},{7,6},{8,9},{9,8},{10,11... | collective-permute-start | bytes 1572872 | tf_op jit(solution)/shard_map/ppermute | solution.py:333
  11.4 8.5 %collective-permute-start.2 = (bf16[512,128]{1,0:T(8,128)(2,1)S(1)}, bf16[512,128]{1,0:T(8,128)(2,1)S(1)}, u32[]{:S(2)}, u32[]{:S(2)}) collective-permute-start(bf16[512,128]{1,0:T(8,128)(2,1)S(1)} %get-tuple-element.71), channel_id=1, source_target_pairs={{0,2},{1,3},{2,4},{3,5},{4,6},{5,7},{6,0},{7,1},{8,10},{9,11},{10,... | collective-permute-start | bytes 393224 | tf_op jit(solution)/shard_map/ppermute | solution.py:296
  11.4 9.0 %collective-permute-start.3 = (bf16[512,128]{1,0:T(8,128)(2,1)S(1)}, bf16[512,128]{1,0:T(8,128)(2,1)S(1)}, u32[]{:S(2)}, u32[]{:S(2)}) collective-permute-start(bf16[512,128]{1,0:T(8,128)(2,1)S(1)} %get-tuple-element.72), channel_id=1, source_target_pairs={{0,4},{1,5},{2,6},{3,7},{4,0},{5,1},{6,2},{7,3},{8,12},{9,13},{10,... | collective-permute-start | bytes 393224 | tf_op jit(solution)/shard_map/ppermute | solution.py:296
  13.4 7.3 %collective-permute-start.4 = (bf16[512,128]{1,0:T(8,128)(2,1)S(1)}, bf16[512,128]{1,0:T(8,128)(2,1)S(1)}, u32[]{:S(2)}, u32[]{:S(2)}) collective-permute-start(bf16[512,128]{1,0:T(8,128)(2,1)S(1)} %get-tuple-element.73), channel_id=1, source_target_pairs={{0,6},{1,7},{2,0},{3,1},{4,2},{5,3},{6,4},{7,5},{8,14},{9,15},{10,... | collective-permute-start | bytes 393224 | tf_op jit(solution)/shard_map/ppermute | solution.py:296
  14.5 9.2 %collective-permute-start.5 = (bf16[512,128]{1,0:T(8,128)(2,1)S(1)}, bf16[512,128]{1,0:T(8,128)(2,1)S(1)}, u32[]{:S(2)}, u32[]{:S(2)}) collective-permute-start(bf16[512,128]{1,0:T(8,128)(2,1)S(1)} %get-tuple-element.74), channel_id=1, source_target_pairs={{0,2},{1,3},{2,4},{3,5},{4,6},{5,7},{6,0},{7,1},{8,10},{9,11},{10,... | collective-permute-start | bytes 393224 | tf_op jit(solution)/shard_map/ppermute | solution.py:296
  14.9 10.5 %collective-permute-start.6 = (bf16[512,128]{1,0:T(8,128)(2,1)S(1)}, bf16[512,128]{1,0:T(8,128)(2,1)S(1)}, u32[]{:S(2)}, u32[]{:S(2)}) collective-permute-start(bf16[512,128]{1,0:T(8,128)(2,1)S(1)} %get-tuple-element.75), channel_id=1, source_target_pairs={{0,4},{1,5},{2,6},{3,7},{4,0},{5,1},{6,2},{7,3},{8,12},{9,13},{10,... | collective-permute-start | bytes 393224 | tf_op jit(solution)/shard_map/ppermute | solution.py:296
  19.9 6.5 %collective-permute-start.7 = (bf16[512,128]{1,0:T(8,128)(2,1)S(1)}, bf16[512,128]{1,0:T(8,128)(2,1)S(1)}, u32[]{:S(2)}, u32[]{:S(2)}) collective-permute-start(bf16[512,128]{1,0:T(8,128)(2,1)S(1)} %get-tuple-element.76), channel_id=1, source_target_pairs={{0,6},{1,7},{2,0},{3,1},{4,2},{5,3},{6,4},{7,5},{8,14},{9,15},{10,... | collective-permute-start | bytes 393224 | tf_op jit(solution)/shard_map/ppermute | solution.py:296
  47.5 5.3 %collective-permute-start.8 = (bf16[2,512,128]{2,1,0:T(8,128)(2,1)S(1)}, bf16[2,512,128]{2,1,0:T(8,128)(2,1)S(1)}, u32[]{:S(2)}, u32[]{:S(2)}) collective-permute-start(bf16[2,512,128]{2,1,0:T(8,128)(2,1)S(1)} %shard_map.128.mine), channel_id=1, source_target_pairs={{0,1},{1,0},{2,3},{3,2},{4,5},{5,4},{6,7},{7,6},{8,9},{9,8},{10,11... | collective-permute-start | bytes 786440 | tf_op jit(solution)/shard_map/ppermute | solution.py:369
  50.2 9.0 %collective-permute-start.9 = (bf16[2,512,128]{2,1,0:T(8,128)(2,1)S(1)}, bf16[2,512,128]{2,1,0:T(8,128)(2,1)S(1)}, u32[]{:S(2)}, u32[]{:S(2)}) collective-permute-start(bf16[2,512,128]{2,1,0:T(8,128)(2,1)S(1)} %shard_map.128.mine), channel_id=1, source_target_pairs={{0,2},{1,3},{2,4},{3,5},{4,6},{5,7},{6,0},{7,1},{8,10},{9,11},{10,... | collective-permute-start | bytes 786440 | tf_op jit(solution)/shard_map/ppermute | solution.py:296
  51.3 10.1 %collective-permute-start.11 = (bf16[2,512,128]{2,1,0:T(8,128)(2,1)S(1)}, bf16[2,512,128]{2,1,0:T(8,128)(2,1)S(1)}, u32[]{:S(2)}, u32[]{:S(2)}) collective-permute-start(bf16[2,512,128]{2,1,0:T(8,128)(2,1)S(1)} %shard_map.128.mine), channel_id=1, source_target_pairs={{0,6},{1,7},{2,0},{3,1},{4,2},{5,3},{6,4},{7,5},{8,14},{9,15},{10,... | collective-permute-start | bytes 786440 | tf_op jit(solution)/shard_map/ppermute | solution.py:296
  59.2 2.4 %collective-permute-start.10 = (bf16[2,512,128]{2,1,0:T(8,128)(2,1)S(1)}, bf16[2,512,128]{2,1,0:T(8,128)(2,1)S(1)}, u32[]{:S(2)}, u32[]{:S(2)}) collective-permute-start(bf16[2,512,128]{2,1,0:T(8,128)(2,1)S(1)} %collective-permute-done.9.mine), channel_id=1, source_target_pairs={{0,1},{1,0},{2,3},{3,2},{4,5},{5,4},{6,7},{7,6},{8,9},{9,8},{10,11... | collective-permute-start | bytes 786440 | tf_op jit(solution)/shard_map/ppermute | solution.py:369
  60.1 9.4 %collective-permute-start.12 = (bf16[2,512,128]{2,1,0:T(8,128)(2,1)S(1)}, bf16[2,512,128]{2,1,0:T(8,128)(2,1)S(1)}, u32[]{:S(2)}, u32[]{:S(2)}) collective-permute-start(bf16[2,512,128]{2,1,0:T(8,128)(2,1)S(1)} %shard_map.128.mine), channel_id=1, source_target_pairs={{0,4},{1,5},{2,6},{3,7},{4,0},{5,1},{6,2},{7,3},{8,12},{9,13},{10,... | collective-permute-start | bytes 786440 | tf_op jit(solution)/shard_map/ppermute | solution.py:296
  61.3 9.0 %collective-permute-start.14 = (bf16[2,512,128]{2,1,0:T(8,128)(2,1)S(1)}, bf16[2,512,128]{2,1,0:T(8,128)(2,1)S(1)}, u32[]{:S(2)}, u32[]{:S(2)}) collective-permute-start(bf16[2,512,128]{2,1,0:T(8,128)(2,1)S(1)} %collective-permute-done.11.mine), channel_id=1, source_target_pairs={{0,1},{1,0},{2,3},{3,2},{4,5},{5,4},{6,7},{7,6},{8,9},{9,8},{10,11... | collective-permute-start | bytes 786440 | tf_op jit(solution)/shard_map/ppermute | solution.py:369
  69.5 2.0 %collective-permute-start.13 = (bf16[2,512,128]{2,1,0:T(8,128)(2,1)S(1)}, bf16[2,512,128]{2,1,0:T(8,128)(2,1)S(1)}, u32[]{:S(2)}, u32[]{:S(2)}) collective-permute-start(bf16[2,512,128]{2,1,0:T(8,128)(2,1)S(1)} %collective-permute-done.12.mine), channel_id=1, source_target_pairs={{0,1},{1,0},{2,3},{3,2},{4,5},{5,4},{6,7},{7,6},{8,9},{9,8},{10,11... | collective-permute-start | bytes 786440 | tf_op jit(solution)/shard_map/ppermute | solution.py:369
